TPU v7x, 32 devices: a whole 2x2x4 slice. The times are simulated.
32 devices in a mesh: blk: 4 (over y, core), dp: 8 (over z, x).
Axes of the slice: x: 2, y: 2, z: 4, core: 2. Of those that a mesh axis runs over, the one named last changes fastest.
Arguments:
- tokens: bfloat16 [16, 4, 512, 768], P('dp', 'blk'), may hold values from -6 to 6
- cotangent: bfloat16 [16, 4, 512, 768], P('dp', 'blk'), may hold values from -6 to 6
- lengths: int32 [16, 2], P('dp'), may hold values from 513 to 1024, as said below
- head_mode: int32 [12], replicated, may hold values from 0 to 1, as said below
- w_query: bfloat16 [589824], P(('blk', 'dp')), may hold values from -0.21875 to 0.21875
- w_key: bfloat16 [589824], P(('blk', 'dp')), may hold values from -0.21875 to 0.21875
- w_value: bfloat16 [589824], P(('blk', 'dp')), may hold values from -0.21875 to 0.21875
- w_out: bfloat16 [589824], P(('blk', 'dp')), may hold values from -0.875 to 0.875
- w_up: bfloat16 [2359296], P(('blk', 'dp')), may hold values from -0.21875 to 0.21875
- w_down: bfloat16 [2359296], P(('blk', 'dp')), may hold values from -0.109375 to 0.109375
- b_up: bfloat16 [3072], P(('blk', 'dp')), may hold values from -3 to 3
- vectors: bfloat16 [6144], P(('blk', 'dp'))
Outputs:
- activations: bfloat16 [16, 4, 512, 768], P('dp', 'blk')
- input_grad: float32 [16, 4, 512, 768], P('dp', 'blk')
- grad_query: float32 [589824], P(('blk', 'dp'))
- grad_key: float32 [589824], P(('blk', 'dp'))
- grad_value: float32 [589824], P(('blk', 'dp'))
- grad_out: float32 [589824], P(('blk', 'dp'))
- grad_up: float32 [2359296], P(('blk', 'dp'))
- grad_down: float32 [2359296], P(('blk', 'dp'))
- grad_up_bias: float32 [3072], P(('blk', 'dp'))
- grad_vectors: float32 [6144], P(('blk', 'dp'))
Inputs may be any that keep to these rules, and one draw needn't show every extreme that they name: `lengths`: key positions at or past a sequence's length are padding. `head_mode`: exactly 6 heads are marked 1.
All inputs are finite; a program needn't handle non-finite values.
Results may differ from a plain program's by a relative error of at most 0.013.
The roundings to bfloat16 on the way count: a program that leaves them out, or rounds other values in their place, can miss the bound.
Values may be sent and summed in bfloat16 or wider, within the bound.
No kernel may reach another device: no remote copies, remote signals or barrier semaphores. Data moves between devices by JAX's collectives and lax.ppermute only.
A program may use at most 192 MiB of HBM per device.

v0:
```python
from functools import partial

import jax
import jax.numpy as jnp
from jax import lax
from jax.sharding import PartitionSpec as P

D = 768
H = 12
HD = 64
FF = 3072
BLOCK = 512


norm_eps = 1e-05
masked_fill = -1000000000.0


def partner(value, axis, distance):
    mask = 2**distance
    pairs = [(source, source ^ mask) for source in range(lax.axis_size(axis))]
    return lax.ppermute(value, axis, pairs)


def layer_norm(inputs, gain_row, bias_row):
    average = jnp.mean(inputs, axis=-1, keepdims=True)
    centred = inputs - average
    variance = jnp.mean(centred * centred, axis=-1, keepdims=True)
    return centred * lax.rsqrt(variance + norm_eps) * gain_row + bias_row


def matmul(left_side, right_side):
    return jnp.dot(left_side, right_side, preferred_element_type=jnp.float32)


def key_mask(head_mode, block_side, seq_length):
    key_start = jnp.where(head_mode == 1, 1 - block_side, block_side) * BLOCK
    position = key_start[:, None] + jnp.arange(BLOCK, dtype=jnp.int32)[None, :]
    return position < seq_length


def masked_scores(queries, key_used, key_valid):
    scores = jnp.einsum(
        "qhd,khd->hqk", queries, key_used, preferred_element_type=jnp.float32
    ) * HD ** (-0.5)
    return jnp.where(key_valid[:, None, :], scores, masked_fill)


def attend_forward(bundle):
    queries, key_used, value_used, key_valid = bundle
    scores = masked_scores(queries, key_used, key_valid)
    top_score = jnp.max(scores, axis=-1, keepdims=True)
    log_total = top_score + jnp.log(jnp.sum(jnp.exp(scores - top_score), axis=-1, keepdims=True))
    attn_probs = jnp.exp(scores - log_total).astype(jnp.bfloat16)
    context = jnp.einsum("hqk,khd->qhd", attn_probs, value_used, preferred_element_type=jnp.float32)
    return (context.astype(jnp.bfloat16), log_total[:, :, 0])


def attend_backward(bundle):
    queries, key_used, value_used, key_valid, log_total, grad_context = bundle
    scores = masked_scores(queries, key_used, key_valid)
    attn_probs = jnp.exp(scores - log_total[:, :, None])
    grad_value = jnp.einsum(
        "hqk,qhd->khd",
        attn_probs.astype(jnp.bfloat16),
        grad_context,
        preferred_element_type=jnp.float32,
    )
    grad_probs = jnp.einsum(
        "qhd,khd->hqk", grad_context, value_used, preferred_element_type=jnp.float32
    )
    row_terms = jnp.sum(attn_probs * grad_probs, axis=-1, keepdims=True)
    grad_scores = (attn_probs * (grad_probs - row_terms)).astype(jnp.bfloat16)
    score_scale = HD ** (-0.5)
    grad_query = (
        jnp.einsum("hqk,khd->qhd", grad_scores, key_used, preferred_element_type=jnp.float32)
        * score_scale
    )
    grad_key = (
        jnp.einsum("hqk,qhd->khd", grad_scores, queries, preferred_element_type=jnp.float32)
        * score_scale
    )
    return (
        grad_query.astype(jnp.bfloat16),
        grad_key.astype(jnp.bfloat16),
        grad_value.astype(jnp.bfloat16),
    )


def attention_mats(pieces):
    query_flat, key_flat, value_flat, out_flat, vector_flat = pieces
    return (
        query_flat.reshape(D, D),
        key_flat.reshape(D, D),
        value_flat.reshape(D, D),
        out_flat.reshape(D, D),
        vector_flat.reshape(8, D).astype(jnp.float32),
    )


def ffn_mats(pieces):
    up_flat, down_flat, bias_flat = pieces
    return (up_flat.reshape(D, FF), down_flat.reshape(FF, D), bias_flat.astype(jnp.float32))


def body(
    tokens,
    cotangent,
    lengths,
    head_mode,
    w_query,
    w_key,
    w_value,
    w_out,
    w_up,
    w_down,
    b_up,
    vectors,
):
    seq_count = tokens.shape[0]
    row_count = seq_count * BLOCK
    blk_index = lax.axis_index("blk")
    block_side = blk_index % 2
    member = blk_index // 2
    seq_lengths = jnp.where(member == 0, lengths[:, 0], lengths[:, 1])
    swapped_cols = jnp.repeat(head_mode == 1, HD)[None, :]
    key_valid = jax.vmap(partial(key_mask, head_mode, block_side))(seq_lengths)
    attn_pieces = (
        lax.all_gather(w_query, ("blk", "dp"), axis=0, tiled=True),
        lax.all_gather(w_key, ("blk", "dp"), axis=0, tiled=True),
        lax.all_gather(w_value, ("blk", "dp"), axis=0, tiled=True),
        lax.all_gather(w_out, ("blk", "dp"), axis=0, tiled=True),
        lax.all_gather(vectors, ("blk", "dp"), axis=0, tiled=True),
    )
    ffn_pieces = (
        lax.all_gather(w_up, ("blk", "dp"), axis=0, tiled=True),
        lax.all_gather(w_down, ("blk", "dp"), axis=0, tiled=True),
        lax.all_gather(b_up, ("blk", "dp"), axis=0, tiled=True),
    )
    mat_query, mat_key, mat_value, mat_out, vec_rows = attention_mats(attn_pieces)
    mat_up, mat_down, up_bias = ffn_mats(ffn_pieces)
    inputs = tokens.reshape(row_count, D)
    queries = (matmul(inputs, mat_query) + vec_rows[0]).astype(jnp.bfloat16)
    key_rows = matmul(inputs, mat_key).astype(jnp.bfloat16)
    value_rows = (matmul(inputs, mat_value) + vec_rows[1]).astype(jnp.bfloat16)
    received = partner(jnp.stack((key_rows, value_rows)), "blk", 0)
    partner_keys = received[0]
    partner_values = received[1]
    key_used = jnp.where(swapped_cols, partner_keys, key_rows)
    value_used = jnp.where(swapped_cols, partner_values, value_rows)
    head_shape = (seq_count, BLOCK, H, HD)
    attn_inputs = (
        queries.reshape(head_shape),
        key_used.reshape(head_shape),
        value_used.reshape(head_shape),
        key_valid,
    )
    context, log_total = lax.map(attend_forward, attn_inputs)
    context_rows = context.reshape(row_count, D)
    residual_one = inputs.astype(jnp.float32) + (matmul(context_rows, mat_out) + vec_rows[2])
    normed_first, first_pull = jax.vjp(layer_norm, residual_one, vec_rows[3], vec_rows[4])
    first_low = normed_first.astype(jnp.bfloat16)
    hidden = matmul(first_low, mat_up) + up_bias
    activated_f, gelu_pull = jax.vjp(partial(jax.nn.gelu, approximate=False), hidden)
    activated = activated_f.astype(jnp.bfloat16)
    residual_two = normed_first + (matmul(activated, mat_down) + vec_rows[5])
    output, second_pull = jax.vjp(layer_norm, residual_two, vec_rows[6], vec_rows[7])
    activations = output.astype(jnp.bfloat16).reshape(tokens.shape)
    ffn_pieces = (
        lax.all_gather(w_up, ("blk", "dp"), axis=0, tiled=True),
        lax.all_gather(w_down, ("blk", "dp"), axis=0, tiled=True),
        lax.all_gather(b_up, ("blk", "dp"), axis=0, tiled=True),
    )
    mat_up, mat_down, up_bias = ffn_mats(ffn_pieces)
    grad_two, grad_gain_two, grad_bias_two = second_pull(
        cotangent.reshape(row_count, D).astype(jnp.float32)
    )
    grad_second = grad_two.astype(jnp.bfloat16)
    grad_down = jnp.einsum("rf,rd->fd", activated, grad_second, preferred_element_type=jnp.float32)
    grad_bias_down = jnp.sum(grad_second.astype(jnp.float32), axis=0)
    grad_activated = jnp.einsum(
        "rd,fd->rf", grad_second, mat_down, preferred_element_type=jnp.float32
    )
    grad_hidden = gelu_pull(grad_activated)[0].astype(jnp.bfloat16)
    grad_up = jnp.einsum("rd,rf->df", first_low, grad_hidden, preferred_element_type=jnp.float32)
    grad_up_bias = jnp.sum(grad_hidden.astype(jnp.float32), axis=0)
    grad_first = grad_two + jnp.einsum(
        "rf,df->rd", grad_hidden, mat_up, preferred_element_type=jnp.float32
    )
    grad_res_one, grad_gain_one, grad_bias_one = first_pull(grad_first)
    attn_pieces = (
        lax.all_gather(w_query, ("blk", "dp"), axis=0, tiled=True),
        lax.all_gather(w_key, ("blk", "dp"), axis=0, tiled=True),
        lax.all_gather(w_value, ("blk", "dp"), axis=0, tiled=True),
        lax.all_gather(w_out, ("blk", "dp"), axis=0, tiled=True),
        lax.all_gather(vectors, ("blk", "dp"), axis=0, tiled=True),
    )
    mat_query, mat_key, mat_value, mat_out, vec_rows = attention_mats(attn_pieces)
    grad_branch = grad_res_one.astype(jnp.bfloat16)
    grad_out = jnp.einsum(
        "rd,re->de", context_rows, grad_branch, preferred_element_type=jnp.float32
    )
    grad_bias_out = jnp.sum(grad_branch.astype(jnp.float32), axis=0)
    grad_context = jnp.einsum(
        "re,de->rd", grad_branch, mat_out, preferred_element_type=jnp.float32
    ).astype(jnp.bfloat16)
    back_inputs = (
        attn_inputs[0],
        attn_inputs[1],
        attn_inputs[2],
        key_valid,
        log_total,
        grad_context.reshape(head_shape),
    )
    grad_queries, grad_key_used, grad_value_used = lax.map(attend_backward, back_inputs)
    grad_queries = grad_queries.reshape(row_count, D)
    grad_key_used = grad_key_used.reshape(row_count, D)
    grad_value_used = grad_value_used.reshape(row_count, D)
    returned = partner(jnp.stack((grad_key_used, grad_value_used)), "blk", 0)
    partner_grad_keys = returned[0]
    partner_grad_values = returned[1]
    grad_keys = jnp.where(swapped_cols, partner_grad_keys, grad_key_used)
    grad_values = jnp.where(swapped_cols, partner_grad_values, grad_value_used)
    grad_query_w = jnp.einsum("rd,re->de", inputs, grad_queries, preferred_element_type=jnp.float32)
    grad_key_w = jnp.einsum("rd,re->de", inputs, grad_keys, preferred_element_type=jnp.float32)
    grad_value_w = jnp.einsum("rd,re->de", inputs, grad_values, preferred_element_type=jnp.float32)
    grad_bias_query = jnp.sum(grad_queries.astype(jnp.float32), axis=0)
    grad_bias_value = jnp.sum(grad_values.astype(jnp.float32), axis=0)
    grad_inputs = grad_res_one + jnp.einsum(
        "re,de->rd", grad_queries, mat_query, preferred_element_type=jnp.float32
    )
    grad_inputs = grad_inputs + jnp.einsum(
        "re,de->rd", grad_keys, mat_key, preferred_element_type=jnp.float32
    )
    grad_inputs = grad_inputs + jnp.einsum(
        "re,de->rd", grad_values, mat_value, preferred_element_type=jnp.float32
    )
    grad_vectors = jnp.stack(
        (
            grad_bias_query,
            grad_bias_value,
            grad_bias_out,
            grad_gain_one,
            grad_bias_one,
            grad_bias_down,
            grad_gain_two,
            grad_bias_two,
        )
    ).reshape(-1)
    every_sum = (
        lax.psum_scatter(grad_query_w.reshape(-1), ("blk", "dp"), scatter_dimension=0, tiled=True),
        lax.psum_scatter(grad_key_w.reshape(-1), ("blk", "dp"), scatter_dimension=0, tiled=True),
        lax.psum_scatter(grad_value_w.reshape(-1), ("blk", "dp"), scatter_dimension=0, tiled=True),
        lax.psum_scatter(grad_out.reshape(-1), ("blk", "dp"), scatter_dimension=0, tiled=True),
        lax.psum_scatter(grad_vectors, ("blk", "dp"), scatter_dimension=0, tiled=True),
        lax.psum_scatter(grad_up.reshape(-1), ("blk", "dp"), scatter_dimension=0, tiled=True),
        lax.psum_scatter(grad_down.reshape(-1), ("blk", "dp"), scatter_dimension=0, tiled=True),
        lax.psum_scatter(grad_up_bias, ("blk", "dp"), scatter_dimension=0, tiled=True),
    )
    attn_sums = every_sum[0:5]
    up_sum, down_sum, up_bias_sum = (every_sum[5], every_sum[6], every_sum[7])
    return (
        activations,
        grad_inputs.reshape(tokens.shape),
        attn_sums[0],
        attn_sums[1],
        attn_sums[2],
        attn_sums[3],
        up_sum,
        down_sum,
        up_bias_sum,
        attn_sums[4],
    )


def solution(mesh):
    placed = (
        P("dp", "blk", None, None),
        P("dp", "blk", None, None),
        P("dp", None),
        P(),
        P(("blk", "dp")),
        P(("blk", "dp")),
        P(("blk", "dp")),
        P(("blk", "dp")),
        P(("blk", "dp")),
        P(("blk", "dp")),
        P(("blk", "dp")),
        P(("blk", "dp")),
    )
    return jax.shard_map(
        body,
        mesh=mesh,
        in_specs=placed,
        out_specs=(
            P("dp", "blk", None, None),
            P("dp", "blk", None, None),
            P(("blk", "dp")),
            P(("blk", "dp")),
            P(("blk", "dp")),
            P(("blk", "dp")),
            P(("blk", "dp")),
            P(("blk", "dp")),
            P(("blk", "dp")),
            P(("blk", "dp")),
        ),
        check_vma=False,
    )
```

profile of v0, /device:TPU:0, one launch (start us, length us, event | category | flops | bytes accessed | tf_op | source)
XLA Modules:
  0.0 1021.6 jit_solution(13917068625463576183)
XLA Ops:
  12.3 42.3 %all-reduce.12 = (bf16[6144]{0:T(1024)(128)(2,1)S(1)}, bf16[3072]{0:T(1024)(128)(2,1)S(1)}) all-reduce(bf16[6144]{0:T(1024)(128)(2,1)S(1)} %dynamic-update-slice, bf16[3072]{0:T(1024)(128)(2,1)S(1)} %dynamic-update-slice.1), channel_id=1, replica_groups=mesh['blk'=4,'dp'=8] {'blk','dp'}, use_global_device_ids=true, to_apply=%add | all-reduce | flops 9216 | bytes 36864
  55.3 12.7 %all-gather.7.cloned.1.call-done = bf16[589824]{0:T(1024)(128)(2,1)} async-done(((bf16[18432]{0:T(1024)(128)(2,1)}), bf16[589824]{0:T(1024)(128)(2,1)}) %all-gather.7.cloned.1.call-update) | async-done | bytes 1179664 | tf_op jit(solution)/shard_map/all_gather | solution.py:130
  67.9 3.4 reshape.284
  71.3 52.7 %all-gather.9.cloned.1.call-done = bf16[589824]{0:T(1024)(128)(2,1)} async-done(((bf16[18432]{0:T(1024)(128)(2,1)}), bf16[589824]{0:T(1024)(128)(2,1)}) %all-gather.9.cloned.1.call-update) | async-done | bytes 1179664 | tf_op jit(solution)/shard_map/all_gather | solution.py:131
  126.6 3.6 convolution_convert_fusion.1
  134.8 45.2 %all-gather.11.cloned.1.call-done = bf16[589824]{0:T(1024)(128)(2,1)} async-done(((bf16[18432]{0:T(1024)(128)(2,1)}), bf16[589824]{0:T(1024)(128)(2,1)}) %all-gather.11.cloned.1.call-update) | async-done | bytes 1179664 | tf_op jit(solution)/shard_map/all_gather | solution.py:129
  183.6 4.0 add_convert_fusion.2
  193.4 42.4 %all-gather.13.cloned.1.call-done = bf16[589824]{0:T(1024)(128)(2,1)} async-done(((bf16[18432]{0:T(1024)(128)(2,1)}), bf16[589824]{0:T(1024)(128)(2,1)}) %all-gather.13.cloned.1.call-update) | async-done | bytes 1179664 | tf_op jit(solution)/shard_map/all_gather | solution.py:132
  235.9 3.3 reshape.291
  239.2 4.3 fusion.69
  246.2 4.0 reshape.286
  254.7 3.8 reshape.289
  261.5 25.2 %while.26 = (s32[]{:T(128)}, bf16[2,512,12,64]{1,3,2,0:T(8,128)(2,1)}, f32[2,12,512]{2,1,0:T(8,128)S(1)}, bf16[2,512,12,64]{1,3,2,0:T(8,128)(2,1)}, pred[2,12,51...) while((s32[]{:T(128)}, ...), condition=%wide.region_3.4_spmd, body=%wide.region_0.3_spmd.sunk | while | flops 840296448 | bytes 60043448 | solution.py:158
  261.5 4.5 fusion.141
  269.1 3.9 fusion.142
  274.1 4.5 fusion.141
  281.6 3.9 fusion.142
  286.7 4.2 copy.78
  293.7 7.8 all-gather.15.cloned.1.call-done
  301.5 8.4 reshape.292
  309.9 35.8 %multiply_convert_fusion.3 = (bf16[1024,3072]{1,0:T(8,128)(2,1)}, f32[1024,3072]{1,0:T(8,128)}, f32[1024,3072]{1,0:T(8,128)}) fusion(f32[3072]{0:T(1024)S(1)} %convert_element_type.104, bf16[768,3072]{1,0:T(8,128)(2,1)} %reshape.292, f32[1024,768]{1,0:T(8,128)S(1)} %get-tuple-element.265, f32[768]{0:T(1024)S(1)} %get-tuple-element.260, ...), kind=kOutput, calls=%fused_computation.67 | convolution fusion | flops 5043388416 | bytes 39348224 | tf_op jit(solution)/shard_map/dot_general | solution.py:33
  345.7 20.7 %all-gather.17.cloned.1.call-done = bf16[2359296]{0:T(1024)(128)(2,1)} async-done(((bf16[73728]{0:T(1024)(128)(2,1)}), bf16[2359296]{0:T(1024)(128)(2,1)}) %all-gather.17.cloned.1.call-update) | async-done | bytes 4718608 | tf_op jit(solution)/shard_map/all_gather | solution.py:137
  366.4 9.2 reshape.293
  375.7 8.8 fusion.89
  392.4 19.2 %convert_reduce_fusion = (f32[3072]{0:T(1024)}, bf16[1024,3072]{1,0:T(8,128)(2,1)}) fusion(f32[1024,3072]{1,0:T(8,128)} %get-tuple-element.248, bf16[1024,768]{1,0:T(8,128)(2,1)} %get-tuple-element.240, bf16[3072,768]{1,0:T(8,128)(2,1)} %reshape.293, f32[1024,3072]{1,0:T(8,128)} %get-tuple-element.266, f32[3072]{0:T(1024)S(1)} %convert_element_type.104), kind=kOutput, calls=%fused_computation.65 | convolution fusion | flops 4885312512 | bytes 37773312 | tf_op jit(solution)/shard_map/rd,fd->rf/dot_general | solution.py:181
  411.6 10.1 multiply_reduce_fusion.1
  437.0 51.0 %while.27 = (s32[]{:T(128)}, bf16[2,512,12,64]{1,3,2,0:T(8,128)(2,1)}, bf16[2,512,12,64]{1,3,2,0:T(8,128)(2,1)}, bf16[2,512,12,64]{1,3,2,0:T(8,128)(2,1)}, bf16[...) while((s32[]{:T(128)}, ...), condition=%wide.region_14.15_spmd, body=%wide.region_12.14_spmd.sunk | while | flops 2062411776 | bytes 152796528 | solution.py:215
  439.1 7.1 multiply_reduce_fusion.6
  446.3 7.0 multiply_convert_fusion.5
  456.8 4.7 fusion.154
  464.5 7.1 multiply_reduce_fusion.6
  471.7 7.0 multiply_convert_fusion.5
  482.2 4.7 fusion.154
  500.9 4.0 pad_maximum_fusion.1
  514.7 3.7 reshape.301
  518.4 7.9 convolution_bitcast_fusion
  526.4 5.8 copy.104
  532.2 10.2 fusion.92
  542.4 11.2 %reshape.303 = f32[2359296]{0:T(1024)} reshape(f32[3072,768]{1,0:T(8,128)} %fusion.92) | data formatting | bytes 18874368 | tf_op jit(solution)/shard_map/reshape | solution.py:257
  553.7 4.3 convolution_bitcast_fusion.2
  561.2 3.3 reshape.299
  564.5 4.3 convolution_bitcast_fusion.1
  571.9 3.2 reshape.300
  582.3 4.9 fusion.90
  589.1 41.7 %all-reduce.10 = (f32[3072]{0:T(1024)S(1)}, f32[6144]{0:T(1024)S(1)}) all-reduce(f32[3072]{0:T(1024)S(1)} %copy-done.62, f32[6144]{0:T(1024)S(1)} %reshape.309), channel_id=8, replica_groups=mesh['blk'=4,'dp'=8] {'blk','dp'}, use_global_device_ids=true, to_apply=%region_22.23.clone | all-reduce | flops 9216 | bytes 73728
  632.1 4.0 fusion.77
  636.9 4.7 add_add_fusion.2
  641.7 363.2 %all-reduce.15.cloned.1.call-done = (f32[589824]{0:T(1024)}, f32[589824]{0:T(1024)}, f32[589824]{0:T(1024)}, f32[589824]{0:T(1024)}, f32[2359296]{0:T(1024)}, /*index=5*/f32[2359296]{0:T(1024)}) async-done(((f32[589824]{0:T(1024)}, f32[589824]{0:T(1024)}, f32[589824]{0:T(1024)}, f32[589824]{0:T(1024)}, f32[2359296]{0:T(1024)}, /*index=5*/f32[2359296]{0:T(1024)}), (f32[589824]{0:T(1024)}, f32[589824]{0:T(1024)}, ...) | async-done | bytes 28311568
  (287 shorter events, 128.3 us)
Async XLA Ops:
  7.2 60.8 %all-gather.7.cloned.1.call-start = ((), (), s32[]{:S(2)}) async-start(), calls=%async_computation | async-start | bytes 1216512 | tf_op jit(solution)/shard_map/all_gather | solution.py:130
  7.9 116.1 %all-gather.9.cloned.1.call-start = ((), (), s32[]{:S(2)}) async-start(), calls=%async_computation.1 | async-start | bytes 1216512 | tf_op jit(solution)/shard_map/all_gather | solution.py:131
  8.7 171.3 %all-gather.11.cloned.1.call-start = ((), (), s32[]{:S(2)}) async-start(), calls=%async_computation.2 | async-start | bytes 1216512 | tf_op jit(solution)/shard_map/all_gather | solution.py:129
  9.4 226.5 %all-gather.13.cloned.1.call-start = ((), (), s32[]{:S(2)}) async-start(), calls=%async_computation.3 | async-start | bytes 1216512 | tf_op jit(solution)/shard_map/all_gather | solution.py:132
  10.0 291.5 %all-gather.15.cloned.1.call-start = ((), (), s32[]{:S(2)}) async-start(), calls=%async_computation.4 | async-start | bytes 4866048 | tf_op jit(solution)/shard_map/all_gather | solution.py:136
  10.6 355.8 %all-gather.17.cloned.1.call-start = ((), (), s32[]{:S(2)}) async-start(), calls=%async_computation.5 | async-start | bytes 4866048 | tf_op jit(solution)/shard_map/all_gather | solution.py:137
  55.3 320.4 %copy-start.49 = (f32[768]{0:T(1024)}, f32[768]{0:T(1024)S(1)}, u32[]{:S(2)}) copy-start(f32[768]{0:T(1024)S(1)} %get-tuple-element.260) | copy-start | bytes 9220
  55.3 366.5 %copy-start.47 = (f32[768]{0:T(1024)}, f32[768]{0:T(1024)S(1)}, u32[]{:S(2)}) copy-start(f32[768]{0:T(1024)S(1)} %get-tuple-element.259) | copy-start | bytes 9220
  133.8 105.4 %collective-permute-start = (bf16[2,1024,768]{2,1,0:T(8,128)(2,1)}, bf16[2,1024,768]{2,1,0:T(8,128)(2,1)}, u32[]{:S(2)}, u32[]{:S(2)}) collective-permute-start(bf16[2,1024,768]{2,1,0:T(8,128)(2,1)} %pad_maximum_fusion), channel_id=1, source_target_pairs={{0,8},{8,0},{16,24},{24,16},{1,9},{9,1},{17,25},{25,17},{2,10},{10... | collective-permute-start | bytes 9437192 | tf_op jit(solution)/shard_map/ppermute | solution.py:22
  134.0 870.9 %all-reduce.15.cloned.1.call-start = ((), (), s32[]{:S(2)}) async-start(), calls=%async_computation.6 | async-start | bytes 56623104
  134.5 104.7 %copy-start.56 = (pred[768]{0:T(1024)(128)(4,1)}, pred[768]{0:T(1024)(128)(4,1)S(1)}, u32[]{:S(2)}) copy-start(pred[768]{0:T(1024)(128)(4,1)S(1)} %broadcast_in_dim.103) | copy-start | bytes 2308
  246.2 6.9 copy-start.20
  286.7 4.7 copy-start
  286.7 4.7 copy-start.2
  286.7 4.7 copy-start.39
  286.7 4.7 copy-start.41
  286.7 4.7 copy-start.37
  286.7 4.7 copy-start.69
  293.1 128.6 %copy-start.4 = (f32[1024,768]{1,0:T(8,128)}, f32[1024,768]{1,0:T(8,128)S(1)}, u32[]{:S(2)}) copy-start(f32[1024,768]{1,0:T(8,128)S(1)} %get-tuple-element.265) | copy-start | bytes 9437188
  293.1 128.6 %copy-start.43 = (f32[1024]{0:T(1024)}, f32[1024]{0:T(1024)S(1)}, u32[]{:S(2)}) copy-start(f32[1024]{0:T(1024)S(1)} %broadcast_multiply_fusion.1) | copy-start | bytes 12292
  293.6 16.3 %copy-start.53 = (f32[1024]{0:T(1024)}, f32[1024]{0:T(1024)S(1)}, u32[]{:S(2)}) copy-start(f32[1024]{0:T(1024)S(1)} %multiply_reduce_fusion.4) | copy-start | bytes 12292
  293.6 128.1 %copy-start.45 = (f32[1024]{0:T(1024)}, f32[1024]{0:T(1024)S(1)}, u32[]{:S(2)}) copy-start(f32[1024]{0:T(1024)S(1)} %fusion.79) | copy-start | bytes 12292
  345.7 30.0 %copy-start.63 = (f32[768]{0:T(1024)S(1)}, f32[768]{0:T(1024)}, u32[]{:S(2)}) copy-start(f32[768]{0:T(1024)} %get-tuple-element.258) | copy-start | bytes 9220
  411.6 10.1 copy-start.54
  433.1 3.9 copy-start.1
  433.1 3.9 copy-start.3
  433.1 3.9 copy-start.40
  433.1 3.9 copy-start.42
  446.2 7.1 copy-start.15
  456.7 4.8 copy-start.22
  471.7 7.1 copy-start.15
  482.2 4.8 copy-start.22
  491.1 5.0 copy-start.25
  500.9 4.0 copy-start.11
  500.9 4.2 copy-start.17
  504.9 48.8 %collective-permute-start.1 = (bf16[2,1024,768]{2,1,0:T(8,128)(2,1)}, bf16[2,1024,768]{2,1,0:T(8,128)(2,1)}, u32[]{:S(2)}, u32[]{:S(2)}) collective-permute-start(bf16[2,1024,768]{2,1,0:T(8,128)(2,1)} %pad_maximum_fusion.1), channel_id=1, source_target_pairs={{0,8},{8,0},{16,24},{24,16},{1,9},{9,1},{17,25},{25,17},{2,10},{10... | collective-permute-start | bytes 9437192 | tf_op jit(solution)/shard_map/ppermute | solution.py:22
  514.7 3.7 copy-start.44
  514.7 3.7 copy-start.46
  514.7 3.7 copy-start.48
  514.7 3.8 copy-start.50
  526.4 5.9 copy-start.35
  542.4 11.3 %copy-start.28 = (bf16[1,1024,768]{2,1,0:T(8,128)(2,1)S(1)}, bf16[1,1024,768]{2,1,0:T(8,128)(2,1)}, u32[]{:S(2)}) copy-start(bf16[1,1024,768]{2,1,0:T(8,128)(2,1)} %copy.87) | copy-start | bytes 4718596
  542.4 11.3 %copy-start.57 = (pred[768]{0:T(1024)(128)(4,1)S(1)}, pred[768]{0:T(1024)(128)(4,1)}, u32[]{:S(2)}) copy-start(pred[768]{0:T(1024)(128)(4,1)} %copy-done.56) | copy-start | bytes 2308
  542.4 11.3 %copy-start.71 = (bf16[2,1,512,768]{3,2,1,0:T(8,128)(2,1)S(1)}, bf16[2,1,512,768]{3,2,1,0:T(8,128)(2,1)}, u32[]{:S(2)}) copy-start(bf16[2,1,512,768]{3,2,1,0:T(8,128)(2,1)} %param.16) | copy-start | bytes 4718596
  632.1 4.1 copy-start.7
  632.1 4.1 copy-start.30
  632.1 4.8 copy-start.31
  632.1 4.8 copy-start.52
  (44 other events, 104.7 us)
Sparse Core Ops, SparseCore 0:
  11.0 56.9 all-gather.6
  70.9 53.0 all-gather.8
  127.0 52.9 all-gather.10
  182.8 52.9 all-gather.12
  238.7 62.7 all-gather.14
  304.3 62.0 all-gather.16
  575.3 429.5 all-reduce.14
where the time goes:
time: 1030 us; the launch traced here: 1020 us
  waiting for transfers between devices  548 us (53%)
  matrix products  182 us (18%)
  local copies, waits for them, and re-layouts  144 us (14%)
  blocking collectives  84.1 us (8%)
  other arithmetic  46.1 us (4%)
  between operations  15.5 us (2%)
    unnamed x8, waiting for transfers between devices  366 us
    unnamed x2, blocking collectives  84.1 us
    dot_general x6, matrix products, matmul(): return jnp.dot(left_side, right_side, preferred_element_type=jnp.float32)  55.2 us
    all_gather x1, waiting for transfers between devices, body(): lax.all_gather(w_value, ('blk', 'dp'), axis=0, tiled=True)  52.7 us
    all_gather x1, waiting for transfers between devices, body(): lax.all_gather(w_query, ('blk', 'dp'), axis=0, tiled=True)  45.2 us
    all_gather x1, waiting for transfers between devices, body(): lax.all_gather(w_out, ('blk', 'dp'), axis=0, tiled=True)  42.4 us
    unnamed x138, local copies, waits for them, and re-layouts  27 us
    all_gather x1, waiting for transfers between devices, body(): lax.all_gather(w_down, ('blk', 'dp'), axis=0, tiled=True)  20.7 us
  transfers between devices with their start and end apart: 9, of which 7 were waited for; matrix products, arithmetic and copies ran while one was open for 19% of the time, Pallas kernels for 0%

commit v1 on v0

v1 whole, which is shorter than its diff:
```python
from functools import partial

import jax
import jax.numpy as jnp
from jax import lax
from jax.experimental import pallas as pl
from jax.experimental.pallas import tpu as pltpu
from jax.sharding import PartitionSpec as P

D = 768
H = 12
HD = 64
FF = 3072
BLOCK = 512
HALF = D // 2
PAIR = 2 * HD
LANES = 128
GROUPS_W = 32
ROWS = D // GROUPS_W

norm_eps = 1e-05
masked_fill = -1000000000.0
LOG2E = 1.4426950408889634
SQRT_HALF = 0.7071067811865476
INV_SQRT_2PI = 0.3989422804014327

bf16 = jnp.bfloat16
f32 = jnp.float32
BOTH = ("blk", "dp")


def partner(value, axis, distance):
    mask = 2**distance
    pairs = [(source, source ^ mask) for source in range(lax.axis_size(axis))]
    return lax.ppermute(value, axis, pairs)


def dot_nn(a, b):
    return lax.dot_general(a, b, (((1,), (0,)), ((), ())), preferred_element_type=f32)


def dot_nt(a, b):
    return lax.dot_general(a, b, (((1,), (1,)), ((), ())), preferred_element_type=f32)


def dot_tn(a, b):
    return lax.dot_general(a, b, (((0,), (0,)), ((), ())), preferred_element_type=f32)


def whole(shape):
    return pl.BlockSpec(shape, lambda *_: (0,) * len(shape))


def call(body, grid, in_specs, out_specs, out_shape, scratch=(), prefetch=0, flops=0, moved=0, name=None):
    return pl.pallas_call(
        body,
        grid_spec=pltpu.PrefetchScalarGridSpec(
            num_scalar_prefetch=prefetch,
            grid=grid,
            in_specs=in_specs,
            out_specs=out_specs,
            scratch_shapes=list(scratch),
        ),
        out_shape=out_shape,
        compiler_params=pltpu.CompilerParams(vmem_limit_bytes=60 * 1024 * 1024),
        cost_estimate=pl.CostEstimate(flops=flops, bytes_accessed=moved, transcendentals=0),
        name=name,
    )


def sds(shape, dtype):
    return jax.ShapeDtypeStruct(shape, dtype)


def square(ref):
    return ref[...].reshape(D, D)


def project_body(x_ref, xp_ref, wq_ref, wk_ref, wv_ref, bias_ref, q_ref, k_ref, v_ref):
    own, other = x_ref[...], xp_ref[...]
    q_ref[...] = (dot_nn(own, square(wq_ref)) + bias_ref[0:1, :]).astype(bf16)
    wk, wv = square(wk_ref), square(wv_ref)
    k_ref[:, :HALF] = dot_nn(other, wk[:, :HALF]).astype(bf16)
    k_ref[:, HALF:] = dot_nn(own, wk[:, HALF:]).astype(bf16)
    v_ref[:, :HALF] = (dot_nn(other, wv[:, :HALF]) + bias_ref[1:2, :HALF]).astype(bf16)
    v_ref[:, HALF:] = (dot_nn(own, wv[:, HALF:]) + bias_ref[1:2, HALF:]).astype(bf16)


def project(x, xp, pack, bias):
    rows = x.shape[0]
    step = BLOCK
    row_spec = pl.BlockSpec((step, D), lambda i: (i, 0))
    weight = [pl.BlockSpec((GROUPS_W, ROWS, D), lambda i, s=s: (0, s, 0)) for s in range(3)]
    return call(
        project_body,
        (rows // step,),
        [row_spec, row_spec, *weight, whole((8, D))],
        [row_spec] * 3,
        [sds((rows, D), bf16)] * 3,
        flops=6 * rows * D * D,
        moved=16 * rows * D,
        name="project",
    )(x, xp, pack, pack, pack, bias)


def attend_body(valid_ref, q_ref, k_ref, v_ref, ctx_ref, p_ref):
    seq, pair = pl.program_id(0), pl.program_id(1)
    valid = valid_ref[seq, pair // 3]
    queries, keys, values = q_ref[...], k_ref[...], v_ref[...]
    lane = lax.broadcasted_iota(jnp.int32, (BLOCK, PAIR), 1)
    key_row = lax.broadcasted_iota(jnp.int32, (BLOCK, 1), 0)
    fill = jnp.where(key_row < valid, 0.0, masked_fill * LOG2E)
    parts = []
    for head in range(2):
        mine = (lane < HD) if head == 0 else (lane >= HD)
        masked = jnp.where(mine, queries, jnp.zeros_like(queries))
        scores = dot_nt(keys, masked) * (LOG2E * HD ** (-0.5)) + fill
        top = jnp.max(scores, axis=0, keepdims=True)
        weights = jnp.exp2(scores - top)
        total = jnp.sum(weights, axis=0, keepdims=True)
        probs = (weights * (1.0 / total)).astype(bf16)
        p_ref[0, head] = probs
        parts.append(dot_tn(probs, values))
    ctx_ref[...] = jnp.where(lane < HD, parts[0], parts[1]).astype(bf16)


def attend(valid, q, k, v):
    rows = q.shape[0]
    seqs = rows // BLOCK
    spec = pl.BlockSpec((BLOCK, PAIR), lambda s, j, *_: (s, j))
    return call(
        attend_body,
        (seqs, H // 2),
        [spec] * 3,
        [spec, pl.BlockSpec((1, 2, BLOCK, BLOCK), lambda s, j, *_: (s, j, 0, 0))],
        [sds((rows, D), bf16), sds((seqs, H, BLOCK, BLOCK), bf16)],
        prefetch=1,
        flops=16 * rows * BLOCK * D,
        moved=8 * rows * D + 2 * rows * H * BLOCK,
        name="attend",
    )(valid, q, k, v)


def attend_back_body(q_ref, k_ref, v_ref, p_ref, gctx_ref, delta_ref, out_ref):
    pair = pl.program_id(1)
    queries, keys, values, grad_ctx = q_ref[...], k_ref[...], v_ref[...], gctx_ref[...]
    lane = lax.broadcasted_iota(jnp.int32, (BLOCK, PAIR), 1)
    scale = HD ** (-0.5)
    gq, gk, gv = [], [], []
    for head in range(2):
        mine = (lane < HD) if head == 0 else (lane >= HD)
        probs = p_ref[0, head]
        delta = delta_ref[pl.ds(2 * pair + head, 1), :]
        grad_probs = dot_nt(jnp.where(mine, values, jnp.zeros_like(values)), grad_ctx)
        grad_scores = (probs.astype(f32) * (grad_probs - delta)).astype(bf16)
        gv.append(dot_nn(probs, grad_ctx))
        gk.append(dot_nn(grad_scores, queries))
        gq.append(dot_tn(grad_scores, keys))
    first = lane < HD
    out_ref[0] = (jnp.where(first, gq[0], gq[1]) * scale).astype(bf16)
    out_ref[1] = (jnp.where(first, gk[0], gk[1]) * scale).astype(bf16)
    out_ref[2] = jnp.where(first, gv[0], gv[1]).astype(bf16)


def attend_back(q, k, v, probs, grad_ctx, delta):
    rows = q.shape[0]
    seqs = rows // BLOCK
    spec = pl.BlockSpec((BLOCK, PAIR), lambda s, j: (s, j))
    return call(
        attend_back_body,
        (seqs, H // 2),
        [spec] * 3
        + [
            pl.BlockSpec((1, 2, BLOCK, BLOCK), lambda s, j: (s, j, 0, 0)),
            spec,
            pl.BlockSpec((16, BLOCK), lambda s, j: (0, s)),
        ],
        pl.BlockSpec((3, BLOCK, PAIR), lambda s, j: (0, s, j)),
        sds((3, rows, D), bf16),
        flops=32 * rows * BLOCK * D,
        moved=14 * rows * D + 2 * rows * H * BLOCK,
        name="attend_back",
    )(q, k, v, probs, grad_ctx, delta)


def mean_last(value):
    return jnp.sum(value, axis=-1, keepdims=True) * (1.0 / D)


def first_norm_body(ctx_ref, x_ref, wo_ref, order_ref, vec_ref, hat_ref, inv_ref, low_ref, wop_ref, wo_scr):
    @pl.when(pl.program_id(0) == 0)
    def _():
        permuted = dot_tn(order_ref[...], square(wo_ref)).astype(bf16)
        wo_scr[...] = permuted
        wop_ref[...] = permuted

    branch = dot_nn(ctx_ref[...], wo_scr[...]) + vec_ref[2:3, :]
    residual = x_ref[...].astype(f32) + branch
    centred = residual - mean_last(residual)
    inv = lax.rsqrt(mean_last(centred * centred) + norm_eps)
    hat = centred * inv
    hat_ref[...] = hat
    inv_ref[...] = jnp.broadcast_to(inv, inv_ref.shape)
    low_ref[...] = (hat * vec_ref[3:4, :] + vec_ref[4:5, :]).astype(bf16)


def first_norm(ctx, x, pack, order, vecs):
    rows = x.shape[0]
    step = 256
    row_spec = pl.BlockSpec((step, D), lambda i: (i, 0))
    return call(
        first_norm_body,
        (rows // step,),
        [
            row_spec,
            row_spec,
            pl.BlockSpec((GROUPS_W, ROWS, D), lambda i: (0, 8, 0)),
            whole((D, D)),
            whole((8, D)),
        ],
        [row_spec, pl.BlockSpec((step, LANES), lambda i: (i, 0)), row_spec, whole((D, D))],
        [sds((rows, D), f32), sds((rows, LANES), f32), sds((rows, D), bf16), sds((D, D), bf16)],
        scratch=[pltpu.VMEM((D, D), bf16)],
        flops=2 * rows * D * D,
        moved=12 * rows * D,
        name="first_norm",
    )(ctx, x, pack, order, vecs)


def gelu_and_slope(value):
    size = jnp.abs(value)
    gauss = jnp.exp2(value * value * (-0.5 * LOG2E))
    knot = 1.0 / (1.0 + size * (0.3275911 * SQRT_HALF))
    poly = knot * (
        0.254829592 + knot * (-0.284496736 + knot * (1.421413741 + knot * (-1.453152027 + knot * 1.061405429)))
    )
    tail = 0.5 * poly * gauss
    normal_cdf = jnp.where(value >= 0.0, 1.0 - tail, tail)
    return value * normal_cdf, normal_cdf + value * gauss * INV_SQRT_2PI


def ffn_forward_body(
    low_ref, hat_ref, cot_ref, up_ref, down_ref, bias_ref, vec_ref,
    act_ref, slope_ref, out_ref, gtwo_ref, gsec_ref, sums_ref, acc,
):
    chunk, last = pl.program_id(1), pl.num_programs(1) - 1
    first = (pl.program_id(0) == 0) & (chunk == 0)
    rows = low_ref.shape[0]
    step = 256
    w_up = square(up_ref)
    w_down = square(down_ref)

    @pl.when(first)
    def _():
        sums_ref[...] = jnp.zeros_like(sums_ref)

    for start in range(0, rows, step):
        part = pl.ds(start, step)
        hidden = dot_nn(low_ref[part, :], w_up) + bias_ref[0]
        activated, slope = gelu_and_slope(hidden)
        activated = activated.astype(bf16)
        act_ref[part, :] = activated
        slope_ref[part, :] = slope.astype(bf16)
        down = dot_nn(activated, w_down)

        @pl.when(chunk == 0)
        def _():
            acc[part, :] = down

        @pl.when(chunk > 0)
        def _():
            acc[part, :] += down

    @pl.when(chunk == last)
    def _():
        gain, bias = vec_ref[6:7, :], vec_ref[7:8, :]

        def rows_of(index, sums):
            part = pl.ds(pl.multiple_of(index * step, step), step)
            residual = hat_ref[part, :] * vec_ref[3:4, :] + vec_ref[4:5, :] + (acc[part, :] + vec_ref[5:6, :])
            centred = residual - mean_last(residual)
            inv = lax.rsqrt(mean_last(centred * centred) + norm_eps)
            hat = centred * inv
            out_ref[part, :] = (hat * gain + bias).astype(bf16)
            cot = cot_ref[part, :].astype(f32)
            scaled = cot * gain
            grad = inv * (scaled - mean_last(scaled) - hat * mean_last(scaled * hat))
            gtwo_ref[part, :] = grad
            low = grad.astype(bf16)
            gsec_ref[part, :] = low
            return (
                sums[0] + jnp.sum(cot * hat, axis=0, keepdims=True),
                sums[1] + jnp.sum(cot, axis=0, keepdims=True),
                sums[2] + jnp.sum(low.astype(f32), axis=0, keepdims=True),
            )

        zero = jnp.zeros((1, D), f32)
        sums = lax.fori_loop(0, rows // step, rows_of, (zero, zero, zero))
        for index, value in enumerate(sums):
            sums_ref[index : index + 1, :] += value


def ffn_forward(low, hat, cot, pack, up_bias, vecs):
    rows = low.shape[0]
    span = 1024
    chunks = FF // D
    row_spec = pl.BlockSpec((span, D), lambda r, c: (r, 0))
    wide = pl.BlockSpec((span, D), lambda r, c: (r, c))
    return call(
        ffn_forward_body,
        (rows // span, chunks),
        [
            row_spec,
            row_spec,
            row_spec,
            pl.BlockSpec((GROUPS_W, ROWS, D), lambda r, c: (0, 4 + c, 0)),
            pl.BlockSpec((GROUPS_W // 4, 4 * ROWS, D), lambda r, c: (c, 0, 0)),
            pl.BlockSpec((1, 1, D), lambda r, c: (c, 0, 0)),
            whole((8, D)),
        ],
        [wide, wide, row_spec, row_spec, row_spec, whole((8, D))],
        [
            sds((rows, FF), bf16),
            sds((rows, FF), bf16),
            sds((rows, D), bf16),
            sds((rows, D), f32),
            sds((rows, D), bf16),
            sds((8, D), f32),
        ],
        scratch=[pltpu.VMEM((span, D), f32)],
        flops=4 * rows * D * FF,
        moved=26 * rows * D + 4 * D * FF,
        name="ffn_forward",
    )(low, hat, cot, pack, pack, up_bias, vecs)


def grad_down_body(act_ref, gsec_ref, out_ref):
    out_ref[...] = dot_tn(act_ref[...], gsec_ref[...]).astype(bf16).reshape(out_ref.shape)


def grad_down_of(act, gsec):
    rows = act.shape[0]
    return call(
        grad_down_body,
        (FF // D,),
        [pl.BlockSpec((rows, D), lambda c: (0, c)), whole((rows, D))],
        pl.BlockSpec((GROUPS_W // 4, 4 * ROWS, D), lambda c: (c, 0, 0)),
        sds((GROUPS_W, 4 * ROWS, D), bf16),
        flops=2 * rows * D * FF,
        moved=10 * rows * D + 2 * D * FF,
        name="grad_down",
    )(act, gsec)


def ffn_backward_body(gsec_ref, slope_ref, low_ref, up_ref, down_ref, gup_ref, gbias_ref, acc_ref):
    chunk = pl.program_id(0)
    grad_act = dot_nt(gsec_ref[...], square(down_ref))
    grad_hidden = (grad_act * slope_ref[...].astype(f32)).astype(bf16)
    gbias_ref[0] = jnp.sum(grad_hidden.astype(f32), axis=0, keepdims=True)
    gup_ref[...] = dot_tn(low_ref[...], grad_hidden).astype(bf16).reshape(gup_ref.shape)
    back = dot_nt(grad_hidden, square(up_ref))

    @pl.when(chunk == 0)
    def _():
        acc_ref[...] = back

    @pl.when(chunk > 0)
    def _():
        acc_ref[...] += back


def ffn_backward(gsec, slope, low, pack):
    rows = gsec.shape[0]
    return call(
        ffn_backward_body,
        (FF // D,),
        [
            whole((rows, D)),
            pl.BlockSpec((rows, D), lambda c: (0, c)),
            whole((rows, D)),
            pl.BlockSpec((GROUPS_W, ROWS, D), lambda c: (0, 4 + c, 0)),
            pl.BlockSpec((GROUPS_W // 4, 4 * ROWS, D), lambda c: (c, 0, 0)),
        ],
        [
            pl.BlockSpec((GROUPS_W, ROWS, D), lambda c: (0, c, 0)),
            pl.BlockSpec((1, 1, D), lambda c: (c, 0, 0)),
            whole((rows, D)),
        ],
        [sds((GROUPS_W, 4 * ROWS, D), bf16), sds((FF // D, 1, D), f32), sds((rows, D), f32)],
        flops=6 * rows * D * FF,
        moved=16 * rows * D + 6 * D * FF,
        name="ffn_backward",
    )(gsec, slope, low, pack, pack)


def first_back_body(
    acc_ref, gtwo_ref, hat_ref, inv_ref, ctx_ref, wop_ref, order_ref, vec_ref,
    gres_ref, gctx_ref, gout_ref, delta_ref, sums_ref, gout_scr,
):
    index, last = pl.program_id(0), pl.num_programs(0) - 1
    hat = hat_ref[...]
    inv = inv_ref[:, 0:1]
    grad_first = gtwo_ref[...] + acc_ref[...]
    scaled = grad_first * vec_ref[3:4, :]
    grad = inv * (scaled - mean_last(scaled) - hat * mean_last(scaled * hat))
    gres_ref[...] = grad
    low = grad.astype(bf16)
    ctx = ctx_ref[...]
    grad_ctx = dot_nt(low, wop_ref[...]).astype(bf16)
    gctx_ref[...] = grad_ctx
    head = lax.broadcasted_iota(jnp.int32, (16, D), 0)
    owner = lax.broadcasted_iota(jnp.int32, (16, D), 1) // HD
    chooser = jnp.where(head == owner, 1.0, 0.0).astype(f32)
    product = grad_ctx.astype(f32) * ctx.astype(f32)
    delta_ref[...] = lax.dot_general(
        chooser, product, (((1,), (1,)), ((), ())), preferred_element_type=f32, precision=lax.Precision.HIGHEST
    )
    grad_out = dot_tn(ctx, low)

    @pl.when(index == 0)
    def _():
        gout_scr[...] = grad_out
        sums_ref[...] = jnp.zeros_like(sums_ref)

    @pl.when(index > 0)
    def _():
        gout_scr[...] += grad_out

    sums_ref[0:1, :] += jnp.sum(grad_first * hat, axis=0, keepdims=True)
    sums_ref[1:2, :] += jnp.sum(grad_first, axis=0, keepdims=True)
    sums_ref[2:3, :] += jnp.sum(low.astype(f32), axis=0, keepdims=True)

    @pl.when(index == last)
    def _():
        ordered = dot_nn(order_ref[...], gout_scr[...].astype(bf16))
        gout_ref[...] = ordered.astype(bf16).reshape(gout_ref.shape)


def first_back(acc, gtwo, hat, inv, ctx, wop, order, vecs):
    rows = acc.shape[0]
    step = 256
    row_spec = pl.BlockSpec((step, D), lambda i: (i, 0))
    return call(
        first_back_body,
        (rows // step,),
        [
            row_spec,
            row_spec,
            row_spec,
            pl.BlockSpec((step, LANES), lambda i: (i, 0)),
            row_spec,
            whole((D, D)),
            whole((D, D)),
            whole((8, D)),
        ],
        [
            row_spec,
            row_spec,
            whole((GROUPS_W, ROWS, D)),
            pl.BlockSpec((16, step), lambda i: (0, i)),
            whole((8, D)),
        ],
        [
            sds((rows, D), f32),
            sds((rows, D), bf16),
            sds((GROUPS_W, ROWS, D), bf16),
            sds((16, rows), f32),
            sds((8, D), f32),
        ],
        scratch=[pltpu.VMEM((D, D), f32)],
        flops=4 * rows * D * D,
        moved=20 * rows * D + 6 * D * D,
        name="first_back",
    )(acc, gtwo, hat, inv, ctx, wop, order, vecs)


def grad_project_body(x_ref, xp_ref, grad_ref, out_ref, sums_ref):
    part = pl.program_id(0)
    own = x_ref[...]
    other = jnp.where(part == 0, own, xp_ref[...])
    grad = grad_ref[0]
    left = dot_tn(other, grad[:, :HALF]).astype(bf16)
    right = dot_tn(own, grad[:, HALF:]).astype(bf16)
    out_ref[:, :, :HALF] = left.reshape(GROUPS_W, ROWS, HALF)
    out_ref[:, :, HALF:] = right.reshape(GROUPS_W, ROWS, HALF)
    sums_ref[0] = jnp.broadcast_to(jnp.sum(grad.astype(f32), axis=0, keepdims=True), (8, D))


def grad_project(x, xp, grads):
    rows = x.shape[0]
    return call(
        grad_project_body,
        (3,),
        [whole((rows, D)), whole((rows, D)), pl.BlockSpec((1, rows, D), lambda s: (s, 0, 0))],
        [pl.BlockSpec((GROUPS_W, ROWS, D), lambda s: (0, s, 0)), pl.BlockSpec((1, 8, D), lambda s: (s, 0, 0))],
        [sds((GROUPS_W, 3 * ROWS, D), bf16), sds((3, 8, D), f32)],
        flops=6 * rows * D * D,
        moved=10 * rows * D + 6 * D * D,
        name="grad_project",
    )(x, xp, grads)


def grad_input_body(gres_ref, grads_ref, back_ref, wq_ref, wk_ref, wv_ref, out_ref):
    wk, wv = square(wk_ref), square(wv_ref)
    total = gres_ref[...] + dot_nt(grads_ref[0], square(wq_ref))
    total = total + dot_nt(back_ref[:, :HALF], wk[:, :HALF]) + dot_nt(grads_ref[1][:, HALF:], wk[:, HALF:])
    total = total + dot_nt(back_ref[:, HALF:], wv[:, :HALF]) + dot_nt(grads_ref[2][:, HALF:], wv[:, HALF:])
    out_ref[...] = total


def grad_input_of(gres, grads, back, pack):
    rows = gres.shape[0]
    step = 256
    row_spec = pl.BlockSpec((step, D), lambda i: (i, 0))
    weight = [pl.BlockSpec((GROUPS_W, ROWS, D), lambda i, s=s: (0, s, 0)) for s in range(3)]
    return call(
        grad_input_body,
        (rows // step,),
        [row_spec, pl.BlockSpec((3, step, D), lambda i: (0, i, 0)), row_spec, *weight],
        row_spec,
        sds((rows, D), f32),
        flops=6 * rows * D * D,
        moved=16 * rows * D + 6 * D * D,
        name="grad_input",
    )(gres, grads, back, pack, pack, pack)


def gather(value):
    return lax.all_gather(value, BOTH, axis=0)


def scatter(value):
    return lax.psum_scatter(value, BOTH, scatter_dimension=0)


def joined(gathered, start, rows, columns=1):
    count = gathered.shape[0]
    part = gathered[:, start : start + columns * rows]
    if columns > 1:
        part = part.reshape(GROUPS_W, count // GROUPS_W, columns, rows, D).transpose(0, 2, 1, 3, 4)
    return part.reshape(GROUPS_W, -1, D)


def parted(grouped, count, rows, columns=1):
    if columns > 1:
        grouped = grouped.reshape(GROUPS_W, columns, count // GROUPS_W, rows, D).transpose(0, 2, 1, 3, 4)
    return grouped.reshape(count, columns * rows, D)


def body(tokens, cotangent, lengths, head_mode, w_query, w_key, w_value, w_out, w_up, w_down, b_up, vectors):
    seq_count = tokens.shape[0]
    row_count = seq_count * BLOCK
    devices = lax.axis_size("blk") * lax.axis_size("dp")
    own_rows = D // devices
    blk_index = lax.axis_index("blk")
    block_side = blk_index % 2
    member = blk_index // 2
    seq_lengths = jnp.where(member == 0, lengths[:, 0], lengths[:, 1])
    valid = jnp.stack(
        (
            jnp.clip(seq_lengths - (1 - block_side) * BLOCK, 0, BLOCK),
            jnp.clip(seq_lengths - block_side * BLOCK, 0, BLOCK),
        ),
        axis=1,
    ).astype(jnp.int32)
    swapped = head_mode == 1
    place = jnp.where(swapped, jnp.cumsum(swapped) - 1, H // 2 + jnp.cumsum(~swapped) - 1)
    target = jnp.repeat(place * HD, HD) + jnp.tile(jnp.arange(HD), H)
    order = (target[:, None] == jnp.arange(D)[None, :]).astype(bf16)

    inputs = tokens.reshape(row_count, D)
    other_inputs = partner(inputs, "blk", 0)

    small = jnp.concatenate((vectors, b_up))
    small = jnp.pad(small, (0, D - small.shape[0])).reshape(1, D)
    small = jnp.pad(small, ((0, 7), (0, 0)))
    stacked = jnp.concatenate([w.reshape(own_rows, D) for w in (w_query, w_key, w_value)])
    stacked = dot_nn(stacked, order).astype(bf16)
    attn_all = gather(jnp.concatenate((stacked, small)))
    ffn_all = gather(
        jnp.concatenate(
            (
                w_down.reshape(4 * own_rows, D),
                w_up.reshape(own_rows, 4, D).transpose(1, 0, 2).reshape(4 * own_rows, D),
                w_out.reshape(own_rows, D),
            )
        )
    )
    n_vec, n_bias = vectors.shape[0], b_up.shape[0]
    small_all = attn_all[:, 3 * own_rows, :]
    vec_low = small_all[:, :n_vec].reshape(8, D)
    vecs = vec_low.astype(f32)
    bias_qv = jnp.pad(dot_nn(vec_low[0:2], order), ((0, 6), (0, 0)))
    up_bias = small_all[:, n_vec : n_vec + n_bias].reshape(FF // D, 1, D).astype(f32)
    if devices == GROUPS_W:
        attn_pack, ffn_pack = attn_all, ffn_all
    else:
        attn_pack = jnp.concatenate([joined(attn_all, s * own_rows, own_rows) for s in range(3)], axis=1)
        ffn_pack = jnp.concatenate(
            (
                joined(ffn_all, 0, 4 * own_rows),
                joined(ffn_all, 4 * own_rows, own_rows, 4),
                joined(ffn_all, 8 * own_rows, own_rows),
            ),
            axis=1,
        )

    q, k, v = project(inputs, other_inputs, attn_pack, bias_qv)
    ctx, probs = attend(valid, q, k, v)
    hat, inv, low, out_weight = first_norm(ctx, inputs, ffn_pack, order, vecs)
    act, slope, output, gtwo, gsec, sums_two = ffn_forward(
        low, hat, cotangent.reshape(row_count, D), ffn_pack, up_bias, vecs
    )
    grad_down = grad_down_of(act, gsec)
    grad_up, grad_up_bias, acc = ffn_backward(gsec, slope, low, ffn_pack)
    gres, grad_ctx, grad_out, delta, sums_one = first_back(acc, gtwo, hat, inv, ctx, out_weight, order, vecs)
    grads = attend_back(q, k, v, probs, grad_ctx, delta)
    back = partner(jnp.concatenate((grads[1][:, :HALF], grads[2][:, :HALF]), axis=1), "blk", 0)
    grad_qkv, sums_qkv = grad_project(inputs, other_inputs, grads)
    grad_inputs = grad_input_of(gres, grads, back, attn_pack)

    bias_grads = lax.dot_general(
        jnp.stack((sums_qkv[0, 0], sums_qkv[2, 0])),
        order.astype(f32),
        (((1,), (1,)), ((), ())),
        precision=lax.Precision.HIGHEST,
    )
    grad_vectors = jnp.concatenate(
        (
            bias_grads,
            sums_one[2:3],
            sums_one[0:2],
            sums_two[2:3],
            sums_two[0:2],
        )
    ).reshape(devices, n_vec)
    small_grads = jnp.concatenate((grad_vectors, grad_up_bias.reshape(devices, n_bias)), axis=1)
    small_grads = jnp.pad(small_grads, ((0, 0), (0, D - n_vec - n_bias))).astype(bf16)
    small_grads = jnp.pad(small_grads[:, None, :], ((0, 0), (0, 7), (0, 0)))
    down_sum = scatter(parted(grad_down, devices, 4 * own_rows))
    rest_sum = scatter(
        jnp.concatenate(
            (
                parted(grad_up, devices, own_rows, 4),
                parted(grad_out, devices, own_rows),
                jnp.concatenate(
                    [parted(grad_qkv[:, s * ROWS : (s + 1) * ROWS], devices, own_rows) for s in range(3)], axis=1
                ),
                small_grads,
            ),
            axis=1,
        )
    ).astype(f32)
    up_sum = rest_sum[: 4 * own_rows].reshape(4, own_rows, D).transpose(1, 0, 2)
    out_sum = rest_sum[4 * own_rows : 5 * own_rows]
    qkv_sum = lax.dot_general(
        rest_sum[5 * own_rows : 8 * own_rows],
        order.astype(f32),
        (((1,), (1,)), ((), ())),
        precision=lax.Precision.HIGHEST,
    ).reshape(3, own_rows * D)
    small_sum = rest_sum[8 * own_rows]
    return (
        output.reshape(tokens.shape),
        grad_inputs.reshape(tokens.shape),
        qkv_sum[0],
        qkv_sum[1],
        qkv_sum[2],
        out_sum.reshape(-1),
        up_sum.reshape(-1),
        down_sum.astype(f32).reshape(-1),
        small_sum[n_vec : n_vec + n_bias],
        small_sum[:n_vec],
    )


def solution(mesh):
    flat = P(BOTH)
    block = P("dp", "blk", None, None)
    return jax.shard_map(
        body,
        mesh=mesh,
        in_specs=(block, block, P("dp", None), P(), *([flat] * 8)),
        out_specs=(block, block, *([flat] * 8)),
        check_vma=False,
    )
```

time: 1030 us -> 484 us (0.47)
  waiting for transfers between devices: 548 us -> 271 us
  matrix products: 182 us -> 3.92 us
  Pallas kernels: 0 us -> 153 us
  local copies, waits for them, and re-layouts: 144 us -> 22.4 us
  blocking collectives: 84.1 us -> 0 us
  other arithmetic: 46.1 us -> 16.8 us
    unnamed x8 -> x4, waiting for transfers between devices: 366 us -> 0.07 us
    dot_general x32 -> x4, matrix products: 182 us -> 3.92 us  [the longest x1 1.54 us: body(): lax.dot_general(rest_sum[5 * own_rows:8 * own_rows], order.astype(f32), (...]
    pallas_call x0 -> x10, Pallas kernels: none -> 153 us  [the longest x1 33.9 us: ffn_forward(): call(ffn_forward_body, (rows // span, chunks), [row_spec, row_spec, row_s...]
    reduce_scatter x0 -> x2, waiting for transfers between devices: none -> 153 us  [scatter(): return lax.psum_scatter(value, BOTH, scatter_dimension=0)]
    unnamed x2 -> x0, blocking collectives: 84.1 us -> none
    all_gather x6 -> x2, waiting for transfers between devices: 182 us -> 115 us  [gather(): return lax.all_gather(value, BOTH, axis=0)]
    reshape x21 -> x12, local copies, waits for them, and re-layouts: 65.7 us -> 7.09 us  [the longest x3 2.47 us: body(): w.reshape(own_rows, D)]
    unnamed x138 -> x15, local copies, waits for them, and re-layouts: 27 us -> 2.36 us
  transfers between devices with their start and end apart: 9 -> 6, of which waited for: 7 -> 5; matrix products, arithmetic and copies ran while one was open for 19% -> 5% of each run, Pallas kernels for 0% -> 21%
where the time goes in v1:
time: 484 us; the launch traced here: 483 us
  waiting for transfers between devices  271 us (56%)
  Pallas kernels  153 us (32%)
  local copies, waits for them, and re-layouts  22.4 us (5%)
  other arithmetic  16.8 us (3%)
  between operations  14 us (3%)
    reduce_scatter x2, waiting for transfers between devices, scatter(): return lax.psum_scatter(value, BOTH, scatter_dimension=0)  153 us
    all_gather x2, waiting for transfers between devices, gather(): return lax.all_gather(value, BOTH, axis=0)  115 us
    pallas_call x1, Pallas kernels, ffn_forward(): call(ffn_forward_body, (rows // span, chunks), [row_spec, row_spec, row_s...  33.9 us
    pallas_call x1, Pallas kernels, ffn_backward(): call(ffn_backward_body, (FF // D,), [whole((rows, D)), pl.BlockSpec((rows...  22.3 us
    pallas_call x1, Pallas kernels, attend_back(): call(attend_back_body, (seqs, H // 2), [spec] * 3 + [pl.BlockSpec((1, 2,...  19.3 us
    pallas_call x1, Pallas kernels, attend(): call(attend_body, (seqs, H // 2), [spec] * 3, [spec, pl.BlockSpec((1, 2,...  18.5 us
    pallas_call x1, Pallas kernels, first_back(): call(first_back_body, (rows // step,), [row_spec, row_spec, row_spec, pl....  15 us
  transfers between devices with their start and end apart: 6, of which 5 were waited for; matrix products, arithmetic and copies ran while one was open for 5% of the time, Pallas kernels for 21%

profile of v1, /device:TPU:0, one launch (start us, length us, event | category | flops | bytes accessed | tf_op | source)
XLA Modules:
  0.0 482.6 jit_solution(3086532949039908770)
XLA Ops:
  7.2 0.8 convert_bitcast_fusion.1
  8.4 0.7 fusion.31
  9.2 0.8 reshape.177
  10.0 0.8 reshape.178
  10.8 0.8 reshape.179
  11.7 0.8 fusion.29
  13.1 0.7 fusion.14
  13.8 1.0 reshape.184
  14.8 1.1 reshape.183
  15.9 0.8 reshape.186
  16.7 0.7 pad_maximum_fusion.1
  18.1 0.6 pad_add_fusion.valid_ref
  18.8 1.3 fusion.4.order_ref
  20.1 57.5 %all-gather.5.cloned.1.call-done = bf16[2560,768]{1,0:T(8,128)(2,1)} async-done(((bf16[80,768]{1,0:T(8,128)(2,1)}), bf16[2560,768]{1,0:T(8,128)(2,1)}) %all-gather.5.cloned.1.call-update) | async-done | bytes 3932176 | tf_op jit(solution)/shard_map/all_gather | solution.py:529
  77.6 1.0 slice.129
  78.7 0.7 reshape.197.vec_ref
  79.5 0.7 reshape.198.bias_ref
  81.4 1.2 copy-done.2
  82.6 8.3 %project.1 = (bf16[1024,768]{1,0:T(8,128)(2,1)}, bf16[1024,768]{1,0:T(8,128)(2,1)}, bf16[1024,768]{1,0:T(8,128)(2,1)}) custom-call(bf16[1024,768]{1,0:T(8,128)(2,1)} %bitcast.60, bf16[1024,768]{1,0:T(8,128)(2,1)} %copy-done.2, bf16[32,80,768]{2,1,0:T(8,128)(2,1)} %bitcast.49, bf16[32,80,768]{2,1,0:T(8,128)(2,1)} %bitcast.50, bf16[32,80,768]{2,1,0:T(8,128)(2,1)} %bitcast.51, ...), custom_call_target="tpu_custom_call" | custom-call | flops 3623878656 | bytes 12582912 | tf_op jit(solution)/shard_map/project/pallas_call | solution.py:94
  90.8 18.5 %attend.1 = (bf16[1024,768]{1,0:T(8,128)(2,1)}, bf16[2,12,512,512]{3,2,1,0:T(8,128)(2,1)}) custom-call(s32[2,2]{1,0:T(2,128)} %pad_add_fusion.valid_ref, bf16[1024,768]{1,0:T(8,128)(2,1)} %get-tuple-element.35.q_ref, bf16[1024,768]{1,0:T(8,128)(2,1)} %get-tuple-element.36.k_ref, bf16[1024,768]{1,0:T(8,128)(2,1)} %get-tuple-element.37.v_ref), custom_call_target="tpu_custom_call" | custom-call | flops 6442450944 | bytes 18874368 | tf_op jit(solution)/shard_map/attend/pallas_call | solution.py:131
  109.3 57.5 %all-gather.7.cloned.1.call-done = bf16[6912,768]{1,0:T(8,128)(2,1)} async-done(((bf16[216,768]{1,0:T(8,128)(2,1)}), bf16[6912,768]{1,0:T(8,128)(2,1)}) %all-gather.7.cloned.1.call-update) | async-done | bytes 10616848 | tf_op jit(solution)/shard_map/all_gather | solution.py:529
  166.8 7.9 %first_norm.1 = (f32[1024,768]{1,0:T(8,128)}, f32[1024,128]{1,0:T(8,128)}, bf16[1024,768]{1,0:T(8,128)(2,1)}, bf16[768,768]{1,0:T(8,128)(2,1)}) custom-call(bf16[1024,768]{1,0:T(8,128)(2,1)} %get-tuple-element.38.ctx_ref, bf16[1024,768]{1,0:T(8,128)(2,1)} %bitcast.61, bf16[32,216,768]{2,1,0:T(8,128)(2,1)} %bitcast.55, bf16[768,768]{1,0:T(8,128)(2,1)} %fusion.4.order_ref, ...), custom_call_target="tpu_custom_call" | custom-call | flops 1207959552 | bytes 9437184 | tf_op jit(solution)/shard_map/first_norm/pallas_call | solution.py:211
  174.7 33.9 %ffn_forward.1 = (bf16[1024,3072]{1,0:T(8,128)(2,1)}, bf16[1024,3072]{1,0:T(8,128)(2,1)}, bf16[1024,768]{1,0:T(8,128)(2,1)}, f32[1024,768]{1,0:T(8,128)}, bf16[1024,768]{1,0:T(8,128)(2,1)}, /*index=5*/f32[8,768]{1,0:T(8,128)}) custom-call(bf16[1024,768]{1,0:T(8,128)(2,1)} %get-tuple-element.39.low_ref, f32[1024,768]{1,0:T(8,128)} %get-tuple-element.40.hat_ref, ...), custom_call_target="tpu_custom_call" | custom-call | flops 9663676416 | bytes 29884416 | tf_op jit(solution)/shard_map/ffn_forward/pallas_call | solution.py:309
  208.6 9.2 %grad_down.1 = bf16[32,96,768]{2,1,0:T(8,128)(2,1)} custom-call(bf16[1024,3072]{1,0:T(8,128)(2,1)} %get-tuple-element.59.act_ref, bf16[1024,768]{1,0:T(8,128)(2,1)} %get-tuple-element.42.gsec_ref), custom_call_target="tpu_custom_call" | custom-call | flops 4831838208 | bytes 12582912 | tf_op jit(solution)/shard_map/grad_down/pallas_call | solution.py:343
  217.9 22.3 %ffn_backward.1 = (bf16[32,96,768]{2,1,0:T(8,128)(2,1)}, f32[4,1,768]{2,1,0:T(1,128)}, f32[1024,768]{1,0:T(8,128)}) custom-call(bf16[1024,768]{1,0:T(8,128)(2,1)} %get-tuple-element.42.gsec_ref, bf16[1024,3072]{1,0:T(8,128)(2,1)} %get-tuple-element.43.slope_ref, bf16[1024,768]{1,0:T(8,128)(2,1)} %get-tuple-element.39.low_ref, ...), custom_call_target="tpu_custom_call" | custom-call | flops 14495514624 | bytes 26738688 | tf_op jit(solution)/shard_map/ffn_backward/pallas_call | solution.py:374
  240.2 15.0 %first_back.1 = (f32[1024,768]{1,0:T(8,128)}, bf16[1024,768]{1,0:T(8,128)(2,1)}, bf16[32,24,768]{2,1,0:T(8,128)(2,1)}, f32[16,1024]{1,0:T(8,128)}, f32[8,768]{1,0:T(8,128)}) custom-call(f32[1024,768]{1,0:T(8,128)} %get-tuple-element.44.acc_ref, f32[1024,768]{1,0:T(8,128)} %get-tuple-element.45.gtwo_ref, f32[1024,768]{1,0:T(8,128)} %get-tuple-element.40.hat_ref, ...), custom_call_target="tpu_custom_call" | custom-call | flops 2415919104 | bytes 19267584 | tf_op jit(solution)/shard_map/first_back/pallas_call | solution.py:443
  255.3 0.7 convert.35
  256.1 19.3 %attend_back.1.grads_ref.grad_ref = bf16[3,1024,768]{2,1,0:T(8,128)(2,1)} custom-call(bf16[1024,768]{1,0:T(8,128)(2,1)} %get-tuple-element.35.q_ref, bf16[1024,768]{1,0:T(8,128)(2,1)} %get-tuple-element.36.k_ref, bf16[1024,768]{1,0:T(8,128)(2,1)} %get-tuple-element.37.v_ref, bf16[2,12,512,512]{3,2,1,0:T(8,128)(2,1)} %get-tuple-element.49.p_ref, ...), custom_call_target="tpu_custom_call" | custom-call | flops 12884901888 | bytes 23592960 | tf_op jit(solution)/shard_map/attend_back/pallas_call | solution.py:169
  275.4 9.1 %grad_project.1 = (bf16[32,72,768]{2,1,0:T(8,128)(2,1)}, f32[3,8,768]{2,1,0:T(8,128)}) custom-call(bf16[1024,768]{1,0:T(8,128)(2,1)} %bitcast.62, bf16[1024,768]{1,0:T(8,128)(2,1)} %copy-done.2, bf16[3,1024,768]{2,1,0:T(8,128)(2,1)} %attend_back.1.grads_ref.grad_ref), custom_call_target="tpu_custom_call" | custom-call | flops 3623878656 | bytes 11403264 | tf_op jit(solution)/shard_map/grad_project/pallas_call | solution.py:491
  284.5 0.8 slice_bitcast_fusion.5
  285.3 1.2 fusion.12
  286.9 8.7 %fusion.1 = bf16[32,200,768]{2,1,0:T(8,128)(2,1)} fusion(bf16[32,1,768]{2,1,0:T(2,128)(2,1)S(1)} %copy.30, bf16[32,72,768]{2,1,0:T(8,128)(2,1)} %get-tuple-element.54, bf16[32,24,768]{2,1,0:T(8,128)(2,1)S(1)} %copy-done.3, bf16[32,96,768]{2,1,0:T(8,128)(2,1)} %get-tuple-element.52), kind=kLoop, calls=%fused_computation.2 | loop fusion | flops 49152000 | bytes 19316736 | tf_op jit(solution)/shard_map/concatenate | solution.py:642
  295.6 2.1 slice_bitcast_fusion.1
  298.4 3.2 collective-permute-done.1.back_ref
  301.5 1.1 copy-done.1
  302.6 9.6 %grad_input.1 = f32[1024,768]{1,0:T(8,128)} custom-call(f32[1024,768]{1,0:T(8,128)} %get-tuple-element.48.gres_ref, bf16[3,1024,768]{2,1,0:T(8,128)(2,1)} %attend_back.1.grads_ref.grad_ref, bf16[1024,768]{1,0:T(8,128)(2,1)} %copy-done.1, bf16[32,80,768]{2,1,0:T(8,128)(2,1)} %bitcast.52, bf16[32,80,768]{2,1,0:T(8,128)(2,1)} %bitcast.53, ...), custom_call_target="tpu_custom_call" | custom-call | flops 3623878656 | bytes 16121856 | tf_op jit(solution)/shard_map/grad_input/pallas_call | solution.py:516
  312.3 11.8 %reduce-scatter.5.cloned.1.call-done = bf16[1,96,768]{2,1,0:T(8,128)(2,1)} async-done(((bf16[32,96,768]{2,1,0:T(8,128)(2,1)}), bf16[1,96,768]{2,1,0:T(8,128)(2,1)}) %reduce-scatter.5.cloned.1.call-update) | async-done | bytes 147472 | tf_op jit(solution)/shard_map/reduce_scatter | solution.py:533
  324.1 1.8 reshape.199
  325.9 141.2 %reduce-scatter.3.cloned.1.call-done = bf16[1,200,768]{2,1,0:T(8,128)(2,1)} async-done(((bf16[32,200,768]{2,1,0:T(8,128)(2,1)}), bf16[1,200,768]{2,1,0:T(8,128)(2,1)}) %reduce-scatter.3.cloned.1.call-update) | async-done | bytes 307216 | tf_op jit(solution)/shard_map/reduce_scatter | solution.py:533
  467.1 1.0 convert_bitcast_fusion
  469.3 0.9 slice.146
  470.3 0.8 reshape.194
  471.2 1.5 fusion.2
  472.7 0.6 squeeze.24
  473.4 0.6 squeeze.25
  474.0 0.6 squeeze.26
  474.7 0.8 slice.145
  475.4 0.6 reshape.192
  (56 shorter events, 5.8 us)
Async XLA Ops:
  7.2 10.3 %copy-start = (bf16[2,1,512,768]{3,2,1,0:T(8,128)(2,1)S(1)}, bf16[2,1,512,768]{3,2,1,0:T(8,128)(2,1)}, u32[]{:S(2)}) copy-start(bf16[2,1,512,768]{3,2,1,0:T(8,128)(2,1)} %param.12) | copy-start | bytes 4718596
  7.2 10.9 %copy-start.6 = (s32[2,2]{1,0:T(2,128)S(1)}, s32[2,2]{1,0:T(2,128)}, u32[]{:S(2)}) copy-start(s32[2,2]{1,0:T(2,128)} %param.14) | copy-start | bytes 52
  7.2 70.4 %all-gather.5.cloned.1.call-start = ((), (), s32[]{:S(2)}) async-start(), calls=%async_computation.4 | async-start | bytes 4055040 | tf_op jit(solution)/shard_map/all_gather | solution.py:529
  13.7 153.1 %all-gather.7.cloned.1.call-start = ((), (), s32[]{:S(2)}) async-start(), calls=%async_computation.5 | async-start | bytes 10948608 | tf_op jit(solution)/shard_map/all_gather | solution.py:529
  17.5 306.7 %reduce-scatter.5.cloned.1.call-start = ((), (), s32[]{:S(2)}) async-start(), calls=%async_computation.3 | async-start | bytes 4866048 | tf_op jit(solution)/shard_map/reduce_scatter | solution.py:533
  17.5 63.9 %collective-permute-start = (bf16[1024,768]{1,0:T(8,128)(2,1)S(1)}, bf16[1024,768]{1,0:T(8,128)(2,1)S(1)}, u32[]{:S(2)}, u32[]{:S(2)}) collective-permute-start(bf16[1024,768]{1,0:T(8,128)(2,1)S(1)} %bitcast.63), channel_id=1, source_target_pairs={{0,8},{8,0},{16,24},{24,16},{1,9},{9,1},{17,25},{25,17},{2,10},{10... | collective-permute-start | bytes 4718600 | tf_op jit(solution)/shard_map/ppermute | solution.py:35
  81.4 1.2 copy-start.2
  217.8 249.3 %reduce-scatter.3.cloned.1.call-start = ((), (), s32[]{:S(2)}) async-start(), calls=%async_computation.2 | async-start | bytes 10137600 | tf_op jit(solution)/shard_map/reduce_scatter | solution.py:533
  240.2 15.8 %copy-start.4 = (f32[8,768]{1,0:T(8,128)S(1)}, f32[8,768]{1,0:T(8,128)}, u32[]{:S(2)}) copy-start(f32[8,768]{1,0:T(8,128)} %get-tuple-element.57) | copy-start | bytes 73732
  275.4 11.2 %copy-start.5 = (f32[4,1,768]{2,1,0:T(1,128)S(1)}, f32[4,1,768]{2,1,0:T(1,128)}, u32[]{:S(2)}) copy-start(f32[4,1,768]{2,1,0:T(1,128)} %get-tuple-element.58) | copy-start | bytes 36868
  275.4 11.5 %copy-start.3 = (bf16[32,24,768]{2,1,0:T(8,128)(2,1)S(1)}, bf16[32,24,768]{2,1,0:T(8,128)(2,1)}, u32[]{:S(2)}) copy-start(bf16[32,24,768]{2,1,0:T(8,128)(2,1)} %get-tuple-element.53) | copy-start | bytes 3538948
  298.0 3.5 collective-permute-start.1
  301.5 1.1 copy-start.1
Sparse Core Ops, SparseCore 0:
  13.9 63.6 all-gather.4
  81.1 85.6 all-gather.6
  218.0 106.1 reduce-scatter.4
  329.9 137.1 reduce-scatter.2

commit v2 on v1

--- a/solution.py
+++ b/solution.py
@@ -29,10 +29,8 @@
 BOTH = ("blk", "dp")
 
 
-def partner(value, axis, distance):
-    mask = 2**distance
-    pairs = [(source, source ^ mask) for source in range(lax.axis_size(axis))]
-    return lax.ppermute(value, axis, pairs)
+def swap(value, axis, mask):
+    return lax.ppermute(value, axis, [(source, source ^ mask) for source in range(lax.axis_size(axis))])
 
 
 def dot_nn(a, b):
@@ -76,31 +74,50 @@
     return ref[...].reshape(D, D)
 
 
-def project_body(x_ref, xp_ref, wq_ref, wk_ref, wv_ref, bias_ref, q_ref, k_ref, v_ref):
+PIECES = [(core, y, x) for core in range(2) for y in range(2) for x in range(2)]
+
+
+def project_body(me_ref, x_ref, xp_ref, *refs):
+    pieces, (q_ref, k_ref, v_ref, w_ref, vec_ref, scr) = refs[: len(PIECES)], refs[len(PIECES) :]
+
+    @pl.when(pl.program_id(0) == 0)
+    def _():
+        me = me_ref[0]
+        total = jnp.zeros((8, D), f32)
+        for (core, y, x), piece in zip(PIECES, pieces):
+            for z in range(piece.shape[0]):
+                group = (16 * y + 8 * core + 2 * z + x) ^ me
+                for part in range(3):
+                    scr[part, group] = piece[z, part * ROWS : (part + 1) * ROWS, :]
+                total = total + piece[z, 3 * ROWS : 3 * ROWS + 8, :].astype(f32)
+        vec_ref[...] = total
+        for part in range(3):
+            w_ref[part] = scr[part].reshape(D, D)
+
     own, other = x_ref[...], xp_ref[...]
-    q_ref[...] = (dot_nn(own, square(wq_ref)) + bias_ref[0:1, :]).astype(bf16)
-    wk, wv = square(wk_ref), square(wv_ref)
-    k_ref[:, :HALF] = dot_nn(other, wk[:, :HALF]).astype(bf16)
-    k_ref[:, HALF:] = dot_nn(own, wk[:, HALF:]).astype(bf16)
-    v_ref[:, :HALF] = (dot_nn(other, wv[:, :HALF]) + bias_ref[1:2, :HALF]).astype(bf16)
-    v_ref[:, HALF:] = (dot_nn(own, wv[:, HALF:]) + bias_ref[1:2, HALF:]).astype(bf16)
-
-
-def project(x, xp, pack, bias):
+    q_ref[...] = (dot_nn(own, w_ref[0]) + vec_ref[0:1, :]).astype(bf16)
+    k_ref[:, :HALF] = dot_nn(other, w_ref[1, :, :HALF]).astype(bf16)
+    k_ref[:, HALF:] = dot_nn(own, w_ref[1, :, HALF:]).astype(bf16)
+    v_ref[:, :HALF] = (dot_nn(other, w_ref[2, :, :HALF]) + vec_ref[1:2, :HALF]).astype(bf16)
+    v_ref[:, HALF:] = (dot_nn(own, w_ref[2, :, HALF:]) + vec_ref[1:2, HALF:]).astype(bf16)
+
+
+def project(me, x, xp, pieces):
     rows = x.shape[0]
     step = BLOCK
-    row_spec = pl.BlockSpec((step, D), lambda i: (i, 0))
-    weight = [pl.BlockSpec((GROUPS_W, ROWS, D), lambda i, s=s: (0, s, 0)) for s in range(3)]
+    row_spec = pl.BlockSpec((step, D), lambda i, *_: (i, 0))
     return call(
         project_body,
         (rows // step,),
-        [row_spec, row_spec, *weight, whole((8, D))],
-        [row_spec] * 3,
-        [sds((rows, D), bf16)] * 3,
+        [row_spec, row_spec] + [whole(pieces[0].shape)] * len(PIECES),
+        [row_spec] * 3 + [whole((3, D, D)), whole((8, D))],
+        [sds((rows, D), bf16)] * 3 + [sds((3, D, D), bf16), sds((8, D), f32)],
+        scratch=[pltpu.VMEM((3, GROUPS_W, ROWS, D), bf16)],
+        prefetch=1,
         flops=6 * rows * D * D,
-        moved=16 * rows * D,
+        moved=10 * rows * D + 12 * D * D,
         name="project",
-    )(x, xp, pack, pack, pack, bias)
+    )(me, x, xp, *pieces)
 
 
 def attend_body(valid_ref, q_ref, k_ref, v_ref, ctx_ref, p_ref):
@@ -141,7 +158,7 @@
     )(valid, q, k, v)
 
 
-def attend_back_body(q_ref, k_ref, v_ref, p_ref, gctx_ref, delta_ref, out_ref):
+def attend_back_body(q_ref, k_ref, v_ref, p_ref, gctx_ref, delta_ref, out_ref, give_ref):
     pair = pl.program_id(1)
     queries, keys, values, grad_ctx = q_ref[...], k_ref[...], v_ref[...], gctx_ref[...]
     lane = lax.broadcasted_iota(jnp.int32, (BLOCK, PAIR), 1)
@@ -158,8 +175,15 @@
         gq.append(dot_tn(grad_scores, keys))
     first = lane < HD
     out_ref[0] = (jnp.where(first, gq[0], gq[1]) * scale).astype(bf16)
-    out_ref[1] = (jnp.where(first, gk[0], gk[1]) * scale).astype(bf16)
-    out_ref[2] = jnp.where(first, gv[0], gv[1]).astype(bf16)
+    grad_keys = (jnp.where(first, gk[0], gk[1]) * scale).astype(bf16)
+    grad_values = jnp.where(first, gv[0], gv[1]).astype(bf16)
+    out_ref[1] = grad_keys
+    out_ref[2] = grad_values
+
+    @pl.when(pair < H // 4)
+    def _():
+        give_ref[0] = grad_keys
+        give_ref[1] = grad_values
 
 
 def attend_back(q, k, v, probs, grad_ctx, delta):
@@ -175,8 +199,11 @@
             spec,
             pl.BlockSpec((16, BLOCK), lambda s, j: (0, s)),
         ],
-        pl.BlockSpec((3, BLOCK, PAIR), lambda s, j: (0, s, j)),
-        sds((3, rows, D), bf16),
+        [
+            pl.BlockSpec((3, BLOCK, PAIR), lambda s, j: (0, s, j)),
+            pl.BlockSpec((2, BLOCK, PAIR), lambda s, j: (0, s, jnp.minimum(j, H // 4 - 1))),
+        ],
+        [sds((3, rows, D), bf16), sds((2, rows, HALF), bf16)],
         flops=32 * rows * BLOCK * D,
         moved=14 * rows * D + 2 * rows * H * BLOCK,
         name="attend_back",
@@ -187,9 +214,15 @@
     return jnp.sum(value, axis=-1, keepdims=True) * (1.0 / D)
 
 
-def first_norm_body(ctx_ref, x_ref, wo_ref, order_ref, vec_ref, hat_ref, inv_ref, low_ref, wop_ref, wo_scr):
+def first_norm_body(
+    ctx_ref, x_ref, wo_ref, bias_ref, order_ref, vec_ref, hat_ref, inv_ref, low_ref, wop_ref, upb_ref, wo_scr
+):
     @pl.when(pl.program_id(0) == 0)
     def _():
+        total = jnp.zeros((8, D), f32)
+        for group in range(GROUPS_W):
+            total = total + bias_ref[group].astype(f32)
+        upb_ref[...] = total
         permuted = dot_tn(order_ref[...], square(wo_ref)).astype(bf16)
         wo_scr[...] = permuted
         wop_ref[...] = permuted
@@ -215,16 +248,23 @@
             row_spec,
             row_spec,
             pl.BlockSpec((GROUPS_W, ROWS, D), lambda i: (0, 8, 0)),
+            pl.BlockSpec((GROUPS_W, 8, D), lambda i: (0, 27, 0)),
             whole((D, D)),
             whole((8, D)),
         ],
-        [row_spec, pl.BlockSpec((step, LANES), lambda i: (i, 0)), row_spec, whole((D, D))],
-        [sds((rows, D), f32), sds((rows, LANES), f32), sds((rows, D), bf16), sds((D, D), bf16)],
+        [row_spec, pl.BlockSpec((step, LANES), lambda i: (i, 0)), row_spec, whole((D, D)), whole((8, D))],
+        [
+            sds((rows, D), f32),
+            sds((rows, LANES), f32),
+            sds((rows, D), bf16),
+            sds((D, D), bf16),
+            sds((8, D), f32),
+        ],
         scratch=[pltpu.VMEM((D, D), bf16)],
         flops=2 * rows * D * D,
         moved=12 * rows * D,
         name="first_norm",
-    )(ctx, x, pack, order, vecs)
+    )(ctx, x, pack, pack, order, vecs)
 
 
 def gelu_and_slope(value):
@@ -256,7 +296,7 @@
 
     for start in range(0, rows, step):
         part = pl.ds(start, step)
-        hidden = dot_nn(low_ref[part, :], w_up) + bias_ref[0]
+        hidden = dot_nn(low_ref[part, :], w_up) + bias_ref[pl.ds(chunk, 1), :]
         activated, slope = gelu_and_slope(hidden)
         activated = activated.astype(bf16)
         act_ref[part, :] = activated
@@ -315,7 +355,7 @@
             row_spec,
             pl.BlockSpec((GROUPS_W, ROWS, D), lambda r, c: (0, 4 + c, 0)),
             pl.BlockSpec((GROUPS_W // 4, 4 * ROWS, D), lambda r, c: (c, 0, 0)),
-            pl.BlockSpec((1, 1, D), lambda r, c: (c, 0, 0)),
+            whole((8, D)),
             whole((8, D)),
         ],
         [wide, wide, row_spec, row_spec, row_spec, whole((8, D))],
@@ -352,12 +392,32 @@
     )(act, gsec)
 
 
-def ffn_backward_body(gsec_ref, slope_ref, low_ref, up_ref, down_ref, gup_ref, gbias_ref, acc_ref):
+def apart(scr, me, keep, send):
+    def one(index, carry):
+        group = (2 * index - jnp.bitwise_and(index, 7)) ^ me
+        keep(index, scr[group])
+        send(index, scr[group ^ 8])
+        return carry
+
+    lax.fori_loop(0, GROUPS_W // 2, one, 0)
+
+
+def ffn_backward_body(
+    me_ref, gsec_ref, slope_ref, low_ref, up_ref, down_ref, keep_ref, send_ref, gbias_ref, acc_ref, scr
+):
     chunk = pl.program_id(0)
     grad_act = dot_nt(gsec_ref[...], square(down_ref))
     grad_hidden = (grad_act * slope_ref[...].astype(f32)).astype(bf16)
     gbias_ref[0] = jnp.sum(grad_hidden.astype(f32), axis=0, keepdims=True)
-    gup_ref[...] = dot_tn(low_ref[...], grad_hidden).astype(bf16).reshape(gup_ref.shape)
+    scr[...] = dot_tn(low_ref[...], grad_hidden).astype(bf16).reshape(scr.shape)
+
+    def keep(index, value):
+        keep_ref[index] = value
+
+    def send(index, value):
+        send_ref[index] = value
+
+    apart(scr, me_ref[0], keep, send)
     back = dot_nt(grad_hidden, square(up_ref))
 
     @pl.when(chunk == 0)
@@ -369,28 +429,27 @@
         acc_ref[...] += back
 
 
-def ffn_backward(gsec, slope, low, pack):
+def ffn_backward(me, gsec, slope, low, pack):
     rows = gsec.shape[0]
+    half = pl.BlockSpec((GROUPS_W // 2, ROWS, D), lambda c, *_: (0, c, 0))
     return call(
         ffn_backward_body,
         (FF // D,),
         [
             whole((rows, D)),
-            pl.BlockSpec((rows, D), lambda c: (0, c)),
+            pl.BlockSpec((rows, D), lambda c, *_: (0, c)),
             whole((rows, D)),
-            pl.BlockSpec((GROUPS_W, ROWS, D), lambda c: (0, 4 + c, 0)),
-            pl.BlockSpec((GROUPS_W // 4, 4 * ROWS, D), lambda c: (c, 0, 0)),
-        ],
-        [
-            pl.BlockSpec((GROUPS_W, ROWS, D), lambda c: (0, c, 0)),
-            pl.BlockSpec((1, 1, D), lambda c: (c, 0, 0)),
-            whole((rows, D)),
-        ],
-        [sds((GROUPS_W, 4 * ROWS, D), bf16), sds((FF // D, 1, D), f32), sds((rows, D), f32)],
+            pl.BlockSpec((GROUPS_W, ROWS, D), lambda c, *_: (0, 4 + c, 0)),
+            pl.BlockSpec((GROUPS_W // 4, 4 * ROWS, D), lambda c, *_: (c, 0, 0)),
+        ],
+        [half, half, pl.BlockSpec((1, 1, D), lambda c, *_: (c, 0, 0)), whole((rows, D))],
+        [sds((GROUPS_W // 2, 4 * ROWS, D), bf16)] * 2 + [sds((FF // D, 1, D), f32), sds((rows, D), f32)],
+        scratch=[pltpu.VMEM((GROUPS_W, ROWS, D), bf16)],
+        prefetch=1,
         flops=6 * rows * D * FF,
         moved=16 * rows * D + 6 * D * FF,
         name="ffn_backward",
-    )(gsec, slope, low, pack, pack)
+    )(me, gsec, slope, low, pack, pack)
 
 
 def first_back_body(
@@ -474,55 +533,123 @@
     )(acc, gtwo, hat, inv, ctx, wop, order, vecs)
 
 
-def grad_project_body(x_ref, xp_ref, grad_ref, out_ref, sums_ref):
+LAST_ROWS = 4 * ROWS + 8
+N_VEC = 8 * D // GROUPS_W
+N_BIAS = FF // GROUPS_W
+
+
+def grad_project_body(
+    me_ref, x_ref, xp_ref, grad_ref, gout_ref, one_ref, two_ref, upb_ref, order_ref, keep_ref, send_ref, scr, sums, small
+):
     part = pl.program_id(0)
+    me = me_ref[0]
     own = x_ref[...]
     other = jnp.where(part == 0, own, xp_ref[...])
     grad = grad_ref[0]
     left = dot_tn(other, grad[:, :HALF]).astype(bf16)
     right = dot_tn(own, grad[:, HALF:]).astype(bf16)
-    out_ref[:, :, :HALF] = left.reshape(GROUPS_W, ROWS, HALF)
-    out_ref[:, :, HALF:] = right.reshape(GROUPS_W, ROWS, HALF)
-    sums_ref[0] = jnp.broadcast_to(jnp.sum(grad.astype(f32), axis=0, keepdims=True), (8, D))
-
-
-def grad_project(x, xp, grads):
+    scr[:, :, :HALF] = left.reshape(GROUPS_W, ROWS, HALF)
+    scr[:, :, HALF:] = right.reshape(GROUPS_W, ROWS, HALF)
+    sums[pl.ds(part, 1), :] = jnp.sum(grad.astype(f32), axis=0, keepdims=True)
+
+    def place(source, start, size):
+        def keep(index, value):
+            keep_ref[index, start : start + size, :] = value.astype(bf16)
+
+        def send(index, value):
+            send_ref[index, start : start + size, :] = value.astype(bf16)
+
+        apart(source, me, keep, send)
+
+    for index in range(3):
+
+        @pl.when(part == index)
+        def _():
+            place(scr, (index + 1) * ROWS, ROWS)
+
+    @pl.when(part == 0)
+    def _():
+        place(gout_ref, 0, ROWS)
+
+    @pl.when(part == 2)
+    def _():
+        bias = lax.dot_general(
+            sums[...],
+            order_ref[...].astype(f32),
+            (((1,), (1,)), ((), ())),
+            precision=lax.Precision.HIGHEST,
+            preferred_element_type=f32,
+        )
+        rows = (
+            bias[0:1], bias[2:3], one_ref[2:3, :], one_ref[0:1, :],
+            one_ref[1:2, :], two_ref[2:3, :], two_ref[0:1, :], two_ref[1:2, :],
+        )
+        small[...] = jnp.zeros_like(small)
+        for group in range(GROUPS_W):
+            row, column = divmod(group, GROUPS_W // 8)
+            small[group, 0:1, :N_VEC] = rows[row][:, column * N_VEC : (column + 1) * N_VEC]
+            row, column = divmod(group, GROUPS_W // 4)
+            small[group, 0:1, N_VEC : N_VEC + N_BIAS] = upb_ref[row, :, column * N_BIAS : (column + 1) * N_BIAS]
+        place(small, 4 * ROWS, 8)
+
+
+def grad_project(me, x, xp, grads, grad_out, sums_one, sums_two, up_bias, order):
     rows = x.shape[0]
+    half = (GROUPS_W // 2, LAST_ROWS, D)
     return call(
         grad_project_body,
         (3,),
-        [whole((rows, D)), whole((rows, D)), pl.BlockSpec((1, rows, D), lambda s: (s, 0, 0))],
-        [pl.BlockSpec((GROUPS_W, ROWS, D), lambda s: (0, s, 0)), pl.BlockSpec((1, 8, D), lambda s: (s, 0, 0))],
-        [sds((GROUPS_W, 3 * ROWS, D), bf16), sds((3, 8, D), f32)],
+        [
+            whole((rows, D)),
+            whole((rows, D)),
+            pl.BlockSpec((1, rows, D), lambda s, *_: (s, 0, 0)),
+            whole((GROUPS_W, ROWS, D)),
+            whole((8, D)),
+            whole((8, D)),
+            whole((FF // D, 1, D)),
+            whole((D, D)),
+        ],
+        [whole(half)] * 2,
+        [sds(half, bf16)] * 2,
+        scratch=[
+            pltpu.VMEM((GROUPS_W, ROWS, D), bf16),
+            pltpu.VMEM((8, D), f32),
+            pltpu.VMEM((GROUPS_W, 8, D), f32),
+        ],
+        prefetch=1,
         flops=6 * rows * D * D,
-        moved=10 * rows * D + 6 * D * D,
+        moved=10 * rows * D + 12 * D * D,
         name="grad_project",
-    )(x, xp, grads)
-
-
-def grad_input_body(gres_ref, grads_ref, back_ref, wq_ref, wk_ref, wv_ref, out_ref):
-    wk, wv = square(wk_ref), square(wv_ref)
-    total = gres_ref[...] + dot_nt(grads_ref[0], square(wq_ref))
-    total = total + dot_nt(back_ref[:, :HALF], wk[:, :HALF]) + dot_nt(grads_ref[1][:, HALF:], wk[:, HALF:])
-    total = total + dot_nt(back_ref[:, HALF:], wv[:, :HALF]) + dot_nt(grads_ref[2][:, HALF:], wv[:, HALF:])
+    )(me, x, xp, grads, grad_out, sums_one, sums_two, up_bias, order)
+
+
+def grad_input_body(gres_ref, grads_ref, back_ref, w_ref, out_ref):
+    total = gres_ref[...] + dot_nt(grads_ref[0], w_ref[0])
+    for part in (1, 2):
+        total = total + dot_nt(back_ref[part - 1], w_ref[part, :, :HALF])
+        total = total + dot_nt(grads_ref[part, :, HALF:], w_ref[part, :, HALF:])
     out_ref[...] = total
 
 
-def grad_input_of(gres, grads, back, pack):
+def grad_input_of(gres, grads, back, weights):
     rows = gres.shape[0]
     step = 256
     row_spec = pl.BlockSpec((step, D), lambda i: (i, 0))
-    weight = [pl.BlockSpec((GROUPS_W, ROWS, D), lambda i, s=s: (0, s, 0)) for s in range(3)]
     return call(
         grad_input_body,
         (rows // step,),
-        [row_spec, pl.BlockSpec((3, step, D), lambda i: (0, i, 0)), row_spec, *weight],
+        [
+            row_spec,
+            pl.BlockSpec((3, step, D), lambda i: (0, i, 0)),
+            pl.BlockSpec((2, step, HALF), lambda i: (0, i, 0)),
+            whole((3, D, D)),
+        ],
         row_spec,
         sds((rows, D), f32),
         flops=6 * rows * D * D,
         moved=16 * rows * D + 6 * D * D,
         name="grad_input",
-    )(gres, grads, back, pack, pack, pack)
+    )(gres, grads, back, weights)
 
 
 def gather(value):
@@ -547,12 +674,64 @@
     return grouped.reshape(count, columns * rows, D)
 
 
+def gather_near(shard):
+    rows = shard.shape[0]
+    half = rows // 16 * 8
+    column = jnp.stack([shard] + [swap(shard, "dp", 2 * step) for step in range(1, 4)])
+    over_x = swap(column, "dp", 1)
+    over_y = swap(column, "blk", 2)
+    over_both = jnp.concatenate((swap(over_y[:, :half], "dp", 1), swap(over_x[:, half:], "blk", 2)), axis=1)
+    near = {(0, 0): column, (0, 1): over_x, (1, 0): over_y, (1, 1): over_both}
+    pieces = {(0, y, x): value for (y, x), value in near.items()}
+    pieces.update({(1, y, x): swap(value, "blk", 1) for (y, x), value in near.items()})
+    return [pieces[key] for key in PIECES]
+
+
+def over_cores(keep, send):
+    rows = keep.shape[1]
+    return (keep + swap(send, "blk", 1)).reshape(2, 4, 2, rows, D)
+
+
+def over_first(total):
+    rows = total.shape[3]
+    half = (rows + 8) // 16 * 8
+    one, two = total[:, :, :, :half], total[:, :, :, half:]
+    return one[:, :, 0] + swap(one[:, :, 1], "dp", 1), two[0] + swap(two[1], "blk", 2)
+
+
+def over_second(pair):
+    one, two = pair
+    one = one[0] + swap(one[1], "blk", 2)
+    two = two[:, 0] + swap(two[:, 1], "dp", 1)
+    return jnp.concatenate((one, two), axis=1)
+
+
+def over_z(column):
+    result = column[0].astype(f32)
+    for step in range(1, 4):
+        result = result + swap(column[step], "dp", 2 * step).astype(f32)
+    return result
+
+
+def together(*values):
+    return lax.optimization_barrier(values)
+
+
+def every_group(keep, send):
+    rows = keep.shape[1]
+    return jnp.stack((keep.reshape(2, 8, rows, D), send.reshape(2, 8, rows, D)), axis=1).reshape(GROUPS_W, rows, D)
+
+
 def body(tokens, cotangent, lengths, head_mode, w_query, w_key, w_value, w_out, w_up, w_down, b_up, vectors):
     seq_count = tokens.shape[0]
     row_count = seq_count * BLOCK
     devices = lax.axis_size("blk") * lax.axis_size("dp")
+    near = devices == GROUPS_W
     own_rows = D // devices
+    n_vec, n_bias = vectors.shape[0], b_up.shape[0]
     blk_index = lax.axis_index("blk")
+    device = blk_index * lax.axis_size("dp") + lax.axis_index("dp")
+    me = (device if near else device * 0).reshape(1).astype(jnp.int32)
     block_side = blk_index % 2
     member = blk_index // 2
     seq_lengths = jnp.where(member == 0, lengths[:, 0], lengths[:, 1])
@@ -569,106 +748,101 @@
     order = (target[:, None] == jnp.arange(D)[None, :]).astype(bf16)
 
     inputs = tokens.reshape(row_count, D)
-    other_inputs = partner(inputs, "blk", 0)
-
-    small = jnp.concatenate((vectors, b_up))
-    small = jnp.pad(small, (0, D - small.shape[0])).reshape(1, D)
-    small = jnp.pad(small, ((0, 7), (0, 0)))
-    stacked = jnp.concatenate([w.reshape(own_rows, D) for w in (w_query, w_key, w_value)])
-    stacked = dot_nn(stacked, order).astype(bf16)
-    attn_all = gather(jnp.concatenate((stacked, small)))
-    ffn_all = gather(
-        jnp.concatenate(
-            (
-                w_down.reshape(4 * own_rows, D),
-                w_up.reshape(own_rows, 4, D).transpose(1, 0, 2).reshape(4 * own_rows, D),
-                w_out.reshape(own_rows, D),
-            )
+    other_inputs = swap(inputs, "blk", 1)
+
+    up_bias = lax.dynamic_update_slice(jnp.zeros((FF,), bf16), b_up, (device * n_bias,)).reshape(FF // D, D)
+    ffn_shard = jnp.concatenate(
+        (
+            w_down.reshape(4 * own_rows, D),
+            w_up.reshape(own_rows, 4, D).transpose(1, 0, 2).reshape(4 * own_rows, D),
+            w_out.reshape(own_rows, D),
+            jnp.pad(up_bias, ((0, 8 - FF // D), (0, 0))),
         )
     )
-    n_vec, n_bias = vectors.shape[0], b_up.shape[0]
-    small_all = attn_all[:, 3 * own_rows, :]
-    vec_low = small_all[:, :n_vec].reshape(8, D)
-    vecs = vec_low.astype(f32)
-    bias_qv = jnp.pad(dot_nn(vec_low[0:2], order), ((0, 6), (0, 0)))
-    up_bias = small_all[:, n_vec : n_vec + n_bias].reshape(FF // D, 1, D).astype(f32)
-    if devices == GROUPS_W:
-        attn_pack, ffn_pack = attn_all, ffn_all
+    ffn_pack = gather(ffn_shard)
+    small = lax.dynamic_update_slice(jnp.zeros((8 * D,), bf16), vectors, (device * n_vec,)).reshape(8, D)
+    stacked = jnp.concatenate([w.reshape(own_rows, D) for w in (w_query, w_key, w_value)] + [small[0:2]])
+    stacked = dot_nn(stacked, order).astype(bf16)
+    attn_shard = jnp.concatenate((stacked, small[2:]))
+    if near:
+        pieces = gather_near(attn_shard)
     else:
-        attn_pack = jnp.concatenate([joined(attn_all, s * own_rows, own_rows) for s in range(3)], axis=1)
+        attn_all = gather(attn_shard)
+        attn_pack = jnp.concatenate(
+            [joined(attn_all, s * own_rows, own_rows) for s in range(3)]
+            + [jnp.sum(attn_all[:, 3 * own_rows :].reshape(GROUPS_W, -1, 8, D), axis=1)],
+            axis=1,
+        ).reshape(2, 2, 4, 2, 3 * ROWS + 8, D)
+        pieces = [attn_pack[y, core, :, x] for core, y, x in PIECES]
         ffn_pack = jnp.concatenate(
             (
-                joined(ffn_all, 0, 4 * own_rows),
-                joined(ffn_all, 4 * own_rows, own_rows, 4),
-                joined(ffn_all, 8 * own_rows, own_rows),
+                joined(ffn_pack, 0, 4 * own_rows),
+                joined(ffn_pack, 4 * own_rows, own_rows, 4),
+                joined(ffn_pack, 8 * own_rows, own_rows),
+                jnp.sum(ffn_pack[:, 9 * own_rows :].reshape(GROUPS_W, -1, 8, D), axis=1),
             ),
             axis=1,
         )
 
-    q, k, v = project(inputs, other_inputs, attn_pack, bias_qv)
+    q, k, v, attn_weights, vecs = project(me, inputs, other_inputs, pieces)
     ctx, probs = attend(valid, q, k, v)
-    hat, inv, low, out_weight = first_norm(ctx, inputs, ffn_pack, order, vecs)
+    hat, inv, low, out_weight, up_biases = first_norm(ctx, inputs, ffn_pack, order, vecs)
     act, slope, output, gtwo, gsec, sums_two = ffn_forward(
-        low, hat, cotangent.reshape(row_count, D), ffn_pack, up_bias, vecs
+        low, hat, cotangent.reshape(row_count, D), ffn_pack, up_biases, vecs
     )
-    grad_down = grad_down_of(act, gsec)
-    grad_up, grad_up_bias, acc = ffn_backward(gsec, slope, low, ffn_pack)
+    grad_down, gsec = together(grad_down_of(act, gsec), gsec)
+    down_sum = scatter(parted(grad_down, devices, 4 * own_rows)).astype(f32)
+    up_keep, up_send, grad_up_bias, acc = ffn_backward(me, gsec, slope, low, ffn_pack)
     gres, grad_ctx, grad_out, delta, sums_one = first_back(acc, gtwo, hat, inv, ctx, out_weight, order, vecs)
-    grads = attend_back(q, k, v, probs, grad_ctx, delta)
-    back = partner(jnp.concatenate((grads[1][:, :HALF], grads[2][:, :HALF]), axis=1), "blk", 0)
-    grad_qkv, sums_qkv = grad_project(inputs, other_inputs, grads)
-    grad_inputs = grad_input_of(gres, grads, back, attn_pack)
-
-    bias_grads = lax.dot_general(
-        jnp.stack((sums_qkv[0, 0], sums_qkv[2, 0])),
-        order.astype(f32),
-        (((1,), (1,)), ((), ())),
-        precision=lax.Precision.HIGHEST,
+    if near:
+        up_total, grad_ctx = together(over_cores(up_keep, up_send), grad_ctx)
+    grads, give = attend_back(q, k, v, probs, grad_ctx, delta)
+    if near:
+        up_pair, grads = together(over_first(up_total), grads)
+    back = swap(give, "blk", 1)
+    last_keep, last_send = grad_project(
+        me, inputs, other_inputs, grads, grad_out, sums_one, sums_two, grad_up_bias, order
     )
-    grad_vectors = jnp.concatenate(
-        (
-            bias_grads,
-            sums_one[2:3],
-            sums_one[0:2],
-            sums_two[2:3],
-            sums_two[0:2],
-        )
-    ).reshape(devices, n_vec)
-    small_grads = jnp.concatenate((grad_vectors, grad_up_bias.reshape(devices, n_bias)), axis=1)
-    small_grads = jnp.pad(small_grads, ((0, 0), (0, D - n_vec - n_bias))).astype(bf16)
-    small_grads = jnp.pad(small_grads[:, None, :], ((0, 0), (0, 7), (0, 0)))
-    down_sum = scatter(parted(grad_down, devices, 4 * own_rows))
-    rest_sum = scatter(
-        jnp.concatenate(
+    if near:
+        up_column = over_second(up_pair)
+        last_total, up_column, gres = together(over_cores(last_keep, last_send), up_column, gres)
+    grad_inputs = grad_input_of(gres, grads, back, attn_weights)
+
+    if near:
+        up_sum = over_z(up_column)
+        last_sum = over_z(over_second(over_first(last_total)))
+    else:
+        up_sum = scatter(parted(every_group(up_keep, up_send), devices, own_rows, 4)).astype(f32)
+        last = every_group(last_keep, last_send)
+        tail = jnp.concatenate(
             (
-                parted(grad_up, devices, own_rows, 4),
-                parted(grad_out, devices, own_rows),
-                jnp.concatenate(
-                    [parted(grad_qkv[:, s * ROWS : (s + 1) * ROWS], devices, own_rows) for s in range(3)], axis=1
-                ),
-                small_grads,
+                last[:, 4 * ROWS, :N_VEC].reshape(devices, n_vec),
+                last[:, 4 * ROWS, N_VEC : N_VEC + N_BIAS].reshape(devices, n_bias),
             ),
             axis=1,
         )
-    ).astype(f32)
-    up_sum = rest_sum[: 4 * own_rows].reshape(4, own_rows, D).transpose(1, 0, 2)
-    out_sum = rest_sum[4 * own_rows : 5 * own_rows]
+        tail = jnp.pad(tail, ((0, 0), (0, D - n_vec - n_bias)))[:, None, :]
+        last_sum = scatter(
+            jnp.concatenate(
+                [parted(last[:, s * ROWS : (s + 1) * ROWS], devices, own_rows) for s in range(4)] + [tail], axis=1
+            )
+        ).astype(f32)
     qkv_sum = lax.dot_general(
-        rest_sum[5 * own_rows : 8 * own_rows],
+        last_sum[own_rows : 4 * own_rows],
         order.astype(f32),
         (((1,), (1,)), ((), ())),
         precision=lax.Precision.HIGHEST,
     ).reshape(3, own_rows * D)
-    small_sum = rest_sum[8 * own_rows]
+    small_sum = last_sum[4 * own_rows]
     return (
         output.reshape(tokens.shape),
         grad_inputs.reshape(tokens.shape),
         qkv_sum[0],
         qkv_sum[1],
         qkv_sum[2],
-        out_sum.reshape(-1),
-        up_sum.reshape(-1),
-        down_sum.astype(f32).reshape(-1),
+        last_sum[:own_rows].reshape(-1),
+        up_sum.reshape(4, own_rows, D).transpose(1, 0, 2).reshape(-1),
+        down_sum.reshape(-1),
         small_sum[n_vec : n_vec + n_bias],
         small_sum[:n_vec],
     )

time: 484 us -> 328 us (0.68)
  waiting for transfers between devices: 271 us -> 89.1 us
  starting transfers between devices: 1.05 us -> 29.1 us
  Pallas kernels: 153 us -> 164 us
  other arithmetic: 16.8 us -> 9.48 us
    reduce_scatter x2 -> x1, waiting for transfers between devices: 153 us -> 11.7 us  [scatter(): return lax.psum_scatter(value, BOTH, scatter_dimension=0)]
    all_gather x2 -> x1, waiting for transfers between devices: 115 us -> 24.4 us  [gather(): return lax.all_gather(value, BOTH, axis=0)]
    ppermute x2 -> x29, waiting for transfers between devices: 3.15 us -> 52.9 us  [swap(): lax.ppermute(value, axis, [(source, source ^ mask) for source in range(la...]
    ppermute x2 -> x29, starting transfers between devices: 0.88 us -> 29.1 us  [swap(): lax.ppermute(value, axis, [(source, source ^ mask) for source in range(la...]
    concatenate x4 -> x2, other arithmetic: 10.2 us -> 0.06 us  [the longest x1 0.04 us: over_second(): return jnp.concatenate((one, two), axis=1)]
  transfers between devices with their start and end apart: 6 -> 31, of which waited for: 5 -> 12; matrix products, arithmetic and copies ran while one was open for 5% -> 5% of each run, Pallas kernels for 21% -> 26%
where the time goes in v2:
time: 328 us; the launch traced here: 327 us
  Pallas kernels  164 us (50%)
  waiting for transfers between devices  89.1 us (27%)
  starting transfers between devices  29.1 us (9%)
  local copies, waits for them, and re-layouts  18.3 us (6%)
  between operations  14.5 us (4%)
  other arithmetic  9.48 us (3%)
    ppermute x29, waiting for transfers between devices, swap(): lax.ppermute(value, axis, [(source, source ^ mask) for source in range(la...  52.9 us
    pallas_call x1, Pallas kernels, ffn_forward(): call(ffn_forward_body, (rows // span, chunks), [row_spec, row_spec, row_s...  34.1 us
    ppermute x29, starting transfers between devices, swap(): lax.ppermute(value, axis, [(source, source ^ mask) for source in range(la...  29.1 us
    pallas_call x1, Pallas kernels, ffn_backward(): call(ffn_backward_body, (FF // D,), [whole((rows, D)), pl.BlockSpec((rows...  26.4 us
    all_gather x1, waiting for transfers between devices, gather(): return lax.all_gather(value, BOTH, axis=0)  24.4 us
    pallas_call x1, Pallas kernels, attend_back(): call(attend_back_body, (seqs, H // 2), [spec] * 3 + [pl.BlockSpec((1, 2,...  19.6 us
    pallas_call x1, Pallas kernels, attend(): call(attend_body, (seqs, H // 2), [spec] * 3, [spec, pl.BlockSpec((1, 2,...  18.5 us
    pallas_call x1, Pallas kernels, first_back(): call(first_back_body, (rows // step,), [row_spec, row_spec, row_spec, pl....  15.1 us
  transfers between devices with their start and end apart: 31, of which 12 were waited for; matrix products, arithmetic and copies ran while one was open for 5% of the time, Pallas kernels for 26%

profile of v2, /device:TPU:0, one launch (start us, length us, event | category | flops | bytes accessed | tf_op | source)
XLA Modules:
  0.0 326.7 jit_solution(475313243034617847)
XLA Ops:
  7.3 1.0 dynamic_update_slice.7
  9.0 1.0 reshape.183
  10.0 1.1 reshape.182
  12.0 0.9 dynamic_update_slice.6
  14.7 0.8 reshape.177
  15.5 0.8 reshape.178
  17.9 4.1 %collective-permute-start.2 = (bf16[80,768]{1,0:T(8,128)(2,1)S(1)}, bf16[80,768]{1,0:T(8,128)(2,1)S(1)}, u32[]{:S(2)}, u32[]{:S(2)}) collective-permute-start(bf16[80,768]{1,0:T(8,128)(2,1)S(1)} %pad_maximum_fusion.3), channel_id=1, source_target_pairs={{0,4},{1,5},{2,6},{3,7},{4,0},{5,1},{6,2},{7,3},{8,12},{9,13},{10,... | collective-permute-start | bytes 368648 | tf_op jit(solution)/shard_map/ppermute | solution.py:33
  22.0 1.6 collective-permute-start.1
  23.6 9.3 %collective-permute-done.2 = bf16[80,768]{1,0:T(8,128)(2,1)S(1)} collective-permute-done((bf16[80,768]{1,0:T(8,128)(2,1)S(1)}, bf16[80,768]{1,0:T(8,128)(2,1)S(1)}, u32[]{:S(2)}, u32[]{:S(2)}) %collective-permute-start.2) | collective-permute-done | bytes 122912 | tf_op jit(solution)/shard_map/ppermute | solution.py:33
  32.9 3.4 %collective-permute-done.3 = bf16[80,768]{1,0:T(8,128)(2,1)S(1)} collective-permute-done((bf16[80,768]{1,0:T(8,128)(2,1)S(1)}, bf16[80,768]{1,0:T(8,128)(2,1)S(1)}, u32[]{:S(2)}, u32[]{:S(2)}) %collective-permute-start.3) | collective-permute-done | bytes 122912 | tf_op jit(solution)/shard_map/ppermute | solution.py:33
  36.4 1.6 collective-permute-start.5
  38.0 1.5 collective-permute-start.4
  39.6 7.1 %collective-permute-done.5.refs_2_ = bf16[4,80,768]{2,1,0:T(8,128)(2,1)S(1)} collective-permute-done((bf16[4,80,768]{2,1,0:T(8,128)(2,1)S(1)}, bf16[4,80,768]{2,1,0:T(8,128)(2,1)S(1)}, u32[]{:S(2)}, u32[]{:S(2)}) %collective-permute-start.5) | collective-permute-done | bytes 491552 | tf_op jit(solution)/shard_map/ppermute | solution.py:33
  46.7 1.3 collective-permute-start.6
  48.1 4.0 %collective-permute-done.4.refs_1_ = bf16[4,80,768]{2,1,0:T(8,128)(2,1)S(1)} collective-permute-done((bf16[4,80,768]{2,1,0:T(8,128)(2,1)S(1)}, bf16[4,80,768]{2,1,0:T(8,128)(2,1)S(1)}, u32[]{:S(2)}, u32[]{:S(2)}) %collective-permute-start.4) | collective-permute-done | bytes 491552 | tf_op jit(solution)/shard_map/ppermute | solution.py:33
  53.5 6.5 %collective-permute-done.6 = bf16[4,40,768]{2,1,0:T(8,128)(2,1)S(1)} collective-permute-done((bf16[4,40,768]{2,1,0:T(8,128)(2,1)S(1)}, bf16[4,40,768]{2,1,0:T(8,128)(2,1)S(1)}, u32[]{:S(2)}, u32[]{:S(2)}) %collective-permute-start.6) | collective-permute-done | bytes 245792 | tf_op jit(solution)/shard_map/ppermute | solution.py:33
  61.4 1.3 fusion.1.order_ref
  63.9 9.9 %project.1 = (bf16[1024,768]{1,0:T(8,128)(2,1)}, bf16[1024,768]{1,0:T(8,128)(2,1)}, bf16[1024,768]{1,0:T(8,128)(2,1)}, bf16[3,768,768]{2,1,0:T(8,128)(2,1)}, f32[8,768]{1,0:T(8,128)}) custom-call(s32[1]{0:T(128)} %bitcast.me_ref, bf16[1024,768]{1,0:T(8,128)(2,1)} %bitcast.114, bf16[1024,768]{1,0:T(8,128)(2,1)} %collective-permute-done.xp_ref, ...), custom_call_target="tpu_custom_call" | custom-call | flops 3623878656 | bytes 14942208 | tf_op jit(solution)/shard_map/project/pallas_call | solution.py:109
  73.9 18.5 %attend.1 = (bf16[1024,768]{1,0:T(8,128)(2,1)}, bf16[2,12,512,512]{3,2,1,0:T(8,128)(2,1)}) custom-call(s32[2,2]{1,0:T(2,128)} %pad_add_fusion.valid_ref, bf16[1024,768]{1,0:T(8,128)(2,1)} %get-tuple-element.51.q_ref, bf16[1024,768]{1,0:T(8,128)(2,1)} %get-tuple-element.52.k_ref, bf16[1024,768]{1,0:T(8,128)(2,1)} %get-tuple-element.53.v_ref), custom_call_target="tpu_custom_call" | custom-call | flops 6442450944 | bytes 18874368 | tf_op jit(solution)/shard_map/attend/pallas_call | solution.py:148
  92.4 24.4 %all-gather.3.cloned.1.call-done = bf16[7168,768]{1,0:T(8,128)(2,1)} async-done(((bf16[224,768]{1,0:T(8,128)(2,1)}), bf16[7168,768]{1,0:T(8,128)(2,1)}) %all-gather.3.cloned.1.call-update) | async-done | bytes 11010064 | tf_op jit(solution)/shard_map/all_gather | solution.py:656
  116.8 8.0 %first_norm.1 = (f32[1024,768]{1,0:T(8,128)}, f32[1024,128]{1,0:T(8,128)}, bf16[1024,768]{1,0:T(8,128)(2,1)}, bf16[768,768]{1,0:T(8,128)(2,1)}, f32[8,768]{1,0:T(8,128)}) custom-call(bf16[1024,768]{1,0:T(8,128)(2,1)} %get-tuple-element.54.ctx_ref, bf16[1024,768]{1,0:T(8,128)(2,1)} %bitcast.115, bf16[32,224,768]{2,1,0:T(8,128)(2,1)} %bitcast.99, ...), custom_call_target="tpu_custom_call" | custom-call | flops 1207959552 | bytes 9437184 | tf_op jit(solution)/shard_map/first_norm/pallas_call | solution.py:244
  124.8 34.1 %ffn_forward.1 = (bf16[1024,3072]{1,0:T(8,128)(2,1)}, bf16[1024,3072]{1,0:T(8,128)(2,1)}, bf16[1024,768]{1,0:T(8,128)(2,1)}, f32[1024,768]{1,0:T(8,128)}, bf16[1024,768]{1,0:T(8,128)(2,1)}, /*index=5*/f32[8,768]{1,0:T(8,128)}) custom-call(bf16[1024,768]{1,0:T(8,128)(2,1)} %get-tuple-element.56.low_ref, f32[1024,768]{1,0:T(8,128)} %get-tuple-element.57.hat_ref, ...), custom_call_target="tpu_custom_call" | custom-call | flops 9663676416 | bytes 29884416 | tf_op jit(solution)/shard_map/ffn_forward/pallas_call | solution.py:349
  158.9 9.2 %grad_down.1 = bf16[32,96,768]{2,1,0:T(8,128)(2,1)} custom-call(bf16[1024,3072]{1,0:T(8,128)(2,1)} %get-tuple-element.60.act_ref, bf16[1024,768]{1,0:T(8,128)(2,1)} %get-tuple-element.62.gsec_ref), custom_call_target="tpu_custom_call" | custom-call | flops 4831838208 | bytes 12582912 | tf_op jit(solution)/shard_map/grad_down/pallas_call | solution.py:383
  168.1 26.4 %ffn_backward.1 = (bf16[16,96,768]{2,1,0:T(8,128)(2,1)}, bf16[16,96,768]{2,1,0:T(8,128)(2,1)}, f32[4,1,768]{2,1,0:T(1,128)}, f32[1024,768]{1,0:T(8,128)}) custom-call(s32[1]{0:T(128)} %bitcast.me_ref, bf16[1024,768]{1,0:T(8,128)(2,1)} %get-tuple-element.62.gsec_ref, bf16[1024,3072]{1,0:T(8,128)(2,1)} %get-tuple-element.63.slope_ref, ...), custom_call_target="tpu_custom_call" | custom-call | flops 14495514624 | bytes 26738688 | tf_op jit(solution)/shard_map/ffn_backward/pallas_call | solution.py:435
  194.8 15.1 %first_back.1 = (f32[1024,768]{1,0:T(8,128)}, bf16[1024,768]{1,0:T(8,128)(2,1)}, bf16[32,24,768]{2,1,0:T(8,128)(2,1)}, f32[16,1024]{1,0:T(8,128)}, f32[8,768]{1,0:T(8,128)}) custom-call(f32[1024,768]{1,0:T(8,128)} %get-tuple-element.66.acc_ref, f32[1024,768]{1,0:T(8,128)} %get-tuple-element.67.gtwo_ref, f32[1024,768]{1,0:T(8,128)} %get-tuple-element.57.hat_ref, ...), custom_call_target="tpu_custom_call" | custom-call | flops 2415919104 | bytes 19267584 | tf_op jit(solution)/shard_map/first_back/pallas_call | solution.py:502
  210.0 1.4 copy-done.1
  211.4 3.2 add.89
  214.5 0.9 slice_bitcast_fusion.4
  215.4 1.5 collective-permute-start.13
  217.5 19.6 %attend_back.1 = (bf16[3,1024,768]{2,1,0:T(8,128)(2,1)}, bf16[2,1024,384]{2,1,0:T(8,128)(2,1)}) custom-call(bf16[1024,768]{1,0:T(8,128)(2,1)} %get-tuple-element.51.q_ref, bf16[1024,768]{1,0:T(8,128)(2,1)} %get-tuple-element.52.k_ref, bf16[1024,768]{1,0:T(8,128)(2,1)} %get-tuple-element.53.v_ref, bf16[2,12,512,512]{3,2,1,0:T(8,128)(2,1)} %get-tuple-element.72.p_ref, ...), custom_call_target="tpu_custom_call" | custom-call | flops 12884901888 | bytes 23592960 | tf_op jit(solution)/shard_map/attend_back/pallas_call | solution.py:193
  237.4 13.8 %grad_project.1 = (bf16[16,104,768]{2,1,0:T(8,128)(2,1)}, bf16[16,104,768]{2,1,0:T(8,128)(2,1)}) custom-call(s32[1]{0:T(128)} %bitcast.me_ref, bf16[1024,768]{1,0:T(8,128)(2,1)} %bitcast.116, bf16[1024,768]{1,0:T(8,128)(2,1)} %collective-permute-done.xp_ref, bf16[3,1024,768]{2,1,0:T(8,128)(2,1)} %get-tuple-element.76.grad_ref.grads_ref, ...), custom_call_target="tpu_custom_call" | custom-call | flops 3623878656 | bytes 14942208 | tf_op jit(solution)/shard_map/grad_project/pallas_call | solution.py:599
  251.2 1.6 collective-permute-start.17
  253.4 7.3 %collective-permute-done.17 = bf16[4,48,768]{2,1,0:T(8,128)(2,1)S(1)} collective-permute-done((bf16[4,48,768]{2,1,0:T(8,128)(2,1)S(1)}, bf16[4,48,768]{2,1,0:T(8,128)(2,1)S(1)}, u32[]{:S(2)}, u32[]{:S(2)}) %collective-permute-start.17) | collective-permute-done | bytes 294944 | tf_op jit(solution)/shard_map/ppermute | solution.py:33
  260.7 1.3 collective-permute-done.16
  263.6 1.5 collective-permute-start.19
  265.1 1.4 collective-permute-start.26
  266.5 2.0 collective-permute-start.28
  268.5 13.4 %collective-permute-done.21 = bf16[4,2,48,768]{3,2,0,1:T(8,128)(2,1)S(1)} collective-permute-done((bf16[4,2,48,768]{3,2,0,1:T(8,128)(2,1)S(1)}, bf16[4,2,48,768]{3,2,0,1:T(8,128)(2,1)S(1)}, u32[]{:S(2)}, u32[]{:S(2)}) %collective-permute-start.21) | collective-permute-done | bytes 589856 | tf_op jit(solution)/shard_map/ppermute | solution.py:33
  281.9 1.9 collective-permute-start.27
  283.9 1.1 collective-permute-start.22
  285.2 1.0 collective-permute-start.20
  286.3 9.6 %grad_input.1 = f32[1024,768]{1,0:T(8,128)} custom-call(f32[1024,768]{1,0:T(8,128)} %get-tuple-element.86.gres_ref, bf16[3,1024,768]{2,1,0:T(8,128)(2,1)} %get-tuple-element.76.grad_ref.grads_ref, bf16[2,1024,384]{2,1,0:T(8,128)(2,1)} %collective-permute-done.18.back_ref, bf16[3,768,768]{2,1,0:T(8,128)(2,1)} %get-tuple-element.88.w_ref), custom_call_target="tpu_custom_call" | custom-call | flops 3623878656 | bytes 16121856 | tf_op jit(solution)/shard_map/grad_input/pallas_call | solution.py:638
  296.0 1.0 collective-permute-start.23
  297.0 2.0 collective-permute-start.25
  299.8 0.8 reshape.194
  300.6 11.7 %reduce-scatter.2.cloned.1.call-done = bf16[1,96,768]{2,1,0:T(8,128)(2,1)} async-done(((bf16[32,96,768]{2,1,0:T(8,128)(2,1)}), bf16[1,96,768]{2,1,0:T(8,128)(2,1)}) %reduce-scatter.2.cloned.1.call-update) | async-done | bytes 147472 | tf_op jit(solution)/shard_map/reduce_scatter | solution.py:660
  312.3 1.8 reshape.199
  315.9 1.4 fusion
  (125 shorter events, 18.3 us)
Async XLA Ops:
  7.2 16.4 %copy-start.2 = (bf16[2,1,512,768]{3,2,1,0:T(8,128)(2,1)S(1)}, bf16[2,1,512,768]{3,2,1,0:T(8,128)(2,1)}, u32[]{:S(2)}) copy-start(bf16[2,1,512,768]{3,2,1,0:T(8,128)(2,1)} %param.12) | copy-start | bytes 4718596
  7.2 109.6 %all-gather.3.cloned.1.call-start = ((), (), s32[]{:S(2)}) async-start(), calls=%async_computation.2 | async-start | bytes 11354112 | tf_op jit(solution)/shard_map/all_gather | solution.py:656
  11.9 300.4 %reduce-scatter.2.cloned.1.call-start = ((), (), s32[]{:S(2)}) async-start(), calls=%async_computation.1 | async-start | bytes 4866048 | tf_op jit(solution)/shard_map/reduce_scatter | solution.py:660
  14.7 46.7 %copy-start.7 = (s32[768]{0:T(1024)}, s32[768]{0:T(1024)S(1)}, u32[]{:S(2)}) copy-start(s32[768]{0:T(1024)S(1)} %add.87) | copy-start | bytes 9220
  17.2 43.5 %copy-start.9 = (s32[2,2]{1,0:T(2,128)S(1)}, s32[2,2]{1,0:T(2,128)}, u32[]{:S(2)}) copy-start(s32[2,2]{1,0:T(2,128)} %param.14) | copy-start | bytes 52
  17.9 15.1 %collective-permute-start.2 = (bf16[80,768]{1,0:T(8,128)(2,1)S(1)}, bf16[80,768]{1,0:T(8,128)(2,1)S(1)}, u32[]{:S(2)}, u32[]{:S(2)}) collective-permute-start(bf16[80,768]{1,0:T(8,128)(2,1)S(1)} %pad_maximum_fusion.3), channel_id=1, source_target_pairs={{0,4},{1,5},{2,6},{3,7},{4,0},{5,1},{6,2},{7,3},{8,12},{9,13},{10,... | collective-permute-start | bytes 368648 | tf_op jit(solution)/shard_map/ppermute | solution.py:33
  22.0 10.9 %collective-permute-start.1 = (bf16[80,768]{1,0:T(8,128)(2,1)S(1)}, bf16[80,768]{1,0:T(8,128)(2,1)S(1)}, u32[]{:S(2)}, u32[]{:S(2)}) collective-permute-start(bf16[80,768]{1,0:T(8,128)(2,1)S(1)} %pad_maximum_fusion.3), channel_id=1, source_target_pairs={{0,2},{1,3},{2,0},{3,1},{4,6},{5,7},{6,4},{7,5},{8,10},{9,11},{10,... | collective-permute-start | bytes 368648 | tf_op jit(solution)/shard_map/ppermute | solution.py:33
  23.6 12.8 %collective-permute-start.3 = (bf16[80,768]{1,0:T(8,128)(2,1)S(1)}, bf16[80,768]{1,0:T(8,128)(2,1)S(1)}, u32[]{:S(2)}, u32[]{:S(2)}) collective-permute-start(bf16[80,768]{1,0:T(8,128)(2,1)S(1)} %pad_maximum_fusion.3), channel_id=1, source_target_pairs={{0,6},{1,7},{2,4},{3,5},{4,2},{5,3},{6,0},{7,1},{8,14},{9,15},{10,... | collective-permute-start | bytes 368648 | tf_op jit(solution)/shard_map/ppermute | solution.py:33
  23.6 39.2 %collective-permute-start = (bf16[1024,768]{1,0:T(8,128)(2,1)S(1)}, bf16[1024,768]{1,0:T(8,128)(2,1)}, u32[]{:S(2)}, u32[]{:S(2)}) collective-permute-start(bf16[1024,768]{1,0:T(8,128)(2,1)S(1)} %bitcast.117), channel_id=1, source_target_pairs={{0,8},{8,0},{16,24},{24,16},{1,9},{9,1},{17,25},{25,17},{2,10},{10... | collective-permute-start | bytes 4718600 | tf_op jit(solution)/shard_map/ppermute | solution.py:33
  36.4 27.4 %copy-start.3 = (bf16[4,80,768]{2,1,0:T(8,128)(2,1)}, bf16[4,80,768]{2,1,0:T(8,128)(2,1)S(1)}, u32[]{:S(2)}) copy-start(bf16[4,80,768]{2,1,0:T(8,128)(2,1)S(1)} %pad_maximum_fusion.1.refs_0_) | copy-start | bytes 1474564
  36.4 10.3 %collective-permute-start.5 = (bf16[4,80,768]{2,1,0:T(8,128)(2,1)S(1)}, bf16[4,80,768]{2,1,0:T(8,128)(2,1)S(1)}, u32[]{:S(2)}, u32[]{:S(2)}) collective-permute-start(bf16[4,80,768]{2,1,0:T(8,128)(2,1)S(1)} %pad_maximum_fusion.1.refs_0_), channel_id=1, source_target_pairs={{0,16},{8,24},{16,0},{24,8},{1,17},{9,25},{17,1},{25,9},{2,18},{10... | collective-permute-start | bytes 1474568 | tf_op jit(solution)/shard_map/ppermute | solution.py:33
  38.0 14.0 %collective-permute-start.4 = (bf16[4,80,768]{2,1,0:T(8,128)(2,1)S(1)}, bf16[4,80,768]{2,1,0:T(8,128)(2,1)S(1)}, u32[]{:S(2)}, u32[]{:S(2)}) collective-permute-start(bf16[4,80,768]{2,1,0:T(8,128)(2,1)S(1)} %pad_maximum_fusion.1.refs_0_), channel_id=1, source_target_pairs={{0,1},{1,0},{2,3},{3,2},{4,5},{5,4},{6,7},{7,6},{8,9},{9,8},{10,11... | collective-permute-start | bytes 1474568 | tf_op jit(solution)/shard_map/ppermute | solution.py:33
  46.7 17.1 %copy-start.4 = (bf16[4,80,768]{2,1,0:T(8,128)(2,1)}, bf16[4,80,768]{2,1,0:T(8,128)(2,1)S(1)}, u32[]{:S(2)}) copy-start(bf16[4,80,768]{2,1,0:T(8,128)(2,1)S(1)} %collective-permute-done.5.refs_2_) | copy-start | bytes 1474564
  46.7 13.3 %collective-permute-start.6 = (bf16[4,40,768]{2,1,0:T(8,128)(2,1)S(1)}, bf16[4,40,768]{2,1,0:T(8,128)(2,1)S(1)}, u32[]{:S(2)}, u32[]{:S(2)}) collective-permute-start(bf16[4,40,768]{2,1,0:T(8,128)(2,1)S(1)} %slice.200), channel_id=1, source_target_pairs={{0,1},{1,0},{2,3},{3,2},{4,5},{5,4},{6,7},{7,6},{8,9},{9,8},{10,11... | collective-permute-start | bytes 737288 | tf_op jit(solution)/shard_map/ppermute | solution.py:33
  52.0 0.8 copy-start.5
  52.8 7.2 %collective-permute-start.7 = (bf16[4,40,768]{2,1,0:T(8,128)(2,1)S(1)}, bf16[4,40,768]{2,1,0:T(8,128)(2,1)S(1)}, u32[]{:S(2)}, u32[]{:S(2)}) collective-permute-start(bf16[4,40,768]{2,1,0:T(8,128)(2,1)S(1)} %slice.201), channel_id=1, source_target_pairs={{0,16},{8,24},{16,0},{24,8},{1,17},{9,25},{17,1},{25,9},{2,18},{10... | collective-permute-start | bytes 737288 | tf_op jit(solution)/shard_map/ppermute | solution.py:33
  52.9 9.7 %collective-permute-start.8 = (bf16[4,80,768]{2,1,0:T(8,128)(2,1)S(1)}, bf16[4,80,768]{2,1,0:T(8,128)(2,1)S(1)}, u32[]{:S(2)}, u32[]{:S(2)}) collective-permute-start(bf16[4,80,768]{2,1,0:T(8,128)(2,1)S(1)} %pad_maximum_fusion.1.refs_0_), channel_id=1, source_target_pairs={{0,8},{8,0},{16,24},{24,16},{1,9},{9,1},{17,25},{25,17},{2,10},{10... | collective-permute-start | bytes 1474568 | tf_op jit(solution)/shard_map/ppermute | solution.py:33
  53.0 9.7 %collective-permute-start.10 = (bf16[4,80,768]{2,1,0:T(8,128)(2,1)S(1)}, bf16[4,80,768]{2,1,0:T(8,128)(2,1)S(1)}, u32[]{:S(2)}, u32[]{:S(2)}) collective-permute-start(bf16[4,80,768]{2,1,0:T(8,128)(2,1)S(1)} %collective-permute-done.5.refs_2_), channel_id=1, source_target_pairs={{0,8},{8,0},{16,24},{24,16},{1,9},{9,1},{17,25},{25,17},{2,10},{10... | collective-permute-start | bytes 1474568 | tf_op jit(solution)/shard_map/ppermute | solution.py:33
  60.0 2.7 collective-permute-start.9
  60.1 3.7 %copy-start.6 = (bf16[4,80,768]{2,1,0:T(8,128)(2,1)}, bf16[4,80,768]{2,1,0:T(8,128)(2,1)S(1)}, u32[]{:S(2)}) copy-start(bf16[4,80,768]{2,1,0:T(8,128)(2,1)S(1)} %constant_dynamic-update-slice_fusion.refs_3_) | copy-start | bytes 1474564
  60.1 2.7 collective-permute-start.11
  62.7 0.8 copy-start.11
  62.7 0.9 copy-start.12
  62.7 1.1 copy-start.13
  62.8 1.2 copy-start.14
  194.5 15.4 %collective-permute-start.12 = (bf16[16,96,768]{2,1,0:T(8,128)(2,1)}, bf16[16,96,768]{2,1,0:T(8,128)(2,1)S(1)}, u32[]{:S(2)}, u32[]{:S(2)}) collective-permute-start(bf16[16,96,768]{2,1,0:T(8,128)(2,1)} %get-tuple-element.65), channel_id=1, source_target_pairs={{0,8},{8,0},{16,24},{24,16},{1,9},{9,1},{17,25},{25,17},{2,10},{10... | collective-permute-start | bytes 7077896 | tf_op jit(solution)/shard_map/ppermute | solution.py:33
  210.0 1.4 copy-start.1
  215.4 21.6 %collective-permute-start.13 = (bf16[2,4,48,768]{3,2,1,0:T(8,128)(2,1)S(1)}, bf16[2,4,48,768]{3,2,1,0:T(8,128)(2,1)S(1)}, u32[]{:S(2)}, u32[]{:S(2)}) collective-permute-start(bf16[2,4,48,768]{3,2,1,0:T(8,128)(2,1)S(1)} %slice_bitcast_fusion.6), channel_id=1, source_target_pairs={{0,1},{1,0},{2,3},{3,2},{4,5},{5,4},{6,7},{7,6},{8,9},{9,8},{10,11... | collective-permute-start | bytes 1769480 | tf_op jit(solution)/shard_map/ppermute | solution.py:33
  217.0 20.3 %collective-permute-start.14 = (bf16[4,2,48,768]{3,2,0,1:T(8,128)(2,1)}, bf16[4,2,48,768]{3,2,0,1:T(8,128)(2,1)S(1)}, u32[]{:S(2)}, u32[]{:S(2)}) collective-permute-start(bf16[4,2,48,768]{3,2,0,1:T(8,128)(2,1)} %slice_bitcast_fusion.4), channel_id=1, source_target_pairs={{0,16},{8,24},{16,0},{24,8},{1,17},{9,25},{17,1},{25,9},{2,18},{10... | collective-permute-start | bytes 1769480 | tf_op jit(solution)/shard_map/ppermute | solution.py:33
  251.2 10.9 %copy-start = (bf16[16,104,768]{2,1,0:T(8,128)(2,1)S(1)}, bf16[16,104,768]{2,1,0:T(8,128)(2,1)}, u32[]{:S(2)}) copy-start(bf16[16,104,768]{2,1,0:T(8,128)(2,1)} %get-tuple-element.81) | copy-start | bytes 7667716
  251.2 10.9 %collective-permute-start.15 = (bf16[16,104,768]{2,1,0:T(8,128)(2,1)}, bf16[16,104,768]{2,1,0:T(8,128)(2,1)S(1)}, u32[]{:S(2)}, u32[]{:S(2)}) collective-permute-start(bf16[16,104,768]{2,1,0:T(8,128)(2,1)} %get-tuple-element.82), channel_id=1, source_target_pairs={{0,8},{8,0},{16,24},{24,16},{1,9},{9,1},{17,25},{25,17},{2,10},{10... | collective-permute-start | bytes 7667720 | tf_op jit(solution)/shard_map/ppermute | solution.py:33
  251.2 9.5 %collective-permute-start.17 = (bf16[4,48,768]{2,1,0:T(8,128)(2,1)S(1)}, bf16[4,48,768]{2,1,0:T(8,128)(2,1)S(1)}, u32[]{:S(2)}, u32[]{:S(2)}) collective-permute-start(bf16[4,48,768]{2,1,0:T(8,128)(2,1)S(1)} %slice_bitcast_fusion.12), channel_id=1, source_target_pairs={{0,1},{1,0},{2,3},{3,2},{4,5},{5,4},{6,7},{7,6},{8,9},{9,8},{10,11... | collective-permute-start | bytes 884744 | tf_op jit(solution)/shard_map/ppermute | solution.py:33
  252.8 9.2 %collective-permute-start.16 = (bf16[4,48,768]{2,1,0:T(8,128)(2,1)S(1)}, bf16[4,48,768]{2,1,0:T(8,128)(2,1)S(1)}, u32[]{:S(2)}, u32[]{:S(2)}) collective-permute-start(bf16[4,48,768]{2,1,0:T(8,128)(2,1)S(1)} %slice_bitcast_fusion.13), channel_id=1, source_target_pairs={{0,16},{8,24},{16,0},{24,8},{1,17},{9,25},{17,1},{25,9},{2,18},{10... | collective-permute-start | bytes 884744 | tf_op jit(solution)/shard_map/ppermute | solution.py:33
  262.1 1.4 copy-start.10
  262.9 19.0 %collective-permute-start.21 = (bf16[4,2,48,768]{3,2,0,1:T(8,128)(2,1)S(1)}, bf16[4,2,48,768]{3,2,0,1:T(8,128)(2,1)S(1)}, u32[]{:S(2)}, u32[]{:S(2)}) collective-permute-start(bf16[4,2,48,768]{3,2,0,1:T(8,128)(2,1)S(1)} %slice_bitcast_fusion.2), channel_id=1, source_target_pairs={{0,16},{8,24},{16,0},{24,8},{1,17},{9,25},{17,1},{25,9},{2,18},{10... | collective-permute-start | bytes 1769480 | tf_op jit(solution)/shard_map/ppermute | solution.py:33
  263.5 21.7 %collective-permute-start.18 = (bf16[2,1024,384]{2,1,0:T(8,128)(2,1)S(1)}, bf16[2,1024,384]{2,1,0:T(8,128)(2,1)}, u32[]{:S(2)}, u32[]{:S(2)}) collective-permute-start(bf16[2,1024,384]{2,1,0:T(8,128)(2,1)S(1)} %copy-done.10), channel_id=1, source_target_pairs={{0,8},{8,0},{16,24},{24,16},{1,9},{9,1},{17,25},{25,17},{2,10},{10... | collective-permute-start | bytes 4718600 | tf_op jit(solution)/shard_map/ppermute | solution.py:33
  263.6 20.3 %collective-permute-start.19 = (bf16[2,4,56,768]{3,2,1,0:T(8,128)(2,1)S(1)}, bf16[2,4,56,768]{3,2,1,0:T(8,128)(2,1)S(1)}, u32[]{:S(2)}, u32[]{:S(2)}) collective-permute-start(bf16[2,4,56,768]{3,2,1,0:T(8,128)(2,1)S(1)} %slice_bitcast_fusion), channel_id=1, source_target_pairs={{0,1},{1,0},{2,3},{3,2},{4,5},{5,4},{6,7},{7,6},{8,9},{9,8},{10,11... | collective-permute-start | bytes 2064392 | tf_op jit(solution)/shard_map/ppermute | solution.py:33
  265.1 33.9 %collective-permute-start.26 = (bf16[96,768]{1,0:T(8,128)(2,1)S(1)}, bf16[96,768]{1,0:T(8,128)(2,1)S(1)}, u32[]{:S(2)}, u32[]{:S(2)}) collective-permute-start(bf16[96,768]{1,0:T(8,128)(2,1)S(1)} %get-tuple-element.125), channel_id=1, source_target_pairs={{0,2},{1,3},{2,0},{3,1},{4,6},{5,7},{6,4},{7,5},{8,10},{9,11},{10,... | collective-permute-start | bytes 442376 | tf_op jit(solution)/shard_map/ppermute | solution.py:33
  266.5 33.1 %collective-permute-start.28 = (bf16[96,768]{1,0:T(8,128)(2,1)S(1)}, bf16[96,768]{1,0:T(8,128)(2,1)S(1)}, u32[]{:S(2)}, u32[]{:S(2)}) collective-permute-start(bf16[96,768]{1,0:T(8,128)(2,1)S(1)} %get-tuple-element.126), channel_id=1, source_target_pairs={{0,6},{1,7},{2,4},{3,5},{4,2},{5,3},{6,0},{7,1},{8,14},{9,15},{10,... | collective-permute-start | bytes 442376 | tf_op jit(solution)/shard_map/ppermute | solution.py:33
  281.9 17.7 %collective-permute-start.27 = (bf16[96,768]{1,0:T(8,128)(2,1)S(1)}, bf16[96,768]{1,0:T(8,128)(2,1)S(1)}, u32[]{:S(2)}, u32[]{:S(2)}) collective-permute-start(bf16[96,768]{1,0:T(8,128)(2,1)S(1)} %get-tuple-element.127), channel_id=1, source_target_pairs={{0,4},{1,5},{2,6},{3,7},{4,0},{5,1},{6,2},{7,3},{8,12},{9,13},{10,... | collective-permute-start | bytes 442376 | tf_op jit(solution)/shard_map/ppermute | solution.py:33
  283.9 12.0 %collective-permute-start.22 = (bf16[4,48,768]{2,1,0:T(8,128)(2,1)S(1)}, bf16[4,48,768]{2,1,0:T(8,128)(2,1)S(1)}, u32[]{:S(2)}, u32[]{:S(2)}) collective-permute-start(bf16[4,48,768]{2,1,0:T(8,128)(2,1)S(1)} %slice_bitcast_fusion.10), channel_id=1, source_target_pairs={{0,1},{1,0},{2,3},{3,2},{4,5},{5,4},{6,7},{7,6},{8,9},{9,8},{10,11... | collective-permute-start | bytes 884744 | tf_op jit(solution)/shard_map/ppermute | solution.py:33
  285.2 10.7 %collective-permute-start.20 = (bf16[4,56,768]{2,1,0:T(8,128)(2,1)S(1)}, bf16[4,56,768]{2,1,0:T(8,128)(2,1)S(1)}, u32[]{:S(2)}, u32[]{:S(2)}) collective-permute-start(bf16[4,56,768]{2,1,0:T(8,128)(2,1)S(1)} %slice_bitcast_fusion.8), channel_id=1, source_target_pairs={{0,16},{8,24},{16,0},{24,8},{1,17},{9,25},{17,1},{25,9},{2,18},{10... | collective-permute-start | bytes 1032200 | tf_op jit(solution)/shard_map/ppermute | solution.py:33
  296.0 19.9 %copy-start.8 = (s32[768]{0:T(1024)S(1)}, s32[768]{0:T(1024)}, u32[]{:S(2)}) copy-start(s32[768]{0:T(1024)} %copy-done.7) | copy-start | bytes 9220
  296.0 18.1 %collective-permute-start.23 = (bf16[104,768]{1,0:T(8,128)(2,1)S(1)}, bf16[104,768]{1,0:T(8,128)(2,1)S(1)}, u32[]{:S(2)}, u32[]{:S(2)}) collective-permute-start(bf16[104,768]{1,0:T(8,128)(2,1)S(1)} %get-tuple-element.122), channel_id=1, source_target_pairs={{0,2},{1,3},{2,0},{3,1},{4,6},{5,7},{6,4},{7,5},{8,10},{9,11},{10,... | collective-permute-start | bytes 479240 | tf_op jit(solution)/shard_map/ppermute | solution.py:33
  297.0 17.1 %collective-permute-start.25 = (bf16[104,768]{1,0:T(8,128)(2,1)S(1)}, bf16[104,768]{1,0:T(8,128)(2,1)S(1)}, u32[]{:S(2)}, u32[]{:S(2)}) collective-permute-start(bf16[104,768]{1,0:T(8,128)(2,1)S(1)} %get-tuple-element.123), channel_id=1, source_target_pairs={{0,6},{1,7},{2,4},{3,5},{4,2},{5,3},{6,0},{7,1},{8,14},{9,15},{10,... | collective-permute-start | bytes 479240 | tf_op jit(solution)/shard_map/ppermute | solution.py:33
  299.0 15.6 %collective-permute-start.24 = (bf16[104,768]{1,0:T(8,128)(2,1)S(1)}, bf16[104,768]{1,0:T(8,128)(2,1)S(1)}, u32[]{:S(2)}, u32[]{:S(2)}) collective-permute-start(bf16[104,768]{1,0:T(8,128)(2,1)S(1)} %get-tuple-element.124), channel_id=1, source_target_pairs={{0,4},{1,5},{2,6},{3,7},{4,0},{5,1},{6,2},{7,3},{8,12},{9,13},{10,... | collective-permute-start | bytes 479240 | tf_op jit(solution)/shard_map/ppermute | solution.py:33
Sparse Core Ops, SparseCore 0:
  12.0 104.7 all-gather.2
  195.0 117.3 reduce-scatter.1

commit v3 on v2

--- a/solution.py
+++ b/solution.py
@@ -78,21 +78,25 @@
 
 
 def project_body(me_ref, x_ref, xp_ref, *refs):
-    pieces, (q_ref, k_ref, v_ref, w_ref, vec_ref, scr) = refs[: len(PIECES)], refs[len(PIECES) :]
+    pieces, (order_ref, q_ref, k_ref, v_ref, w_ref, out_ref, vec_ref, upb_ref, scr) = refs[: len(PIECES)], refs[len(PIECES) :]
 
     @pl.when(pl.program_id(0) == 0)
     def _():
         me = me_ref[0]
         total = jnp.zeros((8, D), f32)
+        up_bias = jnp.zeros((8, D), f32)
         for (core, y, x), piece in zip(PIECES, pieces):
             for z in range(piece.shape[0]):
                 group = (16 * y + 8 * core + 2 * z + x) ^ me
-                for part in range(3):
+                for part in range(4):
                     scr[part, group] = piece[z, part * ROWS : (part + 1) * ROWS, :]
-                total = total + piece[z, 3 * ROWS : 3 * ROWS + 8, :].astype(f32)
+                total = total + piece[z, 4 * ROWS : 4 * ROWS + 8, :].astype(f32)
+                up_bias = up_bias + piece[z, 4 * ROWS + 8 : 4 * ROWS + 16, :].astype(f32)
         vec_ref[...] = total
+        upb_ref[...] = up_bias
         for part in range(3):
             w_ref[part] = scr[part].reshape(D, D)
+        out_ref[...] = dot_tn(order_ref[...], scr[3].reshape(D, D)).astype(bf16)
 
     own, other = x_ref[...], xp_ref[...]
     q_ref[...] = (dot_nn(own, w_ref[0]) + vec_ref[0:1, :]).astype(bf16)
@@ -102,22 +106,22 @@
     v_ref[:, HALF:] = (dot_nn(own, w_ref[2, :, HALF:]) + vec_ref[1:2, HALF:]).astype(bf16)
 
 
-def project(me, x, xp, pieces):
+def project(me, x, xp, pieces, order):
     rows = x.shape[0]
     step = BLOCK
     row_spec = pl.BlockSpec((step, D), lambda i, *_: (i, 0))
     return call(
         project_body,
         (rows // step,),
-        [row_spec, row_spec] + [whole(pieces[0].shape)] * len(PIECES),
-        [row_spec] * 3 + [whole((3, D, D)), whole((8, D))],
-        [sds((rows, D), bf16)] * 3 + [sds((3, D, D), bf16), sds((8, D), f32)],
-        scratch=[pltpu.VMEM((3, GROUPS_W, ROWS, D), bf16)],
+        [row_spec, row_spec] + [whole(pieces[0].shape)] * len(PIECES) + [whole((D, D))],
+        [row_spec] * 3 + [whole((3, D, D)), whole((D, D)), whole((8, D)), whole((8, D))],
+        [sds((rows, D), bf16)] * 3 + [sds((3, D, D), bf16), sds((D, D), bf16), sds((8, D), f32), sds((8, D), f32)],
+        scratch=[pltpu.VMEM((4, GROUPS_W, ROWS, D), bf16)],
         prefetch=1,
         flops=6 * rows * D * D,
         moved=10 * rows * D + 12 * D * D,
         name="project",
-    )(me, x, xp, *pieces)
+    )(me, x, xp, *pieces, order)
 
 
 def attend_body(valid_ref, q_ref, k_ref, v_ref, ctx_ref, p_ref):
@@ -158,7 +162,7 @@
     )(valid, q, k, v)
 
 
-def attend_back_body(q_ref, k_ref, v_ref, p_ref, gctx_ref, delta_ref, out_ref, give_ref):
+def attend_back_body(q_ref, k_ref, v_ref, p_ref, gctx_ref, out_ref, give_ref):
     pair = pl.program_id(1)
     queries, keys, values, grad_ctx = q_ref[...], k_ref[...], v_ref[...], gctx_ref[...]
     lane = lax.broadcasted_iota(jnp.int32, (BLOCK, PAIR), 1)
@@ -167,8 +171,8 @@
     for head in range(2):
         mine = (lane < HD) if head == 0 else (lane >= HD)
         probs = p_ref[0, head]
-        delta = delta_ref[pl.ds(2 * pair + head, 1), :]
         grad_probs = dot_nt(jnp.where(mine, values, jnp.zeros_like(values)), grad_ctx)
+        delta = jnp.sum(probs.astype(f32) * grad_probs, axis=0, keepdims=True)
         grad_scores = (probs.astype(f32) * (grad_probs - delta)).astype(bf16)
         gv.append(dot_nn(probs, grad_ctx))
         gk.append(dot_nn(grad_scores, queries))
@@ -186,7 +190,7 @@
         give_ref[1] = grad_values
 
 
-def attend_back(q, k, v, probs, grad_ctx, delta):
+def attend_back(q, k, v, probs, grad_ctx):
     rows = q.shape[0]
     seqs = rows // BLOCK
     spec = pl.BlockSpec((BLOCK, PAIR), lambda s, j: (s, j))
@@ -197,7 +201,6 @@
         + [
             pl.BlockSpec((1, 2, BLOCK, BLOCK), lambda s, j: (s, j, 0, 0)),
             spec,
-            pl.BlockSpec((16, BLOCK), lambda s, j: (0, s)),
         ],
         [
             pl.BlockSpec((3, BLOCK, PAIR), lambda s, j: (0, s, j)),
@@ -207,27 +210,15 @@
         flops=32 * rows * BLOCK * D,
         moved=14 * rows * D + 2 * rows * H * BLOCK,
         name="attend_back",
-    )(q, k, v, probs, grad_ctx, delta)
+    )(q, k, v, probs, grad_ctx)
 
 
 def mean_last(value):
     return jnp.sum(value, axis=-1, keepdims=True) * (1.0 / D)
 
 
-def first_norm_body(
-    ctx_ref, x_ref, wo_ref, bias_ref, order_ref, vec_ref, hat_ref, inv_ref, low_ref, wop_ref, upb_ref, wo_scr
-):
-    @pl.when(pl.program_id(0) == 0)
-    def _():
-        total = jnp.zeros((8, D), f32)
-        for group in range(GROUPS_W):
-            total = total + bias_ref[group].astype(f32)
-        upb_ref[...] = total
-        permuted = dot_tn(order_ref[...], square(wo_ref)).astype(bf16)
-        wo_scr[...] = permuted
-        wop_ref[...] = permuted
-
-    branch = dot_nn(ctx_ref[...], wo_scr[...]) + vec_ref[2:3, :]
+def first_norm_body(ctx_ref, x_ref, wop_ref, vec_ref, hat_ref, inv_ref, low_ref):
+    branch = dot_nn(ctx_ref[...], wop_ref[...]) + vec_ref[2:3, :]
     residual = x_ref[...].astype(f32) + branch
     centred = residual - mean_last(residual)
     inv = lax.rsqrt(mean_last(centred * centred) + norm_eps)
@@ -237,34 +228,20 @@
     low_ref[...] = (hat * vec_ref[3:4, :] + vec_ref[4:5, :]).astype(bf16)
 
 
-def first_norm(ctx, x, pack, order, vecs):
+def first_norm(ctx, x, wop, vecs):
     rows = x.shape[0]
-    step = 256
+    step = BLOCK
     row_spec = pl.BlockSpec((step, D), lambda i: (i, 0))
     return call(
         first_norm_body,
         (rows // step,),
-        [
-            row_spec,
-            row_spec,
-            pl.BlockSpec((GROUPS_W, ROWS, D), lambda i: (0, 8, 0)),
-            pl.BlockSpec((GROUPS_W, 8, D), lambda i: (0, 27, 0)),
-            whole((D, D)),
-            whole((8, D)),
-        ],
-        [row_spec, pl.BlockSpec((step, LANES), lambda i: (i, 0)), row_spec, whole((D, D)), whole((8, D))],
-        [
-            sds((rows, D), f32),
-            sds((rows, LANES), f32),
-            sds((rows, D), bf16),
-            sds((D, D), bf16),
-            sds((8, D), f32),
-        ],
-        scratch=[pltpu.VMEM((D, D), bf16)],
+        [row_spec, row_spec, whole((D, D)), whole((8, D))],
+        [row_spec, pl.BlockSpec((step, LANES), lambda i: (i, 0)), row_spec],
+        [sds((rows, D), f32), sds((rows, LANES), f32), sds((rows, D), bf16)],
         flops=2 * rows * D * D,
         moved=12 * rows * D,
         name="first_norm",
-    )(ctx, x, pack, pack, order, vecs)
+    )(ctx, x, wop, vecs)
 
 
 def gelu_and_slope(value):
@@ -294,6 +271,10 @@
     def _():
         sums_ref[...] = jnp.zeros_like(sums_ref)
 
+    @pl.when(chunk == 0)
+    def _():
+        acc[...] = jnp.zeros_like(acc)
+
     for start in range(0, rows, step):
         part = pl.ds(start, step)
         hidden = dot_nn(low_ref[part, :], w_up) + bias_ref[pl.ds(chunk, 1), :]
@@ -303,13 +284,7 @@
         slope_ref[part, :] = slope.astype(bf16)
         down = dot_nn(activated, w_down)
 
-        @pl.when(chunk == 0)
-        def _():
-            acc[part, :] = down
-
-        @pl.when(chunk > 0)
-        def _():
-            acc[part, :] += down
+        acc[part, :] += down
 
     @pl.when(chunk == last)
     def _():
@@ -374,22 +349,43 @@
     )(low, hat, cot, pack, pack, up_bias, vecs)
 
 
-def grad_down_body(act_ref, gsec_ref, out_ref):
-    out_ref[...] = dot_tn(act_ref[...], gsec_ref[...]).astype(bf16).reshape(out_ref.shape)
-
-
-def grad_down_of(act, gsec):
+def grad_down_body(me_ref, act_ref, gsec_ref, keep_ref, send_ref, scr):
+    step = pl.program_id(0)
+    scr[...] = dot_tn(act_ref[...], gsec_ref[...]).astype(bf16).reshape(scr.shape)
+    place = jnp.bitwise_and(me_ref[0], 7)
+
+    @pl.when(step < 2)
+    def _():
+        for index in range(8):
+            keep_ref[0, index] = scr[place ^ index]
+
+    @pl.when(step >= 2)
+    def _():
+        for index in range(8):
+            send_ref[0, index] = scr[place ^ index]
+
+
+def grad_down_of(me, act, gsec):
     rows = act.shape[0]
+    block = (1, GROUPS_W // 4, 4 * ROWS, D)
     return call(
         grad_down_body,
         (FF // D,),
-        [pl.BlockSpec((rows, D), lambda c: (0, c)), whole((rows, D))],
-        pl.BlockSpec((GROUPS_W // 4, 4 * ROWS, D), lambda c: (c, 0, 0)),
-        sds((GROUPS_W, 4 * ROWS, D), bf16),
+        [
+            pl.BlockSpec((rows, D), lambda s, me_ref: (0, ((s % 2) * 2 + s // 2) ^ (me_ref[0] // 8))),
+            whole((rows, D)),
+        ],
+        [
+            pl.BlockSpec(block, lambda s, me_ref: (jnp.minimum(s, 1), 0, 0, 0)),
+            pl.BlockSpec(block, lambda s, me_ref: (jnp.maximum(s - 2, 0), 0, 0, 0)),
+        ],
+        [sds((2, *block[1:]), bf16)] * 2,
+        scratch=[pltpu.VMEM(block[1:], bf16)],
+        prefetch=1,
         flops=2 * rows * D * FF,
         moved=10 * rows * D + 2 * D * FF,
         name="grad_down",
-    )(act, gsec)
+    )(me, act, gsec)
 
 
 def apart(scr, me, keep, send):
@@ -454,7 +450,7 @@
 
 def first_back_body(
     acc_ref, gtwo_ref, hat_ref, inv_ref, ctx_ref, wop_ref, order_ref, vec_ref,
-    gres_ref, gctx_ref, gout_ref, delta_ref, sums_ref, gout_scr,
+    gres_ref, gctx_ref, gout_ref, sums_ref, gout_scr,
 ):
     index, last = pl.program_id(0), pl.num_programs(0) - 1
     hat = hat_ref[...]
@@ -465,15 +461,7 @@
     gres_ref[...] = grad
     low = grad.astype(bf16)
     ctx = ctx_ref[...]
-    grad_ctx = dot_nt(low, wop_ref[...]).astype(bf16)
-    gctx_ref[...] = grad_ctx
-    head = lax.broadcasted_iota(jnp.int32, (16, D), 0)
-    owner = lax.broadcasted_iota(jnp.int32, (16, D), 1) // HD
-    chooser = jnp.where(head == owner, 1.0, 0.0).astype(f32)
-    product = grad_ctx.astype(f32) * ctx.astype(f32)
-    delta_ref[...] = lax.dot_general(
-        chooser, product, (((1,), (1,)), ((), ())), preferred_element_type=f32, precision=lax.Precision.HIGHEST
-    )
+    gctx_ref[...] = dot_nt(low, wop_ref[...]).astype(bf16)
     grad_out = dot_tn(ctx, low)
 
     @pl.when(index == 0)
@@ -516,14 +504,12 @@
             row_spec,
             row_spec,
             whole((GROUPS_W, ROWS, D)),
-            pl.BlockSpec((16, step), lambda i: (0, i)),
             whole((8, D)),
         ],
         [
             sds((rows, D), f32),
             sds((rows, D), bf16),
             sds((GROUPS_W, ROWS, D), bf16),
-            sds((16, rows), f32),
             sds((8, D), f32),
         ],
         scratch=[pltpu.VMEM((D, D), f32)],
@@ -531,6 +517,14 @@
         moved=20 * rows * D + 6 * D * D,
         name="first_back",
     )(acc, gtwo, hat, inv, ctx, wop, order, vecs)
+
+
+def in_order(rows, order):
+    high = rows.astype(bf16)
+    rest = rows - high.astype(f32)
+    middle = rest.astype(bf16)
+    low = (rest - middle.astype(f32)).astype(bf16)
+    return dot_nt(high, order) + (dot_nt(middle, order) + dot_nt(low, order))
 
 
 LAST_ROWS = 4 * ROWS + 8
@@ -573,13 +567,7 @@
 
     @pl.when(part == 2)
     def _():
-        bias = lax.dot_general(
-            sums[...],
-            order_ref[...].astype(f32),
-            (((1,), (1,)), ((), ())),
-            precision=lax.Precision.HIGHEST,
-            preferred_element_type=f32,
-        )
+        bias = in_order(sums[...], order_ref[...])
         rows = (
             bias[0:1], bias[2:3], one_ref[2:3, :], one_ref[0:1, :],
             one_ref[1:2, :], two_ref[2:3, :], two_ref[0:1, :], two_ref[1:2, :],
@@ -652,6 +640,67 @@
     )(gres, grads, back, weights)
 
 
+def summed(refs, start, stop):
+    total = refs[0][start:stop, :].astype(f32)
+    for ref in refs[1:]:
+        total = total + ref[start:stop, :].astype(f32)
+    return total
+
+
+def spread(out_ref, total, first, stride):
+    for column in range(D // LANES):
+        out_ref[pl.ds(first + column, total.shape[0], stride=stride), :] = total[:, column * LANES : (column + 1) * LANES]
+
+
+def finish_ffn_body(*refs):
+    up_ref, down_ref = refs[6:]
+    for chunk in range(4):
+        spread(up_ref, summed(refs[:3], chunk * ROWS, (chunk + 1) * ROWS), chunk * (D // LANES), FF // LANES)
+    spread(down_ref, summed(refs[3:6], 0, 4 * ROWS), 0, D // LANES)
+
+
+def finish_last_body(*refs):
+    order_ref, out_ref, q_ref, k_ref, v_ref, vec_ref, upb_ref = refs[6:]
+    one, two = refs[:3], refs[3:6]
+    half = one[0].shape[0]
+    spread(out_ref, summed(one, 0, ROWS), 0, D // LANES)
+    middle = jnp.concatenate((summed(one, ROWS, half), summed(two, 0, 4 * ROWS - half)), axis=0)
+    ordered = in_order(middle, order_ref[...])
+    for part, ref in enumerate((q_ref, k_ref, v_ref)):
+        spread(ref, ordered[part * ROWS : (part + 1) * ROWS], 0, D // LANES)
+    small = summed(two, 4 * ROWS - half, 4 * ROWS - half + 8)
+    vec_ref[...] = small[0, :N_VEC]
+    upb_ref[...] = small[0, N_VEC : N_VEC + N_BIAS]
+
+
+def z_first(one, two):
+    return swap(one[1:3], "dp", 2), swap(two[2:4], "dp", 6)
+
+
+def z_second(one, two, got_one, got_two):
+    return swap(one[3] + got_one[1], "dp", 6), swap(two[1] + got_two[0], "dp", 2)
+
+
+def finish(body, one, two, got, last, extra, sizes, name):
+    shapes = [(size * D // LANES, LANES) for size in sizes]
+    if extra:
+        shapes = shapes + [(N_VEC,), (N_BIAS,)]
+
+    def piece(value, index):
+        return pl.BlockSpec((None, *value.shape[1:]), lambda i: (index, 0, 0))
+
+    return call(
+        body,
+        (1,),
+        [piece(one, 0), piece(got[0], 0), whole(last[0].shape), piece(two, 0), piece(got[1], 1), whole(last[1].shape)]
+        + [whole(value.shape) for value in extra],
+        [whole(shape) for shape in shapes],
+        [sds(shape, f32) for shape in shapes],
+        moved=8 * (one.shape[1] + two.shape[1]) * D,
+        name=name,
+    )(one, got[0], last[0], two, got[1], last[1], *extra)
+
+
 def gather(value):
     return lax.all_gather(value, BOTH, axis=0)
 
@@ -687,9 +736,16 @@
     return [pieces[key] for key in PIECES]
 
 
-def over_cores(keep, send):
-    rows = keep.shape[1]
-    return (keep + swap(send, "blk", 1)).reshape(2, 4, 2, rows, D)
+def over_cores(keep, received):
+    return (keep + received).reshape(2, 4, 2, keep.shape[1], D)
+
+
+def over_x(total):
+    return total[:, :, 0] + swap(total[:, :, 1], "dp", 1)
+
+
+def over_y(total):
+    return total[0] + swap(total[1], "blk", 2)
 
 
 def over_first(total):
@@ -703,14 +759,7 @@
     one, two = pair
     one = one[0] + swap(one[1], "blk", 2)
     two = two[:, 0] + swap(two[:, 1], "dp", 1)
-    return jnp.concatenate((one, two), axis=1)
-
-
-def over_z(column):
-    result = column[0].astype(f32)
-    for step in range(1, 4):
-        result = result + swap(column[step], "dp", 2 * step).astype(f32)
-    return result
+    return one, two
 
 
 def together(*values):
@@ -750,83 +799,104 @@
     inputs = tokens.reshape(row_count, D)
     other_inputs = swap(inputs, "blk", 1)
 
-    up_bias = lax.dynamic_update_slice(jnp.zeros((FF,), bf16), b_up, (device * n_bias,)).reshape(FF // D, D)
     ffn_shard = jnp.concatenate(
         (
             w_down.reshape(4 * own_rows, D),
             w_up.reshape(own_rows, 4, D).transpose(1, 0, 2).reshape(4 * own_rows, D),
-            w_out.reshape(own_rows, D),
-            jnp.pad(up_bias, ((0, 8 - FF // D), (0, 0))),
         )
     )
     ffn_pack = gather(ffn_shard)
+    up_bias = lax.dynamic_update_slice(jnp.zeros((8 * D,), bf16), b_up, (device * n_bias,)).reshape(8, D)
     small = lax.dynamic_update_slice(jnp.zeros((8 * D,), bf16), vectors, (device * n_vec,)).reshape(8, D)
     stacked = jnp.concatenate([w.reshape(own_rows, D) for w in (w_query, w_key, w_value)] + [small[0:2]])
     stacked = dot_nn(stacked, order).astype(bf16)
-    attn_shard = jnp.concatenate((stacked, small[2:]))
+    attn_shard = jnp.concatenate(
+        (stacked[: 3 * own_rows], w_out.reshape(own_rows, D), stacked[3 * own_rows :], small[2:], up_bias)
+    )
     if near:
         pieces = gather_near(attn_shard)
     else:
         attn_all = gather(attn_shard)
         attn_pack = jnp.concatenate(
-            [joined(attn_all, s * own_rows, own_rows) for s in range(3)]
-            + [jnp.sum(attn_all[:, 3 * own_rows :].reshape(GROUPS_W, -1, 8, D), axis=1)],
+            [joined(attn_all, s * own_rows, own_rows) for s in range(4)]
+            + [jnp.sum(attn_all[:, 4 * own_rows :].reshape(GROUPS_W, -1, 16, D), axis=1)],
             axis=1,
-        ).reshape(2, 2, 4, 2, 3 * ROWS + 8, D)
+        ).reshape(2, 2, 4, 2, 4 * ROWS + 16, D)
         pieces = [attn_pack[y, core, :, x] for core, y, x in PIECES]
         ffn_pack = jnp.concatenate(
-            (
-                joined(ffn_pack, 0, 4 * own_rows),
-                joined(ffn_pack, 4 * own_rows, own_rows, 4),
-                joined(ffn_pack, 8 * own_rows, own_rows),
-                jnp.sum(ffn_pack[:, 9 * own_rows :].reshape(GROUPS_W, -1, 8, D), axis=1),
-            ),
-            axis=1,
+            (joined(ffn_pack, 0, 4 * own_rows), joined(ffn_pack, 4 * own_rows, own_rows, 4)), axis=1
         )
 
-    q, k, v, attn_weights, vecs = project(me, inputs, other_inputs, pieces)
+    q, k, v, attn_weights, out_weight, vecs, up_biases = project(me, inputs, other_inputs, pieces, order)
     ctx, probs = attend(valid, q, k, v)
-    hat, inv, low, out_weight, up_biases = first_norm(ctx, inputs, ffn_pack, order, vecs)
+    hat, inv, low = first_norm(ctx, inputs, out_weight, vecs)
     act, slope, output, gtwo, gsec, sums_two = ffn_forward(
         low, hat, cotangent.reshape(row_count, D), ffn_pack, up_biases, vecs
     )
-    grad_down, gsec = together(grad_down_of(act, gsec), gsec)
-    down_sum = scatter(parted(grad_down, devices, 4 * own_rows)).astype(f32)
+    down_keep, down_send = grad_down_of(me, act, gsec)
+    down_keep, down_send = (value.reshape(GROUPS_W // 2, 4 * ROWS, D) for value in (down_keep, down_send))
+    down_keep, down_send, gsec = together(down_keep, down_send, gsec)
     up_keep, up_send, grad_up_bias, acc = ffn_backward(me, gsec, slope, low, ffn_pack)
-    gres, grad_ctx, grad_out, delta, sums_one = first_back(acc, gtwo, hat, inv, ctx, out_weight, order, vecs)
     if near:
-        up_total, grad_ctx = together(over_cores(up_keep, up_send), grad_ctx)
-    grads, give = attend_back(q, k, v, probs, grad_ctx, delta)
+        received, acc = together(swap(down_send, "blk", 1), acc)
+        down = over_cores(down_keep, received)
+    gres, grad_ctx, grad_out, sums_one = first_back(acc, gtwo, hat, inv, ctx, out_weight, order, vecs)
     if near:
-        up_pair, grads = together(over_first(up_total), grads)
+        received, grad_ctx = together(swap(up_send, "blk", 1), grad_ctx)
+        up = over_cores(up_keep, received)
+    grads, give = attend_back(q, k, v, probs, grad_ctx)
+    if near:
+        up, down, grads, give = together(over_x(up), over_y(down), grads, give)
     back = swap(give, "blk", 1)
     last_keep, last_send = grad_project(
         me, inputs, other_inputs, grads, grad_out, sums_one, sums_two, grad_up_bias, order
     )
     if near:
-        up_column = over_second(up_pair)
-        last_total, up_column, gres = together(over_cores(last_keep, last_send), up_column, gres)
+        up, down, last_keep, last_send = together(
+            over_y(up), down[:, 0] + swap(down[:, 1], "dp", 1), last_keep, last_send
+        )
+        received, gres = together(swap(last_send, "blk", 1), gres)
+        last = over_cores(last_keep, received)
     grad_inputs = grad_input_of(gres, grads, back, attn_weights)
+    outputs = (output.reshape(tokens.shape), grad_inputs.reshape(tokens.shape))
 
     if near:
-        up_sum = over_z(up_column)
-        last_sum = over_z(over_second(over_first(last_total)))
-    else:
-        up_sum = scatter(parted(every_group(up_keep, up_send), devices, own_rows, 4)).astype(f32)
-        last = every_group(last_keep, last_send)
-        tail = jnp.concatenate(
-            (
-                last[:, 4 * ROWS, :N_VEC].reshape(devices, n_vec),
-                last[:, 4 * ROWS, N_VEC : N_VEC + N_BIAS].reshape(devices, n_bias),
-            ),
-            axis=1,
+        *got, grad_inputs = together(*z_first(up, down), grad_inputs)
+        outputs = (output.reshape(tokens.shape), grad_inputs.reshape(tokens.shape))
+        *pair, got_up, got_down = together(*over_first(last), *got)
+        one, two, *ends = together(*over_second(pair), *z_second(up, down, got_up, got_down))
+        up_sum, down_sum = finish(
+            finish_ffn_body, up, down, (got_up, got_down), ends, (), (4 * ROWS, 4 * ROWS), "finish_ffn"
         )
-        tail = jnp.pad(tail, ((0, 0), (0, D - n_vec - n_bias)))[:, None, :]
-        last_sum = scatter(
-            jnp.concatenate(
-                [parted(last[:, s * ROWS : (s + 1) * ROWS], devices, own_rows) for s in range(4)] + [tail], axis=1
-            )
-        ).astype(f32)
+        *got, up_sum = together(*z_first(one, two), up_sum)
+        out_sum, query_sum, key_sum, value_sum, vec_sum, bias_sum = finish(
+            finish_last_body, one, two, got, z_second(one, two, *got), (order,), (ROWS,) * 4, "finish_last"
+        )
+        return (
+            *outputs,
+            query_sum.reshape(-1),
+            key_sum.reshape(-1),
+            value_sum.reshape(-1),
+            out_sum.reshape(-1),
+            up_sum.reshape(-1),
+            down_sum.reshape(-1),
+            bias_sum,
+            vec_sum,
+        )
+    down_sum = scatter(parted(every_group(down_keep, down_send), devices, 4 * own_rows)).astype(f32)
+    up_sum = scatter(parted(every_group(up_keep, up_send), devices, own_rows, 4)).astype(f32)
+    last = every_group(last_keep, last_send)
+    tail = jnp.concatenate(
+        (
+            last[:, 4 * ROWS, :N_VEC].reshape(devices, n_vec),
+            last[:, 4 * ROWS, N_VEC : N_VEC + N_BIAS].reshape(devices, n_bias),
+        ),
+        axis=1,
+    )
+    tail = jnp.pad(tail, ((0, 0), (0, D - n_vec - n_bias)))[:, None, :]
+    last_sum = scatter(
+        jnp.concatenate([parted(last[:, s * ROWS : (s + 1) * ROWS], devices, own_rows) for s in range(4)] + [tail], axis=1)
+    ).astype(f32)
     qkv_sum = lax.dot_general(
         last_sum[own_rows : 4 * own_rows],
         order.astype(f32),
@@ -835,8 +905,7 @@
     ).reshape(3, own_rows * D)
     small_sum = last_sum[4 * own_rows]
     return (
-        output.reshape(tokens.shape),
-        grad_inputs.reshape(tokens.shape),
+        *outputs,
         qkv_sum[0],
         qkv_sum[1],
         qkv_sum[2],

time: 328 us -> 321 us (0.979)
  waiting for transfers between devices: 89.1 us -> 81.1 us
  other arithmetic: 9.48 us -> 16.5 us
  local copies, waits for them, and re-layouts: 18.3 us -> 12.5 us
    ppermute x29 -> x32, waiting for transfers between devices: 52.9 us -> 81.1 us  [swap(): lax.ppermute(value, axis, [(source, source ^ mask) for source in range(la...]
    all_gather x1, waiting for transfers between devices: 24.4 us -> 0.01 us  [gather(): return lax.all_gather(value, BOTH, axis=0)]
    reduce_scatter x1 -> x0, waiting for transfers between devices: 11.7 us -> none  [scatter(): return lax.psum_scatter(value, BOTH, scatter_dimension=0)]
    add x4 -> x11, other arithmetic: 4.04 us -> 10.8 us  [the longest x3 6.83 us: over_cores(): return (keep + received).reshape(2, 4, 2, keep.shape[1], D)]
    pallas_call x1, Pallas kernels: 34.1 us -> 29.6 us  [ffn_forward(): call(ffn_forward_body, (rows // span, chunks), [row_spec, row_spec, row_s...]
    pallas_call x2 -> x4, Pallas kernels: 17.2 us -> 21.1 us  [the longest x1 9.8 us: grad_down_of(): call(grad_down_body, (FF // D,), [pl.BlockSpec((rows, D), lambda s, me_re...]
    ppermute x29 -> x32, starting transfers between devices: 29.1 us -> 30.6 us  [swap(): lax.ppermute(value, axis, [(source, source ^ mask) for source in range(la...]
  transfers between devices with their start and end apart: 31 -> 33, of which waited for: 12 -> 16; matrix products, arithmetic and copies ran while one was open for 5% -> 6% of each run, Pallas kernels for 26% -> 38%
where the time goes in v3:
time: 321 us; the launch traced here: 320 us
  Pallas kernels  164 us (51%)
  waiting for transfers between devices  81.1 us (25%)
  starting transfers between devices  30.6 us (10%)
  other arithmetic  16.5 us (5%)
  between operations  14.6 us (5%)
  local copies, waits for them, and re-layouts  12.5 us (4%)
    ppermute x32, waiting for transfers between devices, swap(): lax.ppermute(value, axis, [(source, source ^ mask) for source in range(la...  81.1 us
    ppermute x32, starting transfers between devices, swap(): lax.ppermute(value, axis, [(source, source ^ mask) for source in range(la...  30.6 us
    pallas_call x1, Pallas kernels, ffn_forward(): call(ffn_forward_body, (rows // span, chunks), [row_spec, row_spec, row_s...  29.6 us
    pallas_call x1, Pallas kernels, ffn_backward(): call(ffn_backward_body, (FF // D,), [whole((rows, D)), pl.BlockSpec((rows...  26.4 us
    pallas_call x1, Pallas kernels, attend_back(): call(attend_back_body, (seqs, H // 2), [spec] * 3 + [pl.BlockSpec((1, 2,...  21.9 us
    pallas_call x1, Pallas kernels, attend(): call(attend_body, (seqs, H // 2), [spec] * 3, [spec, pl.BlockSpec((1, 2,...  18.5 us
    pallas_call x1, Pallas kernels, grad_project(): call(grad_project_body, (3,), [whole((rows, D)), whole((rows, D)), pl.Blo...  12.7 us
    pallas_call x1, Pallas kernels, first_back(): call(first_back_body, (rows // step,), [row_spec, row_spec, row_spec, pl....  12.3 us
  transfers between devices with their start and end apart: 33, of which 16 were waited for; matrix products, arithmetic and copies ran while one was open for 6% of the time, Pallas kernels for 38%

profile of v3, /device:TPU:0, one launch (start us, length us, event | category | flops | bytes accessed | tf_op | source)
XLA Modules:
  0.0 320.2 jit_solution(12664573571222312033)
XLA Ops:
  12.3 5.1 %collective-permute-start.3 = (bf16[112,768]{1,0:T(8,128)(2,1)S(1)}, bf16[112,768]{1,0:T(8,128)(2,1)S(1)}, u32[]{:S(2)}, u32[]{:S(2)}) collective-permute-start(bf16[112,768]{1,0:T(8,128)(2,1)S(1)} %concatenate.13), channel_id=1, source_target_pairs={{0,6},{1,7},{2,4},{3,5},{4,2},{5,3},{6,0},{7,1},{8,14},{9,15},{10,... | collective-permute-start | bytes 516104 | tf_op jit(solution)/shard_map/ppermute | solution.py:33
  18.1 4.7 %collective-permute-done.3 = bf16[112,768]{1,0:T(8,128)(2,1)S(1)} collective-permute-done((bf16[112,768]{1,0:T(8,128)(2,1)S(1)}, bf16[112,768]{1,0:T(8,128)(2,1)S(1)}, u32[]{:S(2)}, u32[]{:S(2)}) %collective-permute-start.3) | collective-permute-done | bytes 172064 | tf_op jit(solution)/shard_map/ppermute | solution.py:33
  22.8 15.6 %collective-permute-done.2 = bf16[112,768]{1,0:T(8,128)(2,1)S(1)} collective-permute-done((bf16[112,768]{1,0:T(8,128)(2,1)S(1)}, bf16[112,768]{1,0:T(8,128)(2,1)S(1)}, u32[]{:S(2)}, u32[]{:S(2)}) %collective-permute-start.2) | collective-permute-done | bytes 172064 | tf_op jit(solution)/shard_map/ppermute | solution.py:33
  38.5 1.6 collective-permute-start.5
  40.1 1.5 collective-permute-start.4
  41.6 17.7 %collective-permute-done.5.refs_2_ = bf16[4,112,768]{2,1,0:T(8,128)(2,1)S(1)} collective-permute-done((bf16[4,112,768]{2,1,0:T(8,128)(2,1)S(1)}, bf16[4,112,768]{2,1,0:T(8,128)(2,1)S(1)}, u32[]{:S(2)}, u32[]{:S(2)}) %collective-permute-start.5) | collective-permute-done | bytes 688160 | tf_op jit(solution)/shard_map/ppermute | solution.py:33
  59.2 1.6 collective-permute-start.6
  60.8 6.0 %collective-permute-done.4.refs_1_ = bf16[4,112,768]{2,1,0:T(8,128)(2,1)S(1)} collective-permute-done((bf16[4,112,768]{2,1,0:T(8,128)(2,1)S(1)}, bf16[4,112,768]{2,1,0:T(8,128)(2,1)S(1)}, u32[]{:S(2)}, u32[]{:S(2)}) %collective-permute-start.4) | collective-permute-done | bytes 688160 | tf_op jit(solution)/shard_map/ppermute | solution.py:33
  67.9 4.2 %collective-permute-done.6 = bf16[4,56,768]{2,1,0:T(8,128)(2,1)S(1)} collective-permute-done((bf16[4,56,768]{2,1,0:T(8,128)(2,1)S(1)}, bf16[4,56,768]{2,1,0:T(8,128)(2,1)S(1)}, u32[]{:S(2)}, u32[]{:S(2)}) %collective-permute-start.6) | collective-permute-done | bytes 344096 | tf_op jit(solution)/shard_map/ppermute | solution.py:33
  72.1 2.0 collective-permute-done.7
  75.0 1.3 fusion.refs_8_.order_ref.refs_6_
  76.3 1.2 collective-permute-done.11.refs_7_
  77.5 12.0 %project.1 = (bf16[1024,768]{1,0:T(8,128)(2,1)}, bf16[1024,768]{1,0:T(8,128)(2,1)}, bf16[1024,768]{1,0:T(8,128)(2,1)}, bf16[3,768,768]{2,1,0:T(8,128)(2,1)}, bf1...) custom-call(s32[1]{0:T(128)} %bitcast.me_ref, bf16[1024,768]{1,0:T(8,128)(2,1)} %bitcast.111, ...), custom_call_target="tpu_custom_call" | custom-call | flops 3623878656 | bytes 14942208 | tf_op jit(solution)/shard_map/project/pallas_call | solution.py:113
  89.6 18.5 %attend.1 = (bf16[1024,768]{1,0:T(8,128)(2,1)}, bf16[2,12,512,512]{3,2,1,0:T(8,128)(2,1)}) custom-call(s32[2,2]{1,0:T(2,128)} %pad_add_fusion.valid_ref, bf16[1024,768]{1,0:T(8,128)(2,1)} %get-tuple-element.81.q_ref, bf16[1024,768]{1,0:T(8,128)(2,1)} %get-tuple-element.82.k_ref, bf16[1024,768]{1,0:T(8,128)(2,1)} %get-tuple-element.83.v_ref), custom_call_target="tpu_custom_call" | custom-call | flops 6442450944 | bytes 18874368 | tf_op jit(solution)/shard_map/attend/pallas_call | solution.py:152
  108.0 5.8 %first_norm.1 = (f32[1024,768]{1,0:T(8,128)}, f32[1024,128]{1,0:T(8,128)}, bf16[1024,768]{1,0:T(8,128)(2,1)}) custom-call(bf16[1024,768]{1,0:T(8,128)(2,1)} %get-tuple-element.84.ctx_ref, bf16[1024,768]{1,0:T(8,128)(2,1)} %bitcast.112, bf16[768,768]{1,0:T(8,128)(2,1)} %get-tuple-element.85.wop_ref, f32[8,768]{1,0:T(8,128)} %get-tuple-element.86.vec_ref), custom_call_target="tpu_custom_call" | custom-call | flops 1207959552 | bytes 9437184 | tf_op jit(solution)/shard_map/first_norm/pallas_call | solution.py:235
  113.8 29.6 %ffn_forward.1 = (bf16[1024,3072]{1,0:T(8,128)(2,1)}, bf16[1024,3072]{1,0:T(8,128)(2,1)}, bf16[1024,768]{1,0:T(8,128)(2,1)}, f32[1024,768]{1,0:T(8,128)}, bf16[1024,768]{1,0:T(8,128)(2,1)}, /*index=5*/f32[8,768]{1,0:T(8,128)}) custom-call(bf16[1024,768]{1,0:T(8,128)(2,1)} %get-tuple-element.87.low_ref, f32[1024,768]{1,0:T(8,128)} %get-tuple-element.88.hat_ref, ...), custom_call_target="tpu_custom_call" | custom-call | flops 9663676416 | bytes 29884416 | tf_op jit(solution)/shard_map/ffn_forward/pallas_call | solution.py:324
  143.5 9.8 %grad_down.1 = (bf16[2,8,96,768]{3,2,1,0:T(8,128)(2,1)}, bf16[2,8,96,768]{3,2,1,0:T(8,128)(2,1)}) custom-call(s32[1]{0:T(128)} %bitcast.me_ref, bf16[1024,3072]{1,0:T(8,128)(2,1)} %get-tuple-element.91.act_ref, bf16[1024,768]{1,0:T(8,128)(2,1)} %get-tuple-element.95.gsec_ref), custom_call_target="tpu_custom_call" | custom-call | flops 4831838208 | bytes 12582912 | tf_op jit(solution)/shard_map/grad_down/pallas_call | solution.py:371
  153.4 26.4 %ffn_backward.1 = (bf16[16,96,768]{2,1,0:T(8,128)(2,1)}, bf16[16,96,768]{2,1,0:T(8,128)(2,1)}, f32[4,1,768]{2,1,0:T(1,128)}, f32[1024,768]{1,0:T(8,128)}) custom-call(s32[1]{0:T(128)} %bitcast.me_ref, bf16[1024,768]{1,0:T(8,128)(2,1)} %get-tuple-element.95.gsec_ref, bf16[1024,3072]{1,0:T(8,128)(2,1)} %get-tuple-element.96.slope_ref, ...), custom_call_target="tpu_custom_call" | custom-call | flops 14495514624 | bytes 26738688 | tf_op jit(solution)/shard_map/ffn_backward/pallas_call | solution.py:431
  180.2 3.1 add.96
  183.3 1.1 fusion.18
  185.5 12.3 %first_back.1 = (f32[1024,768]{1,0:T(8,128)}, bf16[1024,768]{1,0:T(8,128)(2,1)}, bf16[32,24,768]{2,1,0:T(8,128)(2,1)}, f32[8,768]{1,0:T(8,128)}) custom-call(f32[1024,768]{1,0:T(8,128)} %get-tuple-element.101.acc_ref, f32[1024,768]{1,0:T(8,128)} %get-tuple-element.102.gtwo_ref, f32[1024,768]{1,0:T(8,128)} %get-tuple-element.88.hat_ref, ...), custom_call_target="tpu_custom_call" | custom-call | flops 2415919104 | bytes 19267584 | tf_op jit(solution)/shard_map/first_back/pallas_call | solution.py:490
  197.9 1.4 copy-done.5
  199.3 3.1 add.94
  202.4 1.6 collective-permute-start.14
  204.4 21.9 %attend_back.1 = (bf16[3,1024,768]{2,1,0:T(8,128)(2,1)}, bf16[2,1024,384]{2,1,0:T(8,128)(2,1)}) custom-call(bf16[1024,768]{1,0:T(8,128)(2,1)} %get-tuple-element.81.q_ref, bf16[1024,768]{1,0:T(8,128)(2,1)} %get-tuple-element.82.k_ref, bf16[1024,768]{1,0:T(8,128)(2,1)} %get-tuple-element.83.v_ref, bf16[2,12,512,512]{3,2,1,0:T(8,128)(2,1)} %get-tuple-element.108.p_ref, ...), custom_call_target="tpu_custom_call" | custom-call | flops 12884901888 | bytes 23592960 | tf_op jit(solution)/shard_map/attend_back/pallas_call | solution.py:197
  226.4 4.2 %collective-permute-done.14 = bf16[2,4,96,768]{3,2,1,0:T(8,128)(2,1)} collective-permute-done((bf16[2,4,96,768]{3,2,1,0:T(8,128)(2,1)S(1)}, bf16[2,4,96,768]{3,2,1,0:T(8,128)(2,1)}, u32[]{:S(2)}, u32[]{:S(2)}) %collective-permute-start.14) | collective-permute-done | bytes 1179680 | tf_op jit(solution)/shard_map/ppermute | solution.py:33
  230.6 1.4 fusion.2
  232.0 1.4 copy_add_fusion
  233.5 1.5 collective-permute-start.17
  236.4 12.7 %grad_project.1 = (bf16[16,104,768]{2,1,0:T(8,128)(2,1)}, bf16[16,104,768]{2,1,0:T(8,128)(2,1)}) custom-call(s32[1]{0:T(128)} %bitcast.me_ref, bf16[1024,768]{1,0:T(8,128)(2,1)} %bitcast.113, bf16[1024,768]{1,0:T(8,128)(2,1)} %collective-permute-done.xp_ref, bf16[3,1024,768]{2,1,0:T(8,128)(2,1)} %get-tuple-element.114.grad_ref.grads_ref, ...), custom_call_target="tpu_custom_call" | custom-call | flops 3623878656 | bytes 14942208 | tf_op jit(solution)/shard_map/grad_project/pallas_call | solution.py:587
  251.0 4.5 %collective-permute-done.20 = bf16[16,104,768]{2,1,0:T(8,128)(2,1)S(1)} collective-permute-done((bf16[16,104,768]{2,1,0:T(8,128)(2,1)}, bf16[16,104,768]{2,1,0:T(8,128)(2,1)S(1)}, u32[]{:S(2)}, u32[]{:S(2)}) %collective-permute-start.20) | collective-permute-done | bytes 2555936 | tf_op jit(solution)/shard_map/ppermute | solution.py:33
  260.6 2.6 collective-permute-start.19
  263.2 9.6 %grad_input.1 = f32[1024,768]{1,0:T(8,128)} custom-call(f32[1024,768]{1,0:T(8,128)} %get-tuple-element.125.gres_ref, bf16[3,1024,768]{2,1,0:T(8,128)(2,1)} %get-tuple-element.114.grad_ref.grads_ref, bf16[2,1024,384]{2,1,0:T(8,128)(2,1)} %collective-permute-done.21.back_ref, bf16[3,768,768]{2,1,0:T(8,128)(2,1)} %get-tuple-element.127.w_ref), custom_call_target="tpu_custom_call" | custom-call | flops 3623878656 | bytes 16121856 | tf_op jit(solution)/shard_map/grad_input/pallas_call | solution.py:626
  272.9 4.8 %collective-permute-done.18.refs_1_ = bf16[2,96,768]{2,1,0:T(8,128)(2,1)} collective-permute-done((bf16[2,96,768]{2,1,0:T(8,128)(2,1)}, bf16[2,96,768]{2,1,0:T(8,128)(2,1)}, u32[]{:S(2)}, u32[]{:S(2)}) %collective-permute-start.18) | collective-permute-done | bytes 294944 | tf_op jit(solution)/shard_map/ppermute | solution.py:33
  277.7 1.1 fusion.6
  278.8 1.2 fusion.5
  280.0 1.6 collective-permute-start.25
  282.7 1.5 collective-permute-start.24
  284.8 1.5 collective-permute-start.26
  286.3 2.8 collective-permute-done.25
  289.1 3.4 %collective-permute-done.24 = bf16[4,56,768]{2,1,0:T(8,128)(2,1)S(1)} collective-permute-done((bf16[4,56,768]{2,1,0:T(8,128)(2,1)S(1)}, bf16[4,56,768]{2,1,0:T(8,128)(2,1)S(1)}, u32[]{:S(2)}, u32[]{:S(2)}) %collective-permute-start.24) | collective-permute-done | bytes 344096 | tf_op jit(solution)/shard_map/ppermute | solution.py:33
  292.7 1.8 collective-permute-start.28
  294.5 1.3 collective-permute-start.29
  295.8 2.1 finish_ffn.1
  297.9 3.6 %collective-permute-done.29.refs_4_ = bf16[2,48,768]{2,1,0:T(8,128)(2,1)S(1)} collective-permute-done((bf16[2,48,768]{2,1,0:T(8,128)(2,1)S(1)}, bf16[2,48,768]{2,1,0:T(8,128)(2,1)S(1)}, u32[]{:S(2)}, u32[]{:S(2)}) %collective-permute-start.29) | collective-permute-done | bytes 147488 | tf_op jit(solution)/shard_map/ppermute | solution.py:33
  301.6 1.7 collective-permute-start.30
  303.4 5.3 %collective-permute-done.31.refs_5_ = bf16[48,768]{1,0:T(8,128)(2,1)S(1)} collective-permute-done((bf16[48,768]{1,0:T(8,128)(2,1)S(1)}, bf16[48,768]{1,0:T(8,128)(2,1)S(1)}, u32[]{:S(2)}, u32[]{:S(2)}) %collective-permute-start.31) | collective-permute-done | bytes 73760 | tf_op jit(solution)/shard_map/ppermute | solution.py:33
  310.0 3.4 %finish_last.1 = (f32[144,128]{1,0:T(8,128)}, f32[144,128]{1,0:T(8,128)}, f32[144,128]{1,0:T(8,128)}, f32[144,128]{1,0:T(8,128)}, f32[192]{0:T(256)}, /*index=5*/f32[96]{0:T(128)}) custom-call(bf16[4,56,768]{2,1,0:T(8,128)(2,1)} %copy-done.3, bf16[2,56,768]{2,1,0:T(8,128)(2,1)} %copy-done.9, bf16[56,768]{1,0:T(8,128)(2,1)} %copy-done.16, ...), custom_call_target="tpu_custom_call" | custom-call | bytes 638976 | tf_op jit(solution)/shard_map/finish_last/pallas_call | solution.py:692
  (149 shorter events, 21.6 us)
Async XLA Ops:
  7.2 3.9 %copy-start.20 = (bf16[18432]{0:T(1024)(128)(2,1)S(1)}, bf16[18432]{0:T(1024)(128)(2,1)}, u32[]{:S(2)}) copy-start(bf16[18432]{0:T(1024)(128)(2,1)} %param.18) | copy-start | bytes 110596
  7.2 106.6 %all-gather.3.cloned.1.call-start = ((), (), s32[]{:S(2)}) async-start(), calls=%async_computation | async-start | bytes 9732096 | tf_op jit(solution)/shard_map/all_gather | solution.py:705
  8.3 3.9 %copy-start.21 = (bf16[18432]{0:T(1024)(128)(2,1)S(1)}, bf16[18432]{0:T(1024)(128)(2,1)}, u32[]{:S(2)}) copy-start(bf16[18432]{0:T(1024)(128)(2,1)} %param.19) | copy-start | bytes 110596
  12.3 10.5 %collective-permute-start.3 = (bf16[112,768]{1,0:T(8,128)(2,1)S(1)}, bf16[112,768]{1,0:T(8,128)(2,1)S(1)}, u32[]{:S(2)}, u32[]{:S(2)}) collective-permute-start(bf16[112,768]{1,0:T(8,128)(2,1)S(1)} %concatenate.13), channel_id=1, source_target_pairs={{0,6},{1,7},{2,4},{3,5},{4,2},{5,3},{6,0},{7,1},{8,14},{9,15},{10,... | collective-permute-start | bytes 516104 | tf_op jit(solution)/shard_map/ppermute | solution.py:33
  17.5 20.9 %collective-permute-start.2 = (bf16[112,768]{1,0:T(8,128)(2,1)S(1)}, bf16[112,768]{1,0:T(8,128)(2,1)S(1)}, u32[]{:S(2)}, u32[]{:S(2)}) collective-permute-start(bf16[112,768]{1,0:T(8,128)(2,1)S(1)} %concatenate.13), channel_id=1, source_target_pairs={{0,4},{1,5},{2,6},{3,7},{4,0},{5,1},{6,2},{7,3},{8,12},{9,13},{10,... | collective-permute-start | bytes 516104 | tf_op jit(solution)/shard_map/ppermute | solution.py:33
  17.5 20.9 %collective-permute-start.1 = (bf16[112,768]{1,0:T(8,128)(2,1)S(1)}, bf16[112,768]{1,0:T(8,128)(2,1)S(1)}, u32[]{:S(2)}, u32[]{:S(2)}) collective-permute-start(bf16[112,768]{1,0:T(8,128)(2,1)S(1)} %concatenate.13), channel_id=1, source_target_pairs={{0,2},{1,3},{2,0},{3,1},{4,6},{5,7},{6,4},{7,5},{8,10},{9,11},{10,... | collective-permute-start | bytes 516104 | tf_op jit(solution)/shard_map/ppermute | solution.py:33
  38.5 37.8 %copy-start.7 = (bf16[4,112,768]{2,1,0:T(8,128)(2,1)}, bf16[4,112,768]{2,1,0:T(8,128)(2,1)S(1)}, u32[]{:S(2)}) copy-start(bf16[4,112,768]{2,1,0:T(8,128)(2,1)S(1)} %pad_maximum_fusion.refs_0_) | copy-start | bytes 2064388
  38.5 35.8 %copy-start.22 = (s32[2,2]{1,0:T(2,128)S(1)}, s32[2,2]{1,0:T(2,128)}, u32[]{:S(2)}) copy-start(s32[2,2]{1,0:T(2,128)} %param.14) | copy-start | bytes 52
  38.5 20.7 %collective-permute-start.5 = (bf16[4,112,768]{2,1,0:T(8,128)(2,1)S(1)}, bf16[4,112,768]{2,1,0:T(8,128)(2,1)S(1)}, u32[]{:S(2)}, u32[]{:S(2)}) collective-permute-start(bf16[4,112,768]{2,1,0:T(8,128)(2,1)S(1)} %pad_maximum_fusion.refs_0_), channel_id=1, source_target_pairs={{0,16},{8,24},{16,0},{24,8},{1,17},{9,25},{17,1},{25,9},{2,18},{10... | collective-permute-start | bytes 2064392 | tf_op jit(solution)/shard_map/ppermute | solution.py:33
  40.1 26.7 %collective-permute-start.4 = (bf16[4,112,768]{2,1,0:T(8,128)(2,1)S(1)}, bf16[4,112,768]{2,1,0:T(8,128)(2,1)S(1)}, u32[]{:S(2)}, u32[]{:S(2)}) collective-permute-start(bf16[4,112,768]{2,1,0:T(8,128)(2,1)S(1)} %pad_maximum_fusion.refs_0_), channel_id=1, source_target_pairs={{0,1},{1,0},{2,3},{3,2},{4,5},{5,4},{6,7},{7,6},{8,9},{9,8},{10,11... | collective-permute-start | bytes 2064392 | tf_op jit(solution)/shard_map/ppermute | solution.py:33
  41.6 34.8 %collective-permute-start = (bf16[1024,768]{1,0:T(8,128)(2,1)}, bf16[1024,768]{1,0:T(8,128)(2,1)}, u32[]{:S(2)}, u32[]{:S(2)}) collective-permute-start(bf16[1024,768]{1,0:T(8,128)(2,1)} %bitcast.110), channel_id=1, source_target_pairs={{0,8},{8,0},{16,24},{24,16},{1,9},{9,1},{17,25},{25,17},{2,10},{10... | collective-permute-start | bytes 4718600 | tf_op jit(solution)/shard_map/ppermute | solution.py:33
  59.2 17.1 %copy-start.11 = (bf16[4,112,768]{2,1,0:T(8,128)(2,1)}, bf16[4,112,768]{2,1,0:T(8,128)(2,1)S(1)}, u32[]{:S(2)}) copy-start(bf16[4,112,768]{2,1,0:T(8,128)(2,1)S(1)} %collective-permute-done.5.refs_2_) | copy-start | bytes 2064388
  59.2 12.8 %collective-permute-start.6 = (bf16[4,56,768]{2,1,0:T(8,128)(2,1)S(1)}, bf16[4,56,768]{2,1,0:T(8,128)(2,1)S(1)}, u32[]{:S(2)}, u32[]{:S(2)}) collective-permute-start(bf16[4,56,768]{2,1,0:T(8,128)(2,1)S(1)} %slice.180), channel_id=1, source_target_pairs={{0,1},{1,0},{2,3},{3,2},{4,5},{5,4},{6,7},{7,6},{8,9},{9,8},{10,11... | collective-permute-start | bytes 1032200 | tf_op jit(solution)/shard_map/ppermute | solution.py:33
  66.8 9.5 %copy-start.12 = (bf16[4,112,768]{2,1,0:T(8,128)(2,1)}, bf16[4,112,768]{2,1,0:T(8,128)(2,1)S(1)}, u32[]{:S(2)}) copy-start(bf16[4,112,768]{2,1,0:T(8,128)(2,1)S(1)} %collective-permute-done.4.refs_1_) | copy-start | bytes 2064388
  66.8 7.3 %collective-permute-start.7 = (bf16[4,56,768]{2,1,0:T(8,128)(2,1)S(1)}, bf16[4,56,768]{2,1,0:T(8,128)(2,1)S(1)}, u32[]{:S(2)}, u32[]{:S(2)}) collective-permute-start(bf16[4,56,768]{2,1,0:T(8,128)(2,1)S(1)} %slice.181), channel_id=1, source_target_pairs={{0,16},{8,24},{16,0},{24,8},{1,17},{9,25},{17,1},{25,9},{2,18},{10... | collective-permute-start | bytes 1032200 | tf_op jit(solution)/shard_map/ppermute | solution.py:33
  67.4 8.9 %collective-permute-start.8 = (bf16[4,112,768]{2,1,0:T(8,128)(2,1)S(1)}, bf16[4,112,768]{2,1,0:T(8,128)(2,1)S(1)}, u32[]{:S(2)}, u32[]{:S(2)}) collective-permute-start(bf16[4,112,768]{2,1,0:T(8,128)(2,1)S(1)} %pad_maximum_fusion.refs_0_), channel_id=1, source_target_pairs={{0,8},{8,0},{16,24},{24,16},{1,9},{9,1},{17,25},{25,17},{2,10},{10... | collective-permute-start | bytes 2064392 | tf_op jit(solution)/shard_map/ppermute | solution.py:33
  67.4 8.9 %collective-permute-start.10 = (bf16[4,112,768]{2,1,0:T(8,128)(2,1)S(1)}, bf16[4,112,768]{2,1,0:T(8,128)(2,1)}, u32[]{:S(2)}, u32[]{:S(2)}) collective-permute-start(bf16[4,112,768]{2,1,0:T(8,128)(2,1)S(1)} %collective-permute-done.5.refs_2_), channel_id=1, source_target_pairs={{0,8},{8,0},{16,24},{24,16},{1,9},{9,1},{17,25},{25,17},{2,10},{10... | collective-permute-start | bytes 2064392 | tf_op jit(solution)/shard_map/ppermute | solution.py:33
  72.1 4.3 %collective-permute-start.9 = (bf16[4,112,768]{2,1,0:T(8,128)(2,1)S(1)}, bf16[4,112,768]{2,1,0:T(8,128)(2,1)}, u32[]{:S(2)}, u32[]{:S(2)}) collective-permute-start(bf16[4,112,768]{2,1,0:T(8,128)(2,1)S(1)} %collective-permute-done.4.refs_1_), channel_id=1, source_target_pairs={{0,8},{8,0},{16,24},{24,16},{1,9},{9,1},{17,25},{25,17},{2,10},{10... | collective-permute-start | bytes 2064392 | tf_op jit(solution)/shard_map/ppermute | solution.py:33
  74.2 3.3 %collective-permute-start.11 = (bf16[4,112,768]{2,1,0:T(8,128)(2,1)S(1)}, bf16[4,112,768]{2,1,0:T(8,128)(2,1)}, u32[]{:S(2)}, u32[]{:S(2)}) collective-permute-start(bf16[4,112,768]{2,1,0:T(8,128)(2,1)S(1)} %constant_dynamic-update-slice_fusion.refs_3_), channel_id=1, source_target_pairs={{0,8},{8,0},{16,24},{24,16},{1,9},{9,1},{17,25},{25,17},{2,10},{10... | collective-permute-start | bytes 2064392 | tf_op jit(solution)/shard_map/ppermute | solution.py:33
  153.3 26.9 %collective-permute-start.13 = (bf16[16,96,768]{2,1,0:T(8,128)(2,1)}, bf16[16,96,768]{2,1,0:T(8,128)(2,1)}, u32[]{:S(2)}, u32[]{:S(2)}) collective-permute-start(bf16[16,96,768]{2,1,0:T(8,128)(2,1)} %bitcast.108), channel_id=1, source_target_pairs={{0,8},{8,0},{16,24},{24,16},{1,9},{9,1},{17,25},{25,17},{2,10},{10... | collective-permute-start | bytes 7077896 | tf_op jit(solution)/shard_map/ppermute | solution.py:33
  179.8 18.1 %collective-permute-start.12 = (bf16[16,96,768]{2,1,0:T(8,128)(2,1)}, bf16[16,96,768]{2,1,0:T(8,128)(2,1)S(1)}, u32[]{:S(2)}, u32[]{:S(2)}) collective-permute-start(bf16[16,96,768]{2,1,0:T(8,128)(2,1)} %get-tuple-element.98), channel_id=1, source_target_pairs={{0,8},{8,0},{16,24},{24,16},{1,9},{9,1},{17,25},{25,17},{2,10},{10... | collective-permute-start | bytes 7077896 | tf_op jit(solution)/shard_map/ppermute | solution.py:33
  202.4 28.2 %collective-permute-start.14 = (bf16[2,4,96,768]{3,2,1,0:T(8,128)(2,1)S(1)}, bf16[2,4,96,768]{3,2,1,0:T(8,128)(2,1)}, u32[]{:S(2)}, u32[]{:S(2)}) collective-permute-start(bf16[2,4,96,768]{3,2,1,0:T(8,128)(2,1)S(1)} %slice_bitcast_fusion), channel_id=1, source_target_pairs={{0,1},{1,0},{2,3},{3,2},{4,5},{5,4},{6,7},{7,6},{8,9},{9,8},{10,11... | collective-permute-start | bytes 3538952 | tf_op jit(solution)/shard_map/ppermute | solution.py:33
  204.0 28.0 %collective-permute-start.15 = (bf16[4,2,96,768]{3,2,0,1:T(8,128)(2,1)}, bf16[4,2,96,768]{3,2,0,1:T(8,128)(2,1)}, u32[]{:S(2)}, u32[]{:S(2)}) collective-permute-start(bf16[4,2,96,768]{3,2,0,1:T(8,128)(2,1)} %copy.38), channel_id=1, source_target_pairs={{0,16},{8,24},{16,0},{24,8},{1,17},{9,25},{17,1},{25,9},{2,18},{10... | collective-permute-start | bytes 3538952 | tf_op jit(solution)/shard_map/ppermute | solution.py:33
  226.4 5.6 %copy-start = (bf16[8,96,768]{2,1,0:T(8,128)(2,1)S(1)}, bf16[8,96,768]{2,1,0:T(8,128)(2,1)}, u32[]{:S(2)}) copy-start(bf16[8,96,768]{2,1,0:T(8,128)(2,1)} %get-tuple-element.184) | copy-start | bytes 3538948
  233.5 15.7 %collective-permute-start.17 = (bf16[4,96,768]{2,1,0:T(8,128)(2,1)S(1)}, bf16[4,96,768]{2,1,0:T(8,128)(2,1)S(1)}, u32[]{:S(2)}, u32[]{:S(2)}) collective-permute-start(bf16[4,96,768]{2,1,0:T(8,128)(2,1)S(1)} %slice_bitcast_fusion.4), channel_id=1, source_target_pairs={{0,1},{1,0},{2,3},{3,2},{4,5},{5,4},{6,7},{7,6},{8,9},{9,8},{10,11... | collective-permute-start | bytes 1769480 | tf_op jit(solution)/shard_map/ppermute | solution.py:33
  235.9 14.4 %collective-permute-start.16 = (bf16[4,96,768]{2,1,0:T(8,128)(2,1)}, bf16[4,96,768]{2,1,0:T(8,128)(2,1)S(1)}, u32[]{:S(2)}, u32[]{:S(2)}) collective-permute-start(bf16[4,96,768]{2,1,0:T(8,128)(2,1)} %slice_bitcast_fusion.5), channel_id=1, source_target_pairs={{0,16},{8,24},{16,0},{24,8},{1,17},{9,25},{17,1},{25,9},{2,18},{10... | collective-permute-start | bytes 1769480 | tf_op jit(solution)/shard_map/ppermute | solution.py:33
  249.2 6.3 %copy-start.4 = (bf16[16,104,768]{2,1,0:T(8,128)(2,1)S(1)}, bf16[16,104,768]{2,1,0:T(8,128)(2,1)}, u32[]{:S(2)}) copy-start(bf16[16,104,768]{2,1,0:T(8,128)(2,1)} %get-tuple-element.129) | copy-start | bytes 7667716
  249.2 34.9 %copy-start.1 = (bf16[4,96,768]{2,1,0:T(8,128)(2,1)}, bf16[4,96,768]{2,1,0:T(8,128)(2,1)S(1)}, u32[]{:S(2)}) copy-start(bf16[4,96,768]{2,1,0:T(8,128)(2,1)S(1)} %bitcast_add_fusion.refs_3_) | copy-start | bytes 1769476
  250.4 8.8 %copy-start.2 = (bf16[4,96,768]{2,1,0:T(8,128)(2,1)}, bf16[4,96,768]{2,1,0:T(8,128)(2,1)S(1)}, u32[]{:S(2)}) copy-start(bf16[4,96,768]{2,1,0:T(8,128)(2,1)S(1)} %bitcast_add_fusion.1.refs_0_) | copy-start | bytes 1769476
  250.4 5.1 %collective-permute-start.20 = (bf16[16,104,768]{2,1,0:T(8,128)(2,1)}, bf16[16,104,768]{2,1,0:T(8,128)(2,1)S(1)}, u32[]{:S(2)}, u32[]{:S(2)}) collective-permute-start(bf16[16,104,768]{2,1,0:T(8,128)(2,1)} %get-tuple-element.123), channel_id=1, source_target_pairs={{0,8},{8,0},{16,24},{24,16},{1,9},{9,1},{17,25},{25,17},{2,10},{10... | collective-permute-start | bytes 7667720 | tf_op jit(solution)/shard_map/ppermute | solution.py:33
  250.5 12.8 %collective-permute-start.21 = (bf16[2,1024,384]{2,1,0:T(8,128)(2,1)}, bf16[2,1024,384]{2,1,0:T(8,128)(2,1)}, u32[]{:S(2)}, u32[]{:S(2)}) collective-permute-start(bf16[2,1024,384]{2,1,0:T(8,128)(2,1)} %get-tuple-element.126), channel_id=1, source_target_pairs={{0,8},{8,0},{16,24},{24,16},{1,9},{9,1},{17,25},{25,17},{2,10},{10... | collective-permute-start | bytes 4718600 | tf_op jit(solution)/shard_map/ppermute | solution.py:33
  257.2 20.5 %collective-permute-start.23 = (bf16[4,2,48,768]{3,2,0,1:T(8,128)(2,1)}, bf16[4,2,48,768]{3,2,0,1:T(8,128)(2,1)}, u32[]{:S(2)}, u32[]{:S(2)}) collective-permute-start(bf16[4,2,48,768]{3,2,0,1:T(8,128)(2,1)} %bitcast.88), channel_id=1, source_target_pairs={{0,16},{8,24},{16,0},{24,8},{1,17},{9,25},{17,1},{25,9},{2,18},{10... | collective-permute-start | bytes 1769480 | tf_op jit(solution)/shard_map/ppermute | solution.py:33
  258.7 20.1 %collective-permute-start.22 = (bf16[2,4,56,768]{3,2,1,0:T(8,128)(2,1)}, bf16[2,4,56,768]{3,2,1,0:T(8,128)(2,1)}, u32[]{:S(2)}, u32[]{:S(2)}) collective-permute-start(bf16[2,4,56,768]{3,2,1,0:T(8,128)(2,1)} %slice_bitcast_fusion.2), channel_id=1, source_target_pairs={{0,1},{1,0},{2,3},{3,2},{4,5},{5,4},{6,7},{7,6},{8,9},{9,8},{10,11... | collective-permute-start | bytes 2064392 | tf_op jit(solution)/shard_map/ppermute | solution.py:33
  260.6 12.2 %collective-permute-start.19 = (bf16[2,96,768]{2,1,0:T(8,128)(2,1)}, bf16[2,96,768]{2,1,0:T(8,128)(2,1)S(1)}, u32[]{:S(2)}, u32[]{:S(2)}) collective-permute-start(bf16[2,96,768]{2,1,0:T(8,128)(2,1)} %slice.157), channel_id=1, source_target_pairs={{0,6},{1,7},{2,4},{3,5},{4,2},{5,3},{6,0},{7,1},{8,14},{9,15},{10,... | collective-permute-start | bytes 884744 | tf_op jit(solution)/shard_map/ppermute | solution.py:33
  263.2 14.4 %collective-permute-start.18 = (bf16[2,96,768]{2,1,0:T(8,128)(2,1)}, bf16[2,96,768]{2,1,0:T(8,128)(2,1)}, u32[]{:S(2)}, u32[]{:S(2)}) collective-permute-start(bf16[2,96,768]{2,1,0:T(8,128)(2,1)} %slice.156), channel_id=1, source_target_pairs={{0,2},{1,3},{2,0},{3,1},{4,6},{5,7},{6,4},{7,5},{8,10},{9,11},{10,... | collective-permute-start | bytes 884744 | tf_op jit(solution)/shard_map/ppermute | solution.py:33
  272.9 11.3 %copy-start.8 = (bf16[2,96,768]{2,1,0:T(8,128)(2,1)}, bf16[2,96,768]{2,1,0:T(8,128)(2,1)S(1)}, u32[]{:S(2)}) copy-start(bf16[2,96,768]{2,1,0:T(8,128)(2,1)S(1)} %collective-permute-done.19.refs_4_) | copy-start | bytes 884740
  280.0 9.0 %collective-permute-start.25 = (bf16[4,48,768]{2,1,0:T(8,128)(2,1)S(1)}, bf16[4,48,768]{2,1,0:T(8,128)(2,1)S(1)}, u32[]{:S(2)}, u32[]{:S(2)}) collective-permute-start(bf16[4,48,768]{2,1,0:T(8,128)(2,1)S(1)} %slice_bitcast_fusion.7), channel_id=1, source_target_pairs={{0,1},{1,0},{2,3},{3,2},{4,5},{5,4},{6,7},{7,6},{8,9},{9,8},{10,11... | collective-permute-start | bytes 884744 | tf_op jit(solution)/shard_map/ppermute | solution.py:33
  282.7 9.8 %collective-permute-start.24 = (bf16[4,56,768]{2,1,0:T(8,128)(2,1)S(1)}, bf16[4,56,768]{2,1,0:T(8,128)(2,1)S(1)}, u32[]{:S(2)}, u32[]{:S(2)}) collective-permute-start(bf16[4,56,768]{2,1,0:T(8,128)(2,1)S(1)} %slice_bitcast_fusion.6), channel_id=1, source_target_pairs={{0,16},{8,24},{16,0},{24,8},{1,17},{9,25},{17,1},{25,9},{2,18},{10... | collective-permute-start | bytes 1032200 | tf_op jit(solution)/shard_map/ppermute | solution.py:33
  284.2 8.3 %collective-permute-start.27 = (bf16[96,768]{1,0:T(8,128)(2,1)S(1)}, bf16[96,768]{1,0:T(8,128)(2,1)S(1)}, u32[]{:S(2)}, u32[]{:S(2)}) collective-permute-start(bf16[96,768]{1,0:T(8,128)(2,1)S(1)} %add_bitcast_fusion), channel_id=1, source_target_pairs={{0,2},{1,3},{2,0},{3,1},{4,6},{5,7},{6,4},{7,5},{8,10},{9,11},{10,... | collective-permute-start | bytes 442376 | tf_op jit(solution)/shard_map/ppermute | solution.py:33
  284.8 7.8 %collective-permute-start.26 = (bf16[96,768]{1,0:T(8,128)(2,1)S(1)}, bf16[96,768]{1,0:T(8,128)(2,1)S(1)}, u32[]{:S(2)}, u32[]{:S(2)}) collective-permute-start(bf16[96,768]{1,0:T(8,128)(2,1)S(1)} %add_bitcast_fusion.1), channel_id=1, source_target_pairs={{0,6},{1,7},{2,4},{3,5},{4,2},{5,3},{6,0},{7,1},{8,14},{9,15},{10,... | collective-permute-start | bytes 442376 | tf_op jit(solution)/shard_map/ppermute | solution.py:33
  289.1 14.3 %copy-start.6 = (bf16[4,48,768]{2,1,0:T(8,128)(2,1)}, bf16[4,48,768]{2,1,0:T(8,128)(2,1)S(1)}, u32[]{:S(2)}) copy-start(bf16[4,48,768]{2,1,0:T(8,128)(2,1)S(1)} %bitcast_add_fusion.3.refs_3_) | copy-start | bytes 884740
  292.5 10.9 %copy-start.3 = (bf16[4,56,768]{2,1,0:T(8,128)(2,1)}, bf16[4,56,768]{2,1,0:T(8,128)(2,1)S(1)}, u32[]{:S(2)}) copy-start(bf16[4,56,768]{2,1,0:T(8,128)(2,1)S(1)} %bitcast_add_fusion.2.refs_0_) | copy-start | bytes 1032196
  292.7 8.9 %collective-permute-start.28 = (bf16[2,56,768]{2,1,0:T(8,128)(2,1)S(1)}, bf16[2,56,768]{2,1,0:T(8,128)(2,1)S(1)}, u32[]{:S(2)}, u32[]{:S(2)}) collective-permute-start(bf16[2,56,768]{2,1,0:T(8,128)(2,1)S(1)} %slice.170), channel_id=1, source_target_pairs={{0,2},{1,3},{2,0},{3,1},{4,6},{5,7},{6,4},{7,5},{8,10},{9,11},{10,... | collective-permute-start | bytes 516104 | tf_op jit(solution)/shard_map/ppermute | solution.py:33
  294.5 7.1 %collective-permute-start.29 = (bf16[2,48,768]{2,1,0:T(8,128)(2,1)S(1)}, bf16[2,48,768]{2,1,0:T(8,128)(2,1)S(1)}, u32[]{:S(2)}, u32[]{:S(2)}) collective-permute-start(bf16[2,48,768]{2,1,0:T(8,128)(2,1)S(1)} %slice.171), channel_id=1, source_target_pairs={{0,6},{1,7},{2,4},{3,5},{4,2},{5,3},{6,0},{7,1},{8,14},{9,15},{10,... | collective-permute-start | bytes 442376 | tf_op jit(solution)/shard_map/ppermute | solution.py:33
  301.6 7.1 %copy-start.10 = (bf16[2,48,768]{2,1,0:T(8,128)(2,1)}, bf16[2,48,768]{2,1,0:T(8,128)(2,1)S(1)}, u32[]{:S(2)}) copy-start(bf16[2,48,768]{2,1,0:T(8,128)(2,1)S(1)} %collective-permute-done.29.refs_4_) | copy-start | bytes 442372
  301.6 7.1 %copy-start.9 = (bf16[2,56,768]{2,1,0:T(8,128)(2,1)}, bf16[2,56,768]{2,1,0:T(8,128)(2,1)S(1)}, u32[]{:S(2)}) copy-start(bf16[2,56,768]{2,1,0:T(8,128)(2,1)S(1)} %collective-permute-done.28.refs_1_) | copy-start | bytes 516100
  301.6 7.1 %collective-permute-start.30 = (bf16[56,768]{1,0:T(8,128)(2,1)S(1)}, bf16[56,768]{1,0:T(8,128)(2,1)S(1)}, u32[]{:S(2)}, u32[]{:S(2)}) collective-permute-start(bf16[56,768]{1,0:T(8,128)(2,1)S(1)} %add_bitcast_fusion.2), channel_id=1, source_target_pairs={{0,6},{1,7},{2,4},{3,5},{4,2},{5,3},{6,0},{7,1},{8,14},{9,15},{10,... | collective-permute-start | bytes 258056 | tf_op jit(solution)/shard_map/ppermute | solution.py:33
  303.4 5.3 %collective-permute-start.31 = (bf16[48,768]{1,0:T(8,128)(2,1)S(1)}, bf16[48,768]{1,0:T(8,128)(2,1)S(1)}, u32[]{:S(2)}, u32[]{:S(2)}) collective-permute-start(bf16[48,768]{1,0:T(8,128)(2,1)S(1)} %add_bitcast_fusion.3), channel_id=1, source_target_pairs={{0,2},{1,3},{2,0},{3,1},{4,6},{5,7},{6,4},{7,5},{8,10},{9,11},{10,... | collective-permute-start | bytes 221192 | tf_op jit(solution)/shard_map/ppermute | solution.py:33
  (12 other events, 31.2 us)
Sparse Core Ops, SparseCore 0:
  11.6 94.5 all-gather.2

commit v4 on v3

--- a/solution.py
+++ b/solution.py
@@ -485,7 +485,7 @@
 
 def first_back(acc, gtwo, hat, inv, ctx, wop, order, vecs):
     rows = acc.shape[0]
-    step = 256
+    step = 2 * BLOCK
     row_spec = pl.BlockSpec((step, D), lambda i: (i, 0))
     return call(
         first_back_body,
@@ -726,7 +726,9 @@
 def gather_near(shard):
     rows = shard.shape[0]
     half = rows // 16 * 8
-    column = jnp.stack([shard] + [swap(shard, "dp", 2 * step) for step in range(1, 4)])
+    one, three = swap(shard, "dp", 2), swap(shard, "dp", 6)
+    two = jnp.concatenate((swap(three[:half], "dp", 2), swap(one[half:], "dp", 6)))
+    column = jnp.stack((shard, one, two, three))
     over_x = swap(column, "dp", 1)
     over_y = swap(column, "blk", 2)
     over_both = jnp.concatenate((swap(over_y[:, :half], "dp", 1), swap(over_x[:, half:], "blk", 2)), axis=1)

time: 321 us -> 317 us (0.988)
  waiting for transfers between devices: 81.1 us -> 75.7 us
    ppermute x32 -> x33, waiting for transfers between devices: 81.1 us -> 75.7 us  [swap(): lax.ppermute(value, axis, [(source, source ^ mask) for source in range(la...]
    ppermute x32 -> x33, starting transfers between devices: 30.6 us -> 33.2 us  [swap(): lax.ppermute(value, axis, [(source, source ^ mask) for source in range(la...]
  transfers between devices with their start and end apart: 33 -> 34, of which waited for: 16 -> 19; matrix products, arithmetic and copies ran while one was open for 6% -> 6% of each run, Pallas kernels for 38% -> 38%
where the time goes in v4:
time: 317 us; the launch traced here: 316 us
  Pallas kernels  163 us (51%)
  waiting for transfers between devices  75.7 us (24%)
  starting transfers between devices  33.2 us (10%)
  other arithmetic  16.5 us (5%)
  between operations  14.7 us (5%)
  local copies, waits for them, and re-layouts  12.8 us (4%)
    ppermute x33, waiting for transfers between devices, swap(): lax.ppermute(value, axis, [(source, source ^ mask) for source in range(la...  75.7 us
    ppermute x33, starting transfers between devices, swap(): lax.ppermute(value, axis, [(source, source ^ mask) for source in range(la...  33.2 us
    pallas_call x1, Pallas kernels, ffn_forward(): call(ffn_forward_body, (rows // span, chunks), [row_spec, row_spec, row_s...  29.6 us
    pallas_call x1, Pallas kernels, ffn_backward(): call(ffn_backward_body, (FF // D,), [whole((rows, D)), pl.BlockSpec((rows...  26.4 us
    pallas_call x1, Pallas kernels, attend_back(): call(attend_back_body, (seqs, H // 2), [spec] * 3 + [pl.BlockSpec((1, 2,...  21.9 us
    pallas_call x1, Pallas kernels, attend(): call(attend_body, (seqs, H // 2), [spec] * 3, [spec, pl.BlockSpec((1, 2,...  18.5 us
    pallas_call x1, Pallas kernels, grad_project(): call(grad_project_body, (3,), [whole((rows, D)), whole((rows, D)), pl.Blo...  12.7 us
    pallas_call x1, Pallas kernels, project(): call(project_body, (rows // step,), [row_spec, row_spec] + [whole(pieces[...  12 us
  transfers between devices with their start and end apart: 34, of which 19 were waited for; matrix products, arithmetic and copies ran while one was open for 6% of the time, Pallas kernels for 38%

profile of v4, /device:TPU:0, one launch (start us, length us, event | category | flops | bytes accessed | tf_op | source)
XLA Modules:
  0.0 316.5 jit_solution(1040377068023299068)
XLA Ops:
  12.3 5.1 %collective-permute-start.2 = (bf16[112,768]{1,0:T(8,128)(2,1)S(1)}, bf16[112,768]{1,0:T(8,128)(2,1)S(1)}, u32[]{:S(2)}, u32[]{:S(2)}) collective-permute-start(bf16[112,768]{1,0:T(8,128)(2,1)S(1)} %concatenate.16), channel_id=1, source_target_pairs={{0,6},{1,7},{2,4},{3,5},{4,2},{5,3},{6,0},{7,1},{8,14},{9,15},{10,... | collective-permute-start | bytes 516104 | tf_op jit(solution)/shard_map/ppermute | solution.py:33
  17.5 5.3 %collective-permute-done.2 = bf16[112,768]{1,0:T(8,128)(2,1)S(1)} collective-permute-done((bf16[112,768]{1,0:T(8,128)(2,1)S(1)}, bf16[112,768]{1,0:T(8,128)(2,1)S(1)}, u32[]{:S(2)}, u32[]{:S(2)}) %collective-permute-start.2) | collective-permute-done | bytes 172064 | tf_op jit(solution)/shard_map/ppermute | solution.py:33
  22.7 2.6 collective-permute-start.3
  25.3 2.6 collective-permute-done.1
  27.9 3.5 %collective-permute-done.3 = bf16[56,768]{1,0:T(8,128)(2,1)S(1)} collective-permute-done((bf16[56,768]{1,0:T(8,128)(2,1)S(1)}, bf16[56,768]{1,0:T(8,128)(2,1)S(1)}, u32[]{:S(2)}, u32[]{:S(2)}) %collective-permute-start.3) | collective-permute-done | bytes 86048 | tf_op jit(solution)/shard_map/ppermute | solution.py:33
  31.4 4.5 %collective-permute-done.4 = bf16[56,768]{1,0:T(8,128)(2,1)S(1)} collective-permute-done((bf16[56,768]{1,0:T(8,128)(2,1)S(1)}, bf16[56,768]{1,0:T(8,128)(2,1)S(1)}, u32[]{:S(2)}, u32[]{:S(2)}) %collective-permute-start.4) | collective-permute-done | bytes 86048 | tf_op jit(solution)/shard_map/ppermute | solution.py:33
  36.1 1.3 collective-permute-start.6
  37.4 1.4 collective-permute-start.5
  38.7 15.7 %collective-permute-done.6.refs_2_ = bf16[4,112,768]{2,1,0:T(8,128)(2,1)S(1)} collective-permute-done((bf16[4,112,768]{2,1,0:T(8,128)(2,1)S(1)}, bf16[4,112,768]{2,1,0:T(8,128)(2,1)S(1)}, u32[]{:S(2)}, u32[]{:S(2)}) %collective-permute-start.6) | collective-permute-done | bytes 688160 | tf_op jit(solution)/shard_map/ppermute | solution.py:33
  54.4 1.8 collective-permute-start.7
  56.3 7.2 %collective-permute-done.5.refs_1_ = bf16[4,112,768]{2,1,0:T(8,128)(2,1)S(1)} collective-permute-done((bf16[4,112,768]{2,1,0:T(8,128)(2,1)S(1)}, bf16[4,112,768]{2,1,0:T(8,128)(2,1)S(1)}, u32[]{:S(2)}, u32[]{:S(2)}) %collective-permute-start.5) | collective-permute-done | bytes 688160 | tf_op jit(solution)/shard_map/ppermute | solution.py:33
  64.1 3.3 %collective-permute-done.7 = bf16[4,56,768]{2,1,0:T(8,128)(2,1)S(1)} collective-permute-done((bf16[4,56,768]{2,1,0:T(8,128)(2,1)S(1)}, bf16[4,56,768]{2,1,0:T(8,128)(2,1)S(1)}, u32[]{:S(2)}, u32[]{:S(2)}) %collective-permute-start.7) | collective-permute-done | bytes 344096 | tf_op jit(solution)/shard_map/ppermute | solution.py:33
  67.5 3.3 %collective-permute-done.8 = bf16[4,56,768]{2,1,0:T(8,128)(2,1)S(1)} collective-permute-done((bf16[4,56,768]{2,1,0:T(8,128)(2,1)S(1)}, bf16[4,56,768]{2,1,0:T(8,128)(2,1)S(1)}, u32[]{:S(2)}, u32[]{:S(2)}) %collective-permute-start.8) | collective-permute-done | bytes 344096 | tf_op jit(solution)/shard_map/ppermute | solution.py:33
  71.7 1.3 fusion.refs_8_.order_ref.refs_6_
  73.8 12.0 %project.1 = (bf16[1024,768]{1,0:T(8,128)(2,1)}, bf16[1024,768]{1,0:T(8,128)(2,1)}, bf16[1024,768]{1,0:T(8,128)(2,1)}, bf16[3,768,768]{2,1,0:T(8,128)(2,1)}, bf1...) custom-call(s32[1]{0:T(128)} %bitcast.me_ref, bf16[1024,768]{1,0:T(8,128)(2,1)} %bitcast.111, ...), custom_call_target="tpu_custom_call" | custom-call | flops 3623878656 | bytes 14942208 | tf_op jit(solution)/shard_map/project/pallas_call | solution.py:113
  85.7 18.5 %attend.1 = (bf16[1024,768]{1,0:T(8,128)(2,1)}, bf16[2,12,512,512]{3,2,1,0:T(8,128)(2,1)}) custom-call(s32[2,2]{1,0:T(2,128)} %pad_add_fusion.valid_ref, bf16[1024,768]{1,0:T(8,128)(2,1)} %get-tuple-element.81.q_ref, bf16[1024,768]{1,0:T(8,128)(2,1)} %get-tuple-element.82.k_ref, bf16[1024,768]{1,0:T(8,128)(2,1)} %get-tuple-element.83.v_ref), custom_call_target="tpu_custom_call" | custom-call | flops 6442450944 | bytes 18874368 | tf_op jit(solution)/shard_map/attend/pallas_call | solution.py:152
  104.2 5.8 %first_norm.1 = (f32[1024,768]{1,0:T(8,128)}, f32[1024,128]{1,0:T(8,128)}, bf16[1024,768]{1,0:T(8,128)(2,1)}) custom-call(bf16[1024,768]{1,0:T(8,128)(2,1)} %get-tuple-element.84.ctx_ref, bf16[1024,768]{1,0:T(8,128)(2,1)} %bitcast.112, bf16[768,768]{1,0:T(8,128)(2,1)} %get-tuple-element.85.wop_ref, f32[8,768]{1,0:T(8,128)} %get-tuple-element.86.vec_ref), custom_call_target="tpu_custom_call" | custom-call | flops 1207959552 | bytes 9437184 | tf_op jit(solution)/shard_map/first_norm/pallas_call | solution.py:235
  110.0 29.6 %ffn_forward.1 = (bf16[1024,3072]{1,0:T(8,128)(2,1)}, bf16[1024,3072]{1,0:T(8,128)(2,1)}, bf16[1024,768]{1,0:T(8,128)(2,1)}, f32[1024,768]{1,0:T(8,128)}, bf16[1024,768]{1,0:T(8,128)(2,1)}, /*index=5*/f32[8,768]{1,0:T(8,128)}) custom-call(bf16[1024,768]{1,0:T(8,128)(2,1)} %get-tuple-element.87.low_ref, f32[1024,768]{1,0:T(8,128)} %get-tuple-element.88.hat_ref, ...), custom_call_target="tpu_custom_call" | custom-call | flops 9663676416 | bytes 29884416 | tf_op jit(solution)/shard_map/ffn_forward/pallas_call | solution.py:324
  139.7 9.8 %grad_down.1 = (bf16[2,8,96,768]{3,2,1,0:T(8,128)(2,1)}, bf16[2,8,96,768]{3,2,1,0:T(8,128)(2,1)}) custom-call(s32[1]{0:T(128)} %bitcast.me_ref, bf16[1024,3072]{1,0:T(8,128)(2,1)} %get-tuple-element.91.act_ref, bf16[1024,768]{1,0:T(8,128)(2,1)} %get-tuple-element.95.gsec_ref), custom_call_target="tpu_custom_call" | custom-call | flops 4831838208 | bytes 12582912 | tf_op jit(solution)/shard_map/grad_down/pallas_call | solution.py:371
  150.0 26.4 %ffn_backward.1 = (bf16[16,96,768]{2,1,0:T(8,128)(2,1)}, bf16[16,96,768]{2,1,0:T(8,128)(2,1)}, f32[4,1,768]{2,1,0:T(1,128)}, f32[1024,768]{1,0:T(8,128)}) custom-call(s32[1]{0:T(128)} %bitcast.me_ref, bf16[1024,768]{1,0:T(8,128)(2,1)} %get-tuple-element.95.gsec_ref, bf16[1024,3072]{1,0:T(8,128)(2,1)} %get-tuple-element.96.slope_ref, ...), custom_call_target="tpu_custom_call" | custom-call | flops 14495514624 | bytes 26738688 | tf_op jit(solution)/shard_map/ffn_backward/pallas_call | solution.py:431
  176.5 3.1 add.96
  181.8 11.0 %first_back.1 = (f32[1024,768]{1,0:T(8,128)}, bf16[1024,768]{1,0:T(8,128)(2,1)}, bf16[32,24,768]{2,1,0:T(8,128)(2,1)}, f32[8,768]{1,0:T(8,128)}) custom-call(f32[1024,768]{1,0:T(8,128)} %get-tuple-element.101.acc_ref, f32[1024,768]{1,0:T(8,128)} %get-tuple-element.102.gtwo_ref, f32[1024,768]{1,0:T(8,128)} %get-tuple-element.88.hat_ref, ...), custom_call_target="tpu_custom_call" | custom-call | flops 2415919104 | bytes 19267584 | tf_op jit(solution)/shard_map/first_back/pallas_call | solution.py:490
  192.9 1.4 copy-done.5
  194.3 3.1 add.94
  197.4 2.1 collective-permute-start.15
  200.1 21.9 %attend_back.1 = (bf16[3,1024,768]{2,1,0:T(8,128)(2,1)}, bf16[2,1024,384]{2,1,0:T(8,128)(2,1)}) custom-call(bf16[1024,768]{1,0:T(8,128)(2,1)} %get-tuple-element.81.q_ref, bf16[1024,768]{1,0:T(8,128)(2,1)} %get-tuple-element.82.k_ref, bf16[1024,768]{1,0:T(8,128)(2,1)} %get-tuple-element.83.v_ref, bf16[2,12,512,512]{3,2,1,0:T(8,128)(2,1)} %get-tuple-element.108.p_ref, ...), custom_call_target="tpu_custom_call" | custom-call | flops 12884901888 | bytes 23592960 | tf_op jit(solution)/shard_map/attend_back/pallas_call | solution.py:197
  222.1 4.2 %collective-permute-done.15 = bf16[2,4,96,768]{3,2,1,0:T(8,128)(2,1)} collective-permute-done((bf16[2,4,96,768]{3,2,1,0:T(8,128)(2,1)S(1)}, bf16[2,4,96,768]{3,2,1,0:T(8,128)(2,1)}, u32[]{:S(2)}, u32[]{:S(2)}) %collective-permute-start.15) | collective-permute-done | bytes 1179680 | tf_op jit(solution)/shard_map/ppermute | solution.py:33
  226.3 1.4 fusion.2
  227.9 1.4 copy_add_fusion
  229.4 1.5 collective-permute-start.18
  232.3 12.7 %grad_project.1 = (bf16[16,104,768]{2,1,0:T(8,128)(2,1)}, bf16[16,104,768]{2,1,0:T(8,128)(2,1)}) custom-call(s32[1]{0:T(128)} %bitcast.me_ref, bf16[1024,768]{1,0:T(8,128)(2,1)} %bitcast.113, bf16[1024,768]{1,0:T(8,128)(2,1)} %collective-permute-done.xp_ref, bf16[3,1024,768]{2,1,0:T(8,128)(2,1)} %get-tuple-element.114.grad_ref.grads_ref, ...), custom_call_target="tpu_custom_call" | custom-call | flops 3623878656 | bytes 14942208 | tf_op jit(solution)/shard_map/grad_project/pallas_call | solution.py:587
  245.1 1.5 collective-permute-done.17
  247.3 4.5 %collective-permute-done.21 = bf16[16,104,768]{2,1,0:T(8,128)(2,1)S(1)} collective-permute-done((bf16[16,104,768]{2,1,0:T(8,128)(2,1)}, bf16[16,104,768]{2,1,0:T(8,128)(2,1)S(1)}, u32[]{:S(2)}, u32[]{:S(2)}) %collective-permute-start.21) | collective-permute-done | bytes 2555936 | tf_op jit(solution)/shard_map/ppermute | solution.py:33
  256.7 3.1 collective-permute-start.20
  259.8 9.6 %grad_input.1 = f32[1024,768]{1,0:T(8,128)} custom-call(f32[1024,768]{1,0:T(8,128)} %get-tuple-element.125.gres_ref, bf16[3,1024,768]{2,1,0:T(8,128)(2,1)} %get-tuple-element.114.grad_ref.grads_ref, bf16[2,1024,384]{2,1,0:T(8,128)(2,1)} %collective-permute-done.22.back_ref, bf16[3,768,768]{2,1,0:T(8,128)(2,1)} %get-tuple-element.127.w_ref), custom_call_target="tpu_custom_call" | custom-call | flops 3623878656 | bytes 16121856 | tf_op jit(solution)/shard_map/grad_input/pallas_call | solution.py:626
  269.5 4.3 %collective-permute-done.19.refs_1_ = bf16[2,96,768]{2,1,0:T(8,128)(2,1)} collective-permute-done((bf16[2,96,768]{2,1,0:T(8,128)(2,1)}, bf16[2,96,768]{2,1,0:T(8,128)(2,1)}, u32[]{:S(2)}, u32[]{:S(2)}) %collective-permute-start.19) | collective-permute-done | bytes 294944 | tf_op jit(solution)/shard_map/ppermute | solution.py:33
  276.1 1.6 collective-permute-start.26
  278.7 1.7 collective-permute-start.25
  281.0 1.6 collective-permute-start.27
  282.5 2.5 collective-permute-done.26
  285.1 3.4 %collective-permute-done.25 = bf16[4,56,768]{2,1,0:T(8,128)(2,1)S(1)} collective-permute-done((bf16[4,56,768]{2,1,0:T(8,128)(2,1)S(1)}, bf16[4,56,768]{2,1,0:T(8,128)(2,1)S(1)}, u32[]{:S(2)}, u32[]{:S(2)}) %collective-permute-start.25) | collective-permute-done | bytes 344096 | tf_op jit(solution)/shard_map/ppermute | solution.py:33
  288.9 1.8 collective-permute-start.29
  290.7 1.4 collective-permute-start.30
  292.1 2.1 finish_ffn.1
  294.3 3.6 %collective-permute-done.30.refs_4_ = bf16[2,48,768]{2,1,0:T(8,128)(2,1)S(1)} collective-permute-done((bf16[2,48,768]{2,1,0:T(8,128)(2,1)S(1)}, bf16[2,48,768]{2,1,0:T(8,128)(2,1)S(1)}, u32[]{:S(2)}, u32[]{:S(2)}) %collective-permute-start.30) | collective-permute-done | bytes 147488 | tf_op jit(solution)/shard_map/ppermute | solution.py:33
  297.9 1.7 collective-permute-start.31
  299.7 5.3 %collective-permute-done.32.refs_5_ = bf16[48,768]{1,0:T(8,128)(2,1)S(1)} collective-permute-done((bf16[48,768]{1,0:T(8,128)(2,1)S(1)}, bf16[48,768]{1,0:T(8,128)(2,1)S(1)}, u32[]{:S(2)}, u32[]{:S(2)}) %collective-permute-start.32) | collective-permute-done | bytes 73760 | tf_op jit(solution)/shard_map/ppermute | solution.py:33
  306.2 3.4 %finish_last.1 = (f32[144,128]{1,0:T(8,128)}, f32[144,128]{1,0:T(8,128)}, f32[144,128]{1,0:T(8,128)}, f32[144,128]{1,0:T(8,128)}, f32[192]{0:T(256)}, /*index=5*/f32[96]{0:T(128)}) custom-call(bf16[4,56,768]{2,1,0:T(8,128)(2,1)} %copy-done.3, bf16[2,56,768]{2,1,0:T(8,128)(2,1)} %copy-done.9, bf16[56,768]{1,0:T(8,128)(2,1)} %copy-done.16, ...), custom_call_target="tpu_custom_call" | custom-call | bytes 638976 | tf_op jit(solution)/shard_map/finish_last/pallas_call | solution.py:692
  (154 shorter events, 24.0 us)
Async XLA Ops:
  7.2 102.8 %all-gather.3.cloned.1.call-start = ((), (), s32[]{:S(2)}) async-start(), calls=%async_computation | async-start | bytes 9732096 | tf_op jit(solution)/shard_map/all_gather | solution.py:705
  8.3 3.9 %copy-start.21 = (bf16[18432]{0:T(1024)(128)(2,1)S(1)}, bf16[18432]{0:T(1024)(128)(2,1)}, u32[]{:S(2)}) copy-start(bf16[18432]{0:T(1024)(128)(2,1)} %param.19) | copy-start | bytes 110596
  12.3 10.4 %collective-permute-start.2 = (bf16[112,768]{1,0:T(8,128)(2,1)S(1)}, bf16[112,768]{1,0:T(8,128)(2,1)S(1)}, u32[]{:S(2)}, u32[]{:S(2)}) collective-permute-start(bf16[112,768]{1,0:T(8,128)(2,1)S(1)} %concatenate.16), channel_id=1, source_target_pairs={{0,6},{1,7},{2,4},{3,5},{4,2},{5,3},{6,0},{7,1},{8,14},{9,15},{10,... | collective-permute-start | bytes 516104 | tf_op jit(solution)/shard_map/ppermute | solution.py:33
  17.5 10.4 %collective-permute-start.1 = (bf16[112,768]{1,0:T(8,128)(2,1)S(1)}, bf16[112,768]{1,0:T(8,128)(2,1)S(1)}, u32[]{:S(2)}, u32[]{:S(2)}) collective-permute-start(bf16[112,768]{1,0:T(8,128)(2,1)S(1)} %concatenate.16), channel_id=1, source_target_pairs={{0,2},{1,3},{2,0},{3,1},{4,6},{5,7},{6,4},{7,5},{8,10},{9,11},{10,... | collective-permute-start | bytes 516104 | tf_op jit(solution)/shard_map/ppermute | solution.py:33
  22.7 8.7 %collective-permute-start.3 = (bf16[56,768]{1,0:T(8,128)(2,1)S(1)}, bf16[56,768]{1,0:T(8,128)(2,1)S(1)}, u32[]{:S(2)}, u32[]{:S(2)}) collective-permute-start(bf16[56,768]{1,0:T(8,128)(2,1)S(1)} %slice.188), channel_id=1, source_target_pairs={{0,2},{1,3},{2,0},{3,1},{4,6},{5,7},{6,4},{7,5},{8,10},{9,11},{10,... | collective-permute-start | bytes 258056 | tf_op jit(solution)/shard_map/ppermute | solution.py:33
  27.9 8.1 %collective-permute-start.4 = (bf16[56,768]{1,0:T(8,128)(2,1)S(1)}, bf16[56,768]{1,0:T(8,128)(2,1)S(1)}, u32[]{:S(2)}, u32[]{:S(2)}) collective-permute-start(bf16[56,768]{1,0:T(8,128)(2,1)S(1)} %slice.189), channel_id=1, source_target_pairs={{0,6},{1,7},{2,4},{3,5},{4,2},{5,3},{6,0},{7,1},{8,14},{9,15},{10,... | collective-permute-start | bytes 258056 | tf_op jit(solution)/shard_map/ppermute | solution.py:33
  36.1 36.9 %copy-start.7 = (bf16[4,112,768]{2,1,0:T(8,128)(2,1)}, bf16[4,112,768]{2,1,0:T(8,128)(2,1)S(1)}, u32[]{:S(2)}) copy-start(bf16[4,112,768]{2,1,0:T(8,128)(2,1)S(1)} %pad_maximum_fusion.refs_0_) | copy-start | bytes 2064388
  36.1 34.9 %copy-start.22 = (s32[2,2]{1,0:T(2,128)S(1)}, s32[2,2]{1,0:T(2,128)}, u32[]{:S(2)}) copy-start(s32[2,2]{1,0:T(2,128)} %param.14) | copy-start | bytes 52
  36.1 18.3 %collective-permute-start.6 = (bf16[4,112,768]{2,1,0:T(8,128)(2,1)S(1)}, bf16[4,112,768]{2,1,0:T(8,128)(2,1)S(1)}, u32[]{:S(2)}, u32[]{:S(2)}) collective-permute-start(bf16[4,112,768]{2,1,0:T(8,128)(2,1)S(1)} %pad_maximum_fusion.refs_0_), channel_id=1, source_target_pairs={{0,16},{8,24},{16,0},{24,8},{1,17},{9,25},{17,1},{25,9},{2,18},{10... | collective-permute-start | bytes 2064392 | tf_op jit(solution)/shard_map/ppermute | solution.py:33
  37.4 26.1 %collective-permute-start.5 = (bf16[4,112,768]{2,1,0:T(8,128)(2,1)S(1)}, bf16[4,112,768]{2,1,0:T(8,128)(2,1)S(1)}, u32[]{:S(2)}, u32[]{:S(2)}) collective-permute-start(bf16[4,112,768]{2,1,0:T(8,128)(2,1)S(1)} %pad_maximum_fusion.refs_0_), channel_id=1, source_target_pairs={{0,1},{1,0},{2,3},{3,2},{4,5},{5,4},{6,7},{7,6},{8,9},{9,8},{10,11... | collective-permute-start | bytes 2064392 | tf_op jit(solution)/shard_map/ppermute | solution.py:33
  38.7 34.2 %collective-permute-start = (bf16[1024,768]{1,0:T(8,128)(2,1)}, bf16[1024,768]{1,0:T(8,128)(2,1)}, u32[]{:S(2)}, u32[]{:S(2)}) collective-permute-start(bf16[1024,768]{1,0:T(8,128)(2,1)} %bitcast.110), channel_id=1, source_target_pairs={{0,8},{8,0},{16,24},{24,16},{1,9},{9,1},{17,25},{25,17},{2,10},{10... | collective-permute-start | bytes 4718600 | tf_op jit(solution)/shard_map/ppermute | solution.py:33
  54.4 18.5 %copy-start.11 = (bf16[4,112,768]{2,1,0:T(8,128)(2,1)}, bf16[4,112,768]{2,1,0:T(8,128)(2,1)S(1)}, u32[]{:S(2)}) copy-start(bf16[4,112,768]{2,1,0:T(8,128)(2,1)S(1)} %collective-permute-done.6.refs_2_) | copy-start | bytes 2064388
  54.4 13.1 %collective-permute-start.7 = (bf16[4,56,768]{2,1,0:T(8,128)(2,1)S(1)}, bf16[4,56,768]{2,1,0:T(8,128)(2,1)S(1)}, u32[]{:S(2)}, u32[]{:S(2)}) collective-permute-start(bf16[4,56,768]{2,1,0:T(8,128)(2,1)S(1)} %slice.190), channel_id=1, source_target_pairs={{0,1},{1,0},{2,3},{3,2},{4,5},{5,4},{6,7},{7,6},{8,9},{9,8},{10,11... | collective-permute-start | bytes 1032200 | tf_op jit(solution)/shard_map/ppermute | solution.py:33
  63.5 9.5 %copy-start.12 = (bf16[4,112,768]{2,1,0:T(8,128)(2,1)}, bf16[4,112,768]{2,1,0:T(8,128)(2,1)S(1)}, u32[]{:S(2)}) copy-start(bf16[4,112,768]{2,1,0:T(8,128)(2,1)S(1)} %collective-permute-done.5.refs_1_) | copy-start | bytes 2064388
  63.5 7.3 %collective-permute-start.8 = (bf16[4,56,768]{2,1,0:T(8,128)(2,1)S(1)}, bf16[4,56,768]{2,1,0:T(8,128)(2,1)S(1)}, u32[]{:S(2)}, u32[]{:S(2)}) collective-permute-start(bf16[4,56,768]{2,1,0:T(8,128)(2,1)S(1)} %slice.191), channel_id=1, source_target_pairs={{0,16},{8,24},{16,0},{24,8},{1,17},{9,25},{17,1},{25,9},{2,18},{10... | collective-permute-start | bytes 1032200 | tf_op jit(solution)/shard_map/ppermute | solution.py:33
  63.6 9.4 %collective-permute-start.9 = (bf16[4,112,768]{2,1,0:T(8,128)(2,1)S(1)}, bf16[4,112,768]{2,1,0:T(8,128)(2,1)S(1)}, u32[]{:S(2)}, u32[]{:S(2)}) collective-permute-start(bf16[4,112,768]{2,1,0:T(8,128)(2,1)S(1)} %pad_maximum_fusion.refs_0_), channel_id=1, source_target_pairs={{0,8},{8,0},{16,24},{24,16},{1,9},{9,1},{17,25},{25,17},{2,10},{10... | collective-permute-start | bytes 2064392 | tf_op jit(solution)/shard_map/ppermute | solution.py:33
  63.6 9.3 %collective-permute-start.11 = (bf16[4,112,768]{2,1,0:T(8,128)(2,1)S(1)}, bf16[4,112,768]{2,1,0:T(8,128)(2,1)}, u32[]{:S(2)}, u32[]{:S(2)}) collective-permute-start(bf16[4,112,768]{2,1,0:T(8,128)(2,1)S(1)} %collective-permute-done.6.refs_2_), channel_id=1, source_target_pairs={{0,8},{8,0},{16,24},{24,16},{1,9},{9,1},{17,25},{25,17},{2,10},{10... | collective-permute-start | bytes 2064392 | tf_op jit(solution)/shard_map/ppermute | solution.py:33
  67.5 5.5 %collective-permute-start.10 = (bf16[4,112,768]{2,1,0:T(8,128)(2,1)S(1)}, bf16[4,112,768]{2,1,0:T(8,128)(2,1)}, u32[]{:S(2)}, u32[]{:S(2)}) collective-permute-start(bf16[4,112,768]{2,1,0:T(8,128)(2,1)S(1)} %collective-permute-done.5.refs_1_), channel_id=1, source_target_pairs={{0,8},{8,0},{16,24},{24,16},{1,9},{9,1},{17,25},{25,17},{2,10},{10... | collective-permute-start | bytes 2064392 | tf_op jit(solution)/shard_map/ppermute | solution.py:33
  70.8 2.6 collective-permute-start.12
  149.5 27.0 %collective-permute-start.14 = (bf16[16,96,768]{2,1,0:T(8,128)(2,1)}, bf16[16,96,768]{2,1,0:T(8,128)(2,1)}, u32[]{:S(2)}, u32[]{:S(2)}) collective-permute-start(bf16[16,96,768]{2,1,0:T(8,128)(2,1)} %bitcast.108), channel_id=1, source_target_pairs={{0,8},{8,0},{16,24},{24,16},{1,9},{9,1},{17,25},{25,17},{2,10},{10... | collective-permute-start | bytes 7077896 | tf_op jit(solution)/shard_map/ppermute | solution.py:33
  176.4 16.5 %collective-permute-start.13 = (bf16[16,96,768]{2,1,0:T(8,128)(2,1)}, bf16[16,96,768]{2,1,0:T(8,128)(2,1)S(1)}, u32[]{:S(2)}, u32[]{:S(2)}) collective-permute-start(bf16[16,96,768]{2,1,0:T(8,128)(2,1)} %get-tuple-element.98), channel_id=1, source_target_pairs={{0,8},{8,0},{16,24},{24,16},{1,9},{9,1},{17,25},{25,17},{2,10},{10... | collective-permute-start | bytes 7077896 | tf_op jit(solution)/shard_map/ppermute | solution.py:33
  197.4 28.8 %collective-permute-start.15 = (bf16[2,4,96,768]{3,2,1,0:T(8,128)(2,1)S(1)}, bf16[2,4,96,768]{3,2,1,0:T(8,128)(2,1)}, u32[]{:S(2)}, u32[]{:S(2)}) collective-permute-start(bf16[2,4,96,768]{3,2,1,0:T(8,128)(2,1)S(1)} %slice_bitcast_fusion), channel_id=1, source_target_pairs={{0,1},{1,0},{2,3},{3,2},{4,5},{5,4},{6,7},{7,6},{8,9},{9,8},{10,11... | collective-permute-start | bytes 3538952 | tf_op jit(solution)/shard_map/ppermute | solution.py:33
  199.6 28.4 %collective-permute-start.16 = (bf16[4,2,96,768]{3,2,0,1:T(8,128)(2,1)}, bf16[4,2,96,768]{3,2,0,1:T(8,128)(2,1)}, u32[]{:S(2)}, u32[]{:S(2)}) collective-permute-start(bf16[4,2,96,768]{3,2,0,1:T(8,128)(2,1)} %copy.38), channel_id=1, source_target_pairs={{0,16},{8,24},{16,0},{24,8},{1,17},{9,25},{17,1},{25,9},{2,18},{10... | collective-permute-start | bytes 3538952 | tf_op jit(solution)/shard_map/ppermute | solution.py:33
  222.1 5.9 %copy-start = (bf16[8,96,768]{2,1,0:T(8,128)(2,1)S(1)}, bf16[8,96,768]{2,1,0:T(8,128)(2,1)}, u32[]{:S(2)}) copy-start(bf16[8,96,768]{2,1,0:T(8,128)(2,1)} %get-tuple-element.184) | copy-start | bytes 3538948
  229.4 15.6 %collective-permute-start.18 = (bf16[4,96,768]{2,1,0:T(8,128)(2,1)S(1)}, bf16[4,96,768]{2,1,0:T(8,128)(2,1)S(1)}, u32[]{:S(2)}, u32[]{:S(2)}) collective-permute-start(bf16[4,96,768]{2,1,0:T(8,128)(2,1)S(1)} %slice_bitcast_fusion.4), channel_id=1, source_target_pairs={{0,1},{1,0},{2,3},{3,2},{4,5},{5,4},{6,7},{7,6},{8,9},{9,8},{10,11... | collective-permute-start | bytes 1769480 | tf_op jit(solution)/shard_map/ppermute | solution.py:33
  231.8 14.8 %collective-permute-start.17 = (bf16[4,96,768]{2,1,0:T(8,128)(2,1)}, bf16[4,96,768]{2,1,0:T(8,128)(2,1)S(1)}, u32[]{:S(2)}, u32[]{:S(2)}) collective-permute-start(bf16[4,96,768]{2,1,0:T(8,128)(2,1)} %slice_bitcast_fusion.5), channel_id=1, source_target_pairs={{0,16},{8,24},{16,0},{24,8},{1,17},{9,25},{17,1},{25,9},{2,18},{10... | collective-permute-start | bytes 1769480 | tf_op jit(solution)/shard_map/ppermute | solution.py:33
  245.0 6.7 %copy-start.4 = (bf16[16,104,768]{2,1,0:T(8,128)(2,1)S(1)}, bf16[16,104,768]{2,1,0:T(8,128)(2,1)}, u32[]{:S(2)}) copy-start(bf16[16,104,768]{2,1,0:T(8,128)(2,1)} %get-tuple-element.129) | copy-start | bytes 7667716
  245.1 35.3 %copy-start.1 = (bf16[4,96,768]{2,1,0:T(8,128)(2,1)}, bf16[4,96,768]{2,1,0:T(8,128)(2,1)S(1)}, u32[]{:S(2)}) copy-start(bf16[4,96,768]{2,1,0:T(8,128)(2,1)S(1)} %bitcast_add_fusion.refs_3_) | copy-start | bytes 1769476
  246.7 8.6 %copy-start.2 = (bf16[4,96,768]{2,1,0:T(8,128)(2,1)}, bf16[4,96,768]{2,1,0:T(8,128)(2,1)S(1)}, u32[]{:S(2)}) copy-start(bf16[4,96,768]{2,1,0:T(8,128)(2,1)S(1)} %bitcast_add_fusion.1.refs_0_) | copy-start | bytes 1769476
  246.7 5.1 %collective-permute-start.21 = (bf16[16,104,768]{2,1,0:T(8,128)(2,1)}, bf16[16,104,768]{2,1,0:T(8,128)(2,1)S(1)}, u32[]{:S(2)}, u32[]{:S(2)}) collective-permute-start(bf16[16,104,768]{2,1,0:T(8,128)(2,1)} %get-tuple-element.123), channel_id=1, source_target_pairs={{0,8},{8,0},{16,24},{24,16},{1,9},{9,1},{17,25},{25,17},{2,10},{10... | collective-permute-start | bytes 7667720 | tf_op jit(solution)/shard_map/ppermute | solution.py:33
  246.8 13.1 %collective-permute-start.22 = (bf16[2,1024,384]{2,1,0:T(8,128)(2,1)}, bf16[2,1024,384]{2,1,0:T(8,128)(2,1)}, u32[]{:S(2)}, u32[]{:S(2)}) collective-permute-start(bf16[2,1024,384]{2,1,0:T(8,128)(2,1)} %get-tuple-element.126), channel_id=1, source_target_pairs={{0,8},{8,0},{16,24},{24,16},{1,9},{9,1},{17,25},{25,17},{2,10},{10... | collective-permute-start | bytes 4718600 | tf_op jit(solution)/shard_map/ppermute | solution.py:33
  253.5 20.3 %collective-permute-start.24 = (bf16[4,2,48,768]{3,2,0,1:T(8,128)(2,1)}, bf16[4,2,48,768]{3,2,0,1:T(8,128)(2,1)}, u32[]{:S(2)}, u32[]{:S(2)}) collective-permute-start(bf16[4,2,48,768]{3,2,0,1:T(8,128)(2,1)} %bitcast.89), channel_id=1, source_target_pairs={{0,16},{8,24},{16,0},{24,8},{1,17},{9,25},{17,1},{25,9},{2,18},{10... | collective-permute-start | bytes 1769480 | tf_op jit(solution)/shard_map/ppermute | solution.py:33
  254.8 20.1 %collective-permute-start.23 = (bf16[2,4,56,768]{3,2,1,0:T(8,128)(2,1)}, bf16[2,4,56,768]{3,2,1,0:T(8,128)(2,1)}, u32[]{:S(2)}, u32[]{:S(2)}) collective-permute-start(bf16[2,4,56,768]{3,2,1,0:T(8,128)(2,1)} %slice_bitcast_fusion.2), channel_id=1, source_target_pairs={{0,1},{1,0},{2,3},{3,2},{4,5},{5,4},{6,7},{7,6},{8,9},{9,8},{10,11... | collective-permute-start | bytes 2064392 | tf_op jit(solution)/shard_map/ppermute | solution.py:33
  256.7 12.8 %collective-permute-start.20 = (bf16[2,96,768]{2,1,0:T(8,128)(2,1)}, bf16[2,96,768]{2,1,0:T(8,128)(2,1)S(1)}, u32[]{:S(2)}, u32[]{:S(2)}) collective-permute-start(bf16[2,96,768]{2,1,0:T(8,128)(2,1)} %slice.165), channel_id=1, source_target_pairs={{0,6},{1,7},{2,4},{3,5},{4,2},{5,3},{6,0},{7,1},{8,14},{9,15},{10,... | collective-permute-start | bytes 884744 | tf_op jit(solution)/shard_map/ppermute | solution.py:33
  259.8 13.9 %collective-permute-start.19 = (bf16[2,96,768]{2,1,0:T(8,128)(2,1)}, bf16[2,96,768]{2,1,0:T(8,128)(2,1)}, u32[]{:S(2)}, u32[]{:S(2)}) collective-permute-start(bf16[2,96,768]{2,1,0:T(8,128)(2,1)} %slice.164), channel_id=1, source_target_pairs={{0,2},{1,3},{2,0},{3,1},{4,6},{5,7},{6,4},{7,5},{8,10},{9,11},{10,... | collective-permute-start | bytes 884744 | tf_op jit(solution)/shard_map/ppermute | solution.py:33
  269.5 11.0 %copy-start.8 = (bf16[2,96,768]{2,1,0:T(8,128)(2,1)}, bf16[2,96,768]{2,1,0:T(8,128)(2,1)S(1)}, u32[]{:S(2)}) copy-start(bf16[2,96,768]{2,1,0:T(8,128)(2,1)S(1)} %collective-permute-done.20.refs_4_) | copy-start | bytes 884740
  276.1 9.0 %collective-permute-start.26 = (bf16[4,48,768]{2,1,0:T(8,128)(2,1)S(1)}, bf16[4,48,768]{2,1,0:T(8,128)(2,1)S(1)}, u32[]{:S(2)}, u32[]{:S(2)}) collective-permute-start(bf16[4,48,768]{2,1,0:T(8,128)(2,1)S(1)} %slice_bitcast_fusion.7), channel_id=1, source_target_pairs={{0,1},{1,0},{2,3},{3,2},{4,5},{5,4},{6,7},{7,6},{8,9},{9,8},{10,11... | collective-permute-start | bytes 884744 | tf_op jit(solution)/shard_map/ppermute | solution.py:33
  278.7 9.8 %collective-permute-start.25 = (bf16[4,56,768]{2,1,0:T(8,128)(2,1)S(1)}, bf16[4,56,768]{2,1,0:T(8,128)(2,1)S(1)}, u32[]{:S(2)}, u32[]{:S(2)}) collective-permute-start(bf16[4,56,768]{2,1,0:T(8,128)(2,1)S(1)} %slice_bitcast_fusion.6), channel_id=1, source_target_pairs={{0,16},{8,24},{16,0},{24,8},{1,17},{9,25},{17,1},{25,9},{2,18},{10... | collective-permute-start | bytes 1032200 | tf_op jit(solution)/shard_map/ppermute | solution.py:33
  280.5 8.1 %collective-permute-start.28 = (bf16[96,768]{1,0:T(8,128)(2,1)S(1)}, bf16[96,768]{1,0:T(8,128)(2,1)S(1)}, u32[]{:S(2)}, u32[]{:S(2)}) collective-permute-start(bf16[96,768]{1,0:T(8,128)(2,1)S(1)} %add_bitcast_fusion), channel_id=1, source_target_pairs={{0,2},{1,3},{2,0},{3,1},{4,6},{5,7},{6,4},{7,5},{8,10},{9,11},{10,... | collective-permute-start | bytes 442376 | tf_op jit(solution)/shard_map/ppermute | solution.py:33
  281.0 7.9 %collective-permute-start.27 = (bf16[96,768]{1,0:T(8,128)(2,1)S(1)}, bf16[96,768]{1,0:T(8,128)(2,1)S(1)}, u32[]{:S(2)}, u32[]{:S(2)}) collective-permute-start(bf16[96,768]{1,0:T(8,128)(2,1)S(1)} %add_bitcast_fusion.1), channel_id=1, source_target_pairs={{0,6},{1,7},{2,4},{3,5},{4,2},{5,3},{6,0},{7,1},{8,14},{9,15},{10,... | collective-permute-start | bytes 442376 | tf_op jit(solution)/shard_map/ppermute | solution.py:33
  285.1 14.5 %copy-start.6 = (bf16[4,48,768]{2,1,0:T(8,128)(2,1)}, bf16[4,48,768]{2,1,0:T(8,128)(2,1)S(1)}, u32[]{:S(2)}) copy-start(bf16[4,48,768]{2,1,0:T(8,128)(2,1)S(1)} %bitcast_add_fusion.3.refs_3_) | copy-start | bytes 884740
  288.5 11.1 %copy-start.3 = (bf16[4,56,768]{2,1,0:T(8,128)(2,1)}, bf16[4,56,768]{2,1,0:T(8,128)(2,1)S(1)}, u32[]{:S(2)}) copy-start(bf16[4,56,768]{2,1,0:T(8,128)(2,1)S(1)} %bitcast_add_fusion.2.refs_0_) | copy-start | bytes 1032196
  288.9 8.9 %collective-permute-start.29 = (bf16[2,56,768]{2,1,0:T(8,128)(2,1)S(1)}, bf16[2,56,768]{2,1,0:T(8,128)(2,1)S(1)}, u32[]{:S(2)}, u32[]{:S(2)}) collective-permute-start(bf16[2,56,768]{2,1,0:T(8,128)(2,1)S(1)} %slice.178), channel_id=1, source_target_pairs={{0,2},{1,3},{2,0},{3,1},{4,6},{5,7},{6,4},{7,5},{8,10},{9,11},{10,... | collective-permute-start | bytes 516104 | tf_op jit(solution)/shard_map/ppermute | solution.py:33
  290.7 7.1 %collective-permute-start.30 = (bf16[2,48,768]{2,1,0:T(8,128)(2,1)S(1)}, bf16[2,48,768]{2,1,0:T(8,128)(2,1)S(1)}, u32[]{:S(2)}, u32[]{:S(2)}) collective-permute-start(bf16[2,48,768]{2,1,0:T(8,128)(2,1)S(1)} %slice.179), channel_id=1, source_target_pairs={{0,6},{1,7},{2,4},{3,5},{4,2},{5,3},{6,0},{7,1},{8,14},{9,15},{10,... | collective-permute-start | bytes 442376 | tf_op jit(solution)/shard_map/ppermute | solution.py:33
  297.9 7.1 %copy-start.10 = (bf16[2,48,768]{2,1,0:T(8,128)(2,1)}, bf16[2,48,768]{2,1,0:T(8,128)(2,1)S(1)}, u32[]{:S(2)}) copy-start(bf16[2,48,768]{2,1,0:T(8,128)(2,1)S(1)} %collective-permute-done.30.refs_4_) | copy-start | bytes 442372
  297.9 7.1 %copy-start.9 = (bf16[2,56,768]{2,1,0:T(8,128)(2,1)}, bf16[2,56,768]{2,1,0:T(8,128)(2,1)S(1)}, u32[]{:S(2)}) copy-start(bf16[2,56,768]{2,1,0:T(8,128)(2,1)S(1)} %collective-permute-done.29.refs_1_) | copy-start | bytes 516100
  297.9 7.1 %collective-permute-start.31 = (bf16[56,768]{1,0:T(8,128)(2,1)S(1)}, bf16[56,768]{1,0:T(8,128)(2,1)S(1)}, u32[]{:S(2)}, u32[]{:S(2)}) collective-permute-start(bf16[56,768]{1,0:T(8,128)(2,1)S(1)} %add_bitcast_fusion.2), channel_id=1, source_target_pairs={{0,6},{1,7},{2,4},{3,5},{4,2},{5,3},{6,0},{7,1},{8,14},{9,15},{10,... | collective-permute-start | bytes 258056 | tf_op jit(solution)/shard_map/ppermute | solution.py:33
  299.6 5.3 %collective-permute-start.32 = (bf16[48,768]{1,0:T(8,128)(2,1)S(1)}, bf16[48,768]{1,0:T(8,128)(2,1)S(1)}, u32[]{:S(2)}, u32[]{:S(2)}) collective-permute-start(bf16[48,768]{1,0:T(8,128)(2,1)S(1)} %add_bitcast_fusion.3), channel_id=1, source_target_pairs={{0,2},{1,3},{2,0},{3,1},{4,6},{5,7},{6,4},{7,5},{8,10},{9,11},{10,... | collective-permute-start | bytes 221192 | tf_op jit(solution)/shard_map/ppermute | solution.py:33
  (13 other events, 34.3 us)
Sparse Core Ops, SparseCore 0:
  11.6 93.4 all-gather.2

commit v5 on v4

--- a/solution.py
+++ b/solution.py
@@ -389,13 +389,10 @@
 
 
 def apart(scr, me, keep, send):
-    def one(index, carry):
-        group = (2 * index - jnp.bitwise_and(index, 7)) ^ me
+    for index in range(GROUPS_W // 2):
+        group = me ^ (2 * index - index % 8)
         keep(index, scr[group])
         send(index, scr[group ^ 8])
-        return carry
-
-    lax.fori_loop(0, GROUPS_W // 2, one, 0)
 
 
 def ffn_backward_body(

time: 317 us -> 313 us (0.987)
  Pallas kernels: 163 us -> 158 us
    pallas_call x1, Pallas kernels: 26.4 us -> 22.2 us  [ffn_backward(): call(ffn_backward_body, (FF // D,), [whole((rows, D)), pl.BlockSpec((rows...]
  transfers between devices with their start and end apart: 34 -> 34, of which waited for: 19 -> 19; matrix products, arithmetic and copies ran while one was open for 6% -> 6% of each run, Pallas kernels for 38% -> 37%
where the time goes in v5:
time: 313 us; the launch traced here: 312 us
  Pallas kernels  158 us (50%)
  waiting for transfers between devices  76 us (24%)
  starting transfers between devices  33.3 us (11%)
  other arithmetic  16.5 us (5%)
  between operations  14.7 us (5%)
  local copies, waits for them, and re-layouts  12.8 us (4%)
    ppermute x33, waiting for transfers between devices, swap(): lax.ppermute(value, axis, [(source, source ^ mask) for source in range(la...  75.9 us
    ppermute x33, starting transfers between devices, swap(): lax.ppermute(value, axis, [(source, source ^ mask) for source in range(la...  33.2 us
    pallas_call x1, Pallas kernels, ffn_forward(): call(ffn_forward_body, (rows // span, chunks), [row_spec, row_spec, row_s...  29.6 us
    pallas_call x1, Pallas kernels, ffn_backward(): call(ffn_backward_body, (FF // D,), [whole((rows, D)), pl.BlockSpec((rows...  22.2 us
    pallas_call x1, Pallas kernels, attend_back(): call(attend_back_body, (seqs, H // 2), [spec] * 3 + [pl.BlockSpec((1, 2,...  21.9 us
    pallas_call x1, Pallas kernels, attend(): call(attend_body, (seqs, H // 2), [spec] * 3, [spec, pl.BlockSpec((1, 2,...  18.5 us
    pallas_call x1, Pallas kernels, grad_project(): call(grad_project_body, (3,), [whole((rows, D)), whole((rows, D)), pl.Blo...  12.4 us
    pallas_call x1, Pallas kernels, project(): call(project_body, (rows // step,), [row_spec, row_spec] + [whole(pieces[...  12 us
  transfers between devices with their start and end apart: 34, of which 19 were waited for; matrix products, arithmetic and copies ran while one was open for 6% of the time, Pallas kernels for 37%

profile of v5, /device:TPU:0, one launch (start us, length us, event | category | flops | bytes accessed | tf_op | source)
XLA Modules:
  0.0 312.3 jit_solution(142679355639360369)
XLA Ops:
  12.3 5.1 %collective-permute-start.2 = (bf16[112,768]{1,0:T(8,128)(2,1)S(1)}, bf16[112,768]{1,0:T(8,128)(2,1)S(1)}, u32[]{:S(2)}, u32[]{:S(2)}) collective-permute-start(bf16[112,768]{1,0:T(8,128)(2,1)S(1)} %concatenate.16), channel_id=1, source_target_pairs={{0,6},{1,7},{2,4},{3,5},{4,2},{5,3},{6,0},{7,1},{8,14},{9,15},{10,... | collective-permute-start | bytes 516104 | tf_op jit(solution)/shard_map/ppermute | solution.py:33
  17.5 5.3 %collective-permute-done.2 = bf16[112,768]{1,0:T(8,128)(2,1)S(1)} collective-permute-done((bf16[112,768]{1,0:T(8,128)(2,1)S(1)}, bf16[112,768]{1,0:T(8,128)(2,1)S(1)}, u32[]{:S(2)}, u32[]{:S(2)}) %collective-permute-start.2) | collective-permute-done | bytes 172064 | tf_op jit(solution)/shard_map/ppermute | solution.py:33
  22.7 2.6 collective-permute-start.3
  25.3 2.6 collective-permute-done.1
  27.9 3.5 %collective-permute-done.3 = bf16[56,768]{1,0:T(8,128)(2,1)S(1)} collective-permute-done((bf16[56,768]{1,0:T(8,128)(2,1)S(1)}, bf16[56,768]{1,0:T(8,128)(2,1)S(1)}, u32[]{:S(2)}, u32[]{:S(2)}) %collective-permute-start.3) | collective-permute-done | bytes 86048 | tf_op jit(solution)/shard_map/ppermute | solution.py:33
  31.4 4.5 %collective-permute-done.4 = bf16[56,768]{1,0:T(8,128)(2,1)S(1)} collective-permute-done((bf16[56,768]{1,0:T(8,128)(2,1)S(1)}, bf16[56,768]{1,0:T(8,128)(2,1)S(1)}, u32[]{:S(2)}, u32[]{:S(2)}) %collective-permute-start.4) | collective-permute-done | bytes 86048 | tf_op jit(solution)/shard_map/ppermute | solution.py:33
  36.1 1.3 collective-permute-start.6
  37.4 1.4 collective-permute-start.5
  38.7 15.7 %collective-permute-done.6.refs_2_ = bf16[4,112,768]{2,1,0:T(8,128)(2,1)S(1)} collective-permute-done((bf16[4,112,768]{2,1,0:T(8,128)(2,1)S(1)}, bf16[4,112,768]{2,1,0:T(8,128)(2,1)S(1)}, u32[]{:S(2)}, u32[]{:S(2)}) %collective-permute-start.6) | collective-permute-done | bytes 688160 | tf_op jit(solution)/shard_map/ppermute | solution.py:33
  54.4 1.8 collective-permute-start.7
  56.3 7.2 %collective-permute-done.5.refs_1_ = bf16[4,112,768]{2,1,0:T(8,128)(2,1)S(1)} collective-permute-done((bf16[4,112,768]{2,1,0:T(8,128)(2,1)S(1)}, bf16[4,112,768]{2,1,0:T(8,128)(2,1)S(1)}, u32[]{:S(2)}, u32[]{:S(2)}) %collective-permute-start.5) | collective-permute-done | bytes 688160 | tf_op jit(solution)/shard_map/ppermute | solution.py:33
  64.1 3.3 %collective-permute-done.7 = bf16[4,56,768]{2,1,0:T(8,128)(2,1)S(1)} collective-permute-done((bf16[4,56,768]{2,1,0:T(8,128)(2,1)S(1)}, bf16[4,56,768]{2,1,0:T(8,128)(2,1)S(1)}, u32[]{:S(2)}, u32[]{:S(2)}) %collective-permute-start.7) | collective-permute-done | bytes 344096 | tf_op jit(solution)/shard_map/ppermute | solution.py:33
  67.5 3.3 %collective-permute-done.8 = bf16[4,56,768]{2,1,0:T(8,128)(2,1)S(1)} collective-permute-done((bf16[4,56,768]{2,1,0:T(8,128)(2,1)S(1)}, bf16[4,56,768]{2,1,0:T(8,128)(2,1)S(1)}, u32[]{:S(2)}, u32[]{:S(2)}) %collective-permute-start.8) | collective-permute-done | bytes 344096 | tf_op jit(solution)/shard_map/ppermute | solution.py:33
  71.7 1.3 fusion.refs_8_.order_ref.refs_6_
  73.8 12.0 %project.1 = (bf16[1024,768]{1,0:T(8,128)(2,1)}, bf16[1024,768]{1,0:T(8,128)(2,1)}, bf16[1024,768]{1,0:T(8,128)(2,1)}, bf16[3,768,768]{2,1,0:T(8,128)(2,1)}, bf1...) custom-call(s32[1]{0:T(128)} %bitcast.me_ref, bf16[1024,768]{1,0:T(8,128)(2,1)} %bitcast.111, ...), custom_call_target="tpu_custom_call" | custom-call | flops 3623878656 | bytes 14942208 | tf_op jit(solution)/shard_map/project/pallas_call | solution.py:113
  85.7 18.5 %attend.1 = (bf16[1024,768]{1,0:T(8,128)(2,1)}, bf16[2,12,512,512]{3,2,1,0:T(8,128)(2,1)}) custom-call(s32[2,2]{1,0:T(2,128)} %pad_add_fusion.valid_ref, bf16[1024,768]{1,0:T(8,128)(2,1)} %get-tuple-element.81.q_ref, bf16[1024,768]{1,0:T(8,128)(2,1)} %get-tuple-element.82.k_ref, bf16[1024,768]{1,0:T(8,128)(2,1)} %get-tuple-element.83.v_ref), custom_call_target="tpu_custom_call" | custom-call | flops 6442450944 | bytes 18874368 | tf_op jit(solution)/shard_map/attend/pallas_call | solution.py:152
  104.2 5.8 %first_norm.1 = (f32[1024,768]{1,0:T(8,128)}, f32[1024,128]{1,0:T(8,128)}, bf16[1024,768]{1,0:T(8,128)(2,1)}) custom-call(bf16[1024,768]{1,0:T(8,128)(2,1)} %get-tuple-element.84.ctx_ref, bf16[1024,768]{1,0:T(8,128)(2,1)} %bitcast.112, bf16[768,768]{1,0:T(8,128)(2,1)} %get-tuple-element.85.wop_ref, f32[8,768]{1,0:T(8,128)} %get-tuple-element.86.vec_ref), custom_call_target="tpu_custom_call" | custom-call | flops 1207959552 | bytes 9437184 | tf_op jit(solution)/shard_map/first_norm/pallas_call | solution.py:235
  110.0 29.6 %ffn_forward.1 = (bf16[1024,3072]{1,0:T(8,128)(2,1)}, bf16[1024,3072]{1,0:T(8,128)(2,1)}, bf16[1024,768]{1,0:T(8,128)(2,1)}, f32[1024,768]{1,0:T(8,128)}, bf16[1024,768]{1,0:T(8,128)(2,1)}, /*index=5*/f32[8,768]{1,0:T(8,128)}) custom-call(bf16[1024,768]{1,0:T(8,128)(2,1)} %get-tuple-element.87.low_ref, f32[1024,768]{1,0:T(8,128)} %get-tuple-element.88.hat_ref, ...), custom_call_target="tpu_custom_call" | custom-call | flops 9663676416 | bytes 29884416 | tf_op jit(solution)/shard_map/ffn_forward/pallas_call | solution.py:324
  139.7 9.8 %grad_down.1 = (bf16[2,8,96,768]{3,2,1,0:T(8,128)(2,1)}, bf16[2,8,96,768]{3,2,1,0:T(8,128)(2,1)}) custom-call(s32[1]{0:T(128)} %bitcast.me_ref, bf16[1024,3072]{1,0:T(8,128)(2,1)} %get-tuple-element.91.act_ref, bf16[1024,768]{1,0:T(8,128)(2,1)} %get-tuple-element.95.gsec_ref), custom_call_target="tpu_custom_call" | custom-call | flops 4831838208 | bytes 12582912 | tf_op jit(solution)/shard_map/grad_down/pallas_call | solution.py:371
  150.0 22.2 %ffn_backward.1 = (bf16[16,96,768]{2,1,0:T(8,128)(2,1)}, bf16[16,96,768]{2,1,0:T(8,128)(2,1)}, f32[4,1,768]{2,1,0:T(1,128)}, f32[1024,768]{1,0:T(8,128)}) custom-call(s32[1]{0:T(128)} %bitcast.me_ref, bf16[1024,768]{1,0:T(8,128)(2,1)} %get-tuple-element.95.gsec_ref, bf16[1024,3072]{1,0:T(8,128)(2,1)} %get-tuple-element.96.slope_ref, ...), custom_call_target="tpu_custom_call" | custom-call | flops 14495514624 | bytes 26738688 | tf_op jit(solution)/shard_map/ffn_backward/pallas_call | solution.py:428
  172.3 3.1 add.96
  177.7 11.0 %first_back.1 = (f32[1024,768]{1,0:T(8,128)}, bf16[1024,768]{1,0:T(8,128)(2,1)}, bf16[32,24,768]{2,1,0:T(8,128)(2,1)}, f32[8,768]{1,0:T(8,128)}) custom-call(f32[1024,768]{1,0:T(8,128)} %get-tuple-element.101.acc_ref, f32[1024,768]{1,0:T(8,128)} %get-tuple-element.102.gtwo_ref, f32[1024,768]{1,0:T(8,128)} %get-tuple-element.88.hat_ref, ...), custom_call_target="tpu_custom_call" | custom-call | flops 2415919104 | bytes 19267584 | tf_op jit(solution)/shard_map/first_back/pallas_call | solution.py:487
  188.7 1.4 copy-done.5
  190.1 3.1 add.94
  193.3 2.1 collective-permute-start.15
  196.0 21.9 %attend_back.1 = (bf16[3,1024,768]{2,1,0:T(8,128)(2,1)}, bf16[2,1024,384]{2,1,0:T(8,128)(2,1)}) custom-call(bf16[1024,768]{1,0:T(8,128)(2,1)} %get-tuple-element.81.q_ref, bf16[1024,768]{1,0:T(8,128)(2,1)} %get-tuple-element.82.k_ref, bf16[1024,768]{1,0:T(8,128)(2,1)} %get-tuple-element.83.v_ref, bf16[2,12,512,512]{3,2,1,0:T(8,128)(2,1)} %get-tuple-element.108.p_ref, ...), custom_call_target="tpu_custom_call" | custom-call | flops 12884901888 | bytes 23592960 | tf_op jit(solution)/shard_map/attend_back/pallas_call | solution.py:197
  218.0 4.2 %collective-permute-done.15 = bf16[2,4,96,768]{3,2,1,0:T(8,128)(2,1)} collective-permute-done((bf16[2,4,96,768]{3,2,1,0:T(8,128)(2,1)S(1)}, bf16[2,4,96,768]{3,2,1,0:T(8,128)(2,1)}, u32[]{:S(2)}, u32[]{:S(2)}) %collective-permute-start.15) | collective-permute-done | bytes 1179680 | tf_op jit(solution)/shard_map/ppermute | solution.py:33
  222.1 1.4 fusion.2
  223.8 1.4 copy_add_fusion
  225.3 1.5 collective-permute-start.18
  228.2 12.4 %grad_project.1 = (bf16[16,104,768]{2,1,0:T(8,128)(2,1)}, bf16[16,104,768]{2,1,0:T(8,128)(2,1)}) custom-call(s32[1]{0:T(128)} %bitcast.me_ref, bf16[1024,768]{1,0:T(8,128)(2,1)} %bitcast.113, bf16[1024,768]{1,0:T(8,128)(2,1)} %collective-permute-done.xp_ref, bf16[3,1024,768]{2,1,0:T(8,128)(2,1)} %get-tuple-element.114.grad_ref.grads_ref, ...), custom_call_target="tpu_custom_call" | custom-call | flops 3623878656 | bytes 14942208 | tf_op jit(solution)/shard_map/grad_project/pallas_call | solution.py:584
  240.7 1.8 collective-permute-done.17
  243.1 4.5 %collective-permute-done.21 = bf16[16,104,768]{2,1,0:T(8,128)(2,1)S(1)} collective-permute-done((bf16[16,104,768]{2,1,0:T(8,128)(2,1)}, bf16[16,104,768]{2,1,0:T(8,128)(2,1)S(1)}, u32[]{:S(2)}, u32[]{:S(2)}) %collective-permute-start.21) | collective-permute-done | bytes 2555936 | tf_op jit(solution)/shard_map/ppermute | solution.py:33
  252.6 3.1 collective-permute-start.20
  255.7 9.7 %grad_input.1 = f32[1024,768]{1,0:T(8,128)} custom-call(f32[1024,768]{1,0:T(8,128)} %get-tuple-element.125.gres_ref, bf16[3,1024,768]{2,1,0:T(8,128)(2,1)} %get-tuple-element.114.grad_ref.grads_ref, bf16[2,1024,384]{2,1,0:T(8,128)(2,1)} %collective-permute-done.22.back_ref, bf16[3,768,768]{2,1,0:T(8,128)(2,1)} %get-tuple-element.127.w_ref), custom_call_target="tpu_custom_call" | custom-call | flops 3623878656 | bytes 16121856 | tf_op jit(solution)/shard_map/grad_input/pallas_call | solution.py:623
  265.4 4.2 %collective-permute-done.19.refs_1_ = bf16[2,96,768]{2,1,0:T(8,128)(2,1)} collective-permute-done((bf16[2,96,768]{2,1,0:T(8,128)(2,1)}, bf16[2,96,768]{2,1,0:T(8,128)(2,1)}, u32[]{:S(2)}, u32[]{:S(2)}) %collective-permute-start.19) | collective-permute-done | bytes 294944 | tf_op jit(solution)/shard_map/ppermute | solution.py:33
  271.9 1.6 collective-permute-start.26
  274.6 1.7 collective-permute-start.25
  276.9 1.5 collective-permute-start.27
  278.4 2.5 collective-permute-done.26
  281.0 3.4 %collective-permute-done.25 = bf16[4,56,768]{2,1,0:T(8,128)(2,1)S(1)} collective-permute-done((bf16[4,56,768]{2,1,0:T(8,128)(2,1)S(1)}, bf16[4,56,768]{2,1,0:T(8,128)(2,1)S(1)}, u32[]{:S(2)}, u32[]{:S(2)}) %collective-permute-start.25) | collective-permute-done | bytes 344096 | tf_op jit(solution)/shard_map/ppermute | solution.py:33
  284.8 1.8 collective-permute-start.29
  286.6 1.4 collective-permute-start.30
  288.0 2.1 finish_ffn.1
  290.1 3.6 %collective-permute-done.30.refs_4_ = bf16[2,48,768]{2,1,0:T(8,128)(2,1)S(1)} collective-permute-done((bf16[2,48,768]{2,1,0:T(8,128)(2,1)S(1)}, bf16[2,48,768]{2,1,0:T(8,128)(2,1)S(1)}, u32[]{:S(2)}, u32[]{:S(2)}) %collective-permute-start.30) | collective-permute-done | bytes 147488 | tf_op jit(solution)/shard_map/ppermute | solution.py:33
  293.7 1.7 collective-permute-start.31
  295.6 5.3 %collective-permute-done.32.refs_5_ = bf16[48,768]{1,0:T(8,128)(2,1)S(1)} collective-permute-done((bf16[48,768]{1,0:T(8,128)(2,1)S(1)}, bf16[48,768]{1,0:T(8,128)(2,1)S(1)}, u32[]{:S(2)}, u32[]{:S(2)}) %collective-permute-start.32) | collective-permute-done | bytes 73760 | tf_op jit(solution)/shard_map/ppermute | solution.py:33
  302.1 3.4 %finish_last.1 = (f32[144,128]{1,0:T(8,128)}, f32[144,128]{1,0:T(8,128)}, f32[144,128]{1,0:T(8,128)}, f32[144,128]{1,0:T(8,128)}, f32[192]{0:T(256)}, /*index=5*/f32[96]{0:T(128)}) custom-call(bf16[4,56,768]{2,1,0:T(8,128)(2,1)} %copy-done.3, bf16[2,56,768]{2,1,0:T(8,128)(2,1)} %copy-done.9, bf16[56,768]{1,0:T(8,128)(2,1)} %copy-done.16, ...), custom_call_target="tpu_custom_call" | custom-call | bytes 638976 | tf_op jit(solution)/shard_map/finish_last/pallas_call | solution.py:689
  (154 shorter events, 24.0 us)
Async XLA Ops:
  7.2 102.8 %all-gather.3.cloned.1.call-start = ((), (), s32[]{:S(2)}) async-start(), calls=%async_computation | async-start | bytes 9732096 | tf_op jit(solution)/shard_map/all_gather | solution.py:702
  8.3 3.9 %copy-start.21 = (bf16[18432]{0:T(1024)(128)(2,1)S(1)}, bf16[18432]{0:T(1024)(128)(2,1)}, u32[]{:S(2)}) copy-start(bf16[18432]{0:T(1024)(128)(2,1)} %param.19) | copy-start | bytes 110596
  12.3 10.4 %collective-permute-start.2 = (bf16[112,768]{1,0:T(8,128)(2,1)S(1)}, bf16[112,768]{1,0:T(8,128)(2,1)S(1)}, u32[]{:S(2)}, u32[]{:S(2)}) collective-permute-start(bf16[112,768]{1,0:T(8,128)(2,1)S(1)} %concatenate.16), channel_id=1, source_target_pairs={{0,6},{1,7},{2,4},{3,5},{4,2},{5,3},{6,0},{7,1},{8,14},{9,15},{10,... | collective-permute-start | bytes 516104 | tf_op jit(solution)/shard_map/ppermute | solution.py:33
  17.5 10.4 %collective-permute-start.1 = (bf16[112,768]{1,0:T(8,128)(2,1)S(1)}, bf16[112,768]{1,0:T(8,128)(2,1)S(1)}, u32[]{:S(2)}, u32[]{:S(2)}) collective-permute-start(bf16[112,768]{1,0:T(8,128)(2,1)S(1)} %concatenate.16), channel_id=1, source_target_pairs={{0,2},{1,3},{2,0},{3,1},{4,6},{5,7},{6,4},{7,5},{8,10},{9,11},{10,... | collective-permute-start | bytes 516104 | tf_op jit(solution)/shard_map/ppermute | solution.py:33
  22.7 8.7 %collective-permute-start.3 = (bf16[56,768]{1,0:T(8,128)(2,1)S(1)}, bf16[56,768]{1,0:T(8,128)(2,1)S(1)}, u32[]{:S(2)}, u32[]{:S(2)}) collective-permute-start(bf16[56,768]{1,0:T(8,128)(2,1)S(1)} %slice.188), channel_id=1, source_target_pairs={{0,2},{1,3},{2,0},{3,1},{4,6},{5,7},{6,4},{7,5},{8,10},{9,11},{10,... | collective-permute-start | bytes 258056 | tf_op jit(solution)/shard_map/ppermute | solution.py:33
  27.9 8.1 %collective-permute-start.4 = (bf16[56,768]{1,0:T(8,128)(2,1)S(1)}, bf16[56,768]{1,0:T(8,128)(2,1)S(1)}, u32[]{:S(2)}, u32[]{:S(2)}) collective-permute-start(bf16[56,768]{1,0:T(8,128)(2,1)S(1)} %slice.189), channel_id=1, source_target_pairs={{0,6},{1,7},{2,4},{3,5},{4,2},{5,3},{6,0},{7,1},{8,14},{9,15},{10,... | collective-permute-start | bytes 258056 | tf_op jit(solution)/shard_map/ppermute | solution.py:33
  36.1 36.9 %copy-start.7 = (bf16[4,112,768]{2,1,0:T(8,128)(2,1)}, bf16[4,112,768]{2,1,0:T(8,128)(2,1)S(1)}, u32[]{:S(2)}) copy-start(bf16[4,112,768]{2,1,0:T(8,128)(2,1)S(1)} %pad_maximum_fusion.refs_0_) | copy-start | bytes 2064388
  36.1 34.9 %copy-start.22 = (s32[2,2]{1,0:T(2,128)S(1)}, s32[2,2]{1,0:T(2,128)}, u32[]{:S(2)}) copy-start(s32[2,2]{1,0:T(2,128)} %param.14) | copy-start | bytes 52
  36.1 18.3 %collective-permute-start.6 = (bf16[4,112,768]{2,1,0:T(8,128)(2,1)S(1)}, bf16[4,112,768]{2,1,0:T(8,128)(2,1)S(1)}, u32[]{:S(2)}, u32[]{:S(2)}) collective-permute-start(bf16[4,112,768]{2,1,0:T(8,128)(2,1)S(1)} %pad_maximum_fusion.refs_0_), channel_id=1, source_target_pairs={{0,16},{8,24},{16,0},{24,8},{1,17},{9,25},{17,1},{25,9},{2,18},{10... | collective-permute-start | bytes 2064392 | tf_op jit(solution)/shard_map/ppermute | solution.py:33
  37.4 26.1 %collective-permute-start.5 = (bf16[4,112,768]{2,1,0:T(8,128)(2,1)S(1)}, bf16[4,112,768]{2,1,0:T(8,128)(2,1)S(1)}, u32[]{:S(2)}, u32[]{:S(2)}) collective-permute-start(bf16[4,112,768]{2,1,0:T(8,128)(2,1)S(1)} %pad_maximum_fusion.refs_0_), channel_id=1, source_target_pairs={{0,1},{1,0},{2,3},{3,2},{4,5},{5,4},{6,7},{7,6},{8,9},{9,8},{10,11... | collective-permute-start | bytes 2064392 | tf_op jit(solution)/shard_map/ppermute | solution.py:33
  38.7 34.2 %collective-permute-start = (bf16[1024,768]{1,0:T(8,128)(2,1)}, bf16[1024,768]{1,0:T(8,128)(2,1)}, u32[]{:S(2)}, u32[]{:S(2)}) collective-permute-start(bf16[1024,768]{1,0:T(8,128)(2,1)} %bitcast.110), channel_id=1, source_target_pairs={{0,8},{8,0},{16,24},{24,16},{1,9},{9,1},{17,25},{25,17},{2,10},{10... | collective-permute-start | bytes 4718600 | tf_op jit(solution)/shard_map/ppermute | solution.py:33
  54.4 18.5 %copy-start.11 = (bf16[4,112,768]{2,1,0:T(8,128)(2,1)}, bf16[4,112,768]{2,1,0:T(8,128)(2,1)S(1)}, u32[]{:S(2)}) copy-start(bf16[4,112,768]{2,1,0:T(8,128)(2,1)S(1)} %collective-permute-done.6.refs_2_) | copy-start | bytes 2064388
  54.4 13.1 %collective-permute-start.7 = (bf16[4,56,768]{2,1,0:T(8,128)(2,1)S(1)}, bf16[4,56,768]{2,1,0:T(8,128)(2,1)S(1)}, u32[]{:S(2)}, u32[]{:S(2)}) collective-permute-start(bf16[4,56,768]{2,1,0:T(8,128)(2,1)S(1)} %slice.190), channel_id=1, source_target_pairs={{0,1},{1,0},{2,3},{3,2},{4,5},{5,4},{6,7},{7,6},{8,9},{9,8},{10,11... | collective-permute-start | bytes 1032200 | tf_op jit(solution)/shard_map/ppermute | solution.py:33
  63.5 9.5 %copy-start.12 = (bf16[4,112,768]{2,1,0:T(8,128)(2,1)}, bf16[4,112,768]{2,1,0:T(8,128)(2,1)S(1)}, u32[]{:S(2)}) copy-start(bf16[4,112,768]{2,1,0:T(8,128)(2,1)S(1)} %collective-permute-done.5.refs_1_) | copy-start | bytes 2064388
  63.5 7.3 %collective-permute-start.8 = (bf16[4,56,768]{2,1,0:T(8,128)(2,1)S(1)}, bf16[4,56,768]{2,1,0:T(8,128)(2,1)S(1)}, u32[]{:S(2)}, u32[]{:S(2)}) collective-permute-start(bf16[4,56,768]{2,1,0:T(8,128)(2,1)S(1)} %slice.191), channel_id=1, source_target_pairs={{0,16},{8,24},{16,0},{24,8},{1,17},{9,25},{17,1},{25,9},{2,18},{10... | collective-permute-start | bytes 1032200 | tf_op jit(solution)/shard_map/ppermute | solution.py:33
  63.6 9.4 %collective-permute-start.9 = (bf16[4,112,768]{2,1,0:T(8,128)(2,1)S(1)}, bf16[4,112,768]{2,1,0:T(8,128)(2,1)S(1)}, u32[]{:S(2)}, u32[]{:S(2)}) collective-permute-start(bf16[4,112,768]{2,1,0:T(8,128)(2,1)S(1)} %pad_maximum_fusion.refs_0_), channel_id=1, source_target_pairs={{0,8},{8,0},{16,24},{24,16},{1,9},{9,1},{17,25},{25,17},{2,10},{10... | collective-permute-start | bytes 2064392 | tf_op jit(solution)/shard_map/ppermute | solution.py:33
  63.6 9.3 %collective-permute-start.11 = (bf16[4,112,768]{2,1,0:T(8,128)(2,1)S(1)}, bf16[4,112,768]{2,1,0:T(8,128)(2,1)}, u32[]{:S(2)}, u32[]{:S(2)}) collective-permute-start(bf16[4,112,768]{2,1,0:T(8,128)(2,1)S(1)} %collective-permute-done.6.refs_2_), channel_id=1, source_target_pairs={{0,8},{8,0},{16,24},{24,16},{1,9},{9,1},{17,25},{25,17},{2,10},{10... | collective-permute-start | bytes 2064392 | tf_op jit(solution)/shard_map/ppermute | solution.py:33
  67.5 5.5 %collective-permute-start.10 = (bf16[4,112,768]{2,1,0:T(8,128)(2,1)S(1)}, bf16[4,112,768]{2,1,0:T(8,128)(2,1)}, u32[]{:S(2)}, u32[]{:S(2)}) collective-permute-start(bf16[4,112,768]{2,1,0:T(8,128)(2,1)S(1)} %collective-permute-done.5.refs_1_), channel_id=1, source_target_pairs={{0,8},{8,0},{16,24},{24,16},{1,9},{9,1},{17,25},{25,17},{2,10},{10... | collective-permute-start | bytes 2064392 | tf_op jit(solution)/shard_map/ppermute | solution.py:33
  70.8 2.6 collective-permute-start.12
  149.5 22.8 %collective-permute-start.14 = (bf16[16,96,768]{2,1,0:T(8,128)(2,1)}, bf16[16,96,768]{2,1,0:T(8,128)(2,1)}, u32[]{:S(2)}, u32[]{:S(2)}) collective-permute-start(bf16[16,96,768]{2,1,0:T(8,128)(2,1)} %bitcast.108), channel_id=1, source_target_pairs={{0,8},{8,0},{16,24},{24,16},{1,9},{9,1},{17,25},{25,17},{2,10},{10... | collective-permute-start | bytes 7077896 | tf_op jit(solution)/shard_map/ppermute | solution.py:33
  172.2 16.5 %collective-permute-start.13 = (bf16[16,96,768]{2,1,0:T(8,128)(2,1)}, bf16[16,96,768]{2,1,0:T(8,128)(2,1)S(1)}, u32[]{:S(2)}, u32[]{:S(2)}) collective-permute-start(bf16[16,96,768]{2,1,0:T(8,128)(2,1)} %get-tuple-element.98), channel_id=1, source_target_pairs={{0,8},{8,0},{16,24},{24,16},{1,9},{9,1},{17,25},{25,17},{2,10},{10... | collective-permute-start | bytes 7077896 | tf_op jit(solution)/shard_map/ppermute | solution.py:33
  193.3 28.9 %collective-permute-start.15 = (bf16[2,4,96,768]{3,2,1,0:T(8,128)(2,1)S(1)}, bf16[2,4,96,768]{3,2,1,0:T(8,128)(2,1)}, u32[]{:S(2)}, u32[]{:S(2)}) collective-permute-start(bf16[2,4,96,768]{3,2,1,0:T(8,128)(2,1)S(1)} %slice_bitcast_fusion), channel_id=1, source_target_pairs={{0,1},{1,0},{2,3},{3,2},{4,5},{5,4},{6,7},{7,6},{8,9},{9,8},{10,11... | collective-permute-start | bytes 3538952 | tf_op jit(solution)/shard_map/ppermute | solution.py:33
  195.4 28.4 %collective-permute-start.16 = (bf16[4,2,96,768]{3,2,0,1:T(8,128)(2,1)}, bf16[4,2,96,768]{3,2,0,1:T(8,128)(2,1)}, u32[]{:S(2)}, u32[]{:S(2)}) collective-permute-start(bf16[4,2,96,768]{3,2,0,1:T(8,128)(2,1)} %copy.38), channel_id=1, source_target_pairs={{0,16},{8,24},{16,0},{24,8},{1,17},{9,25},{17,1},{25,9},{2,18},{10... | collective-permute-start | bytes 3538952 | tf_op jit(solution)/shard_map/ppermute | solution.py:33
  218.0 5.8 %copy-start = (bf16[8,96,768]{2,1,0:T(8,128)(2,1)S(1)}, bf16[8,96,768]{2,1,0:T(8,128)(2,1)}, u32[]{:S(2)}) copy-start(bf16[8,96,768]{2,1,0:T(8,128)(2,1)} %get-tuple-element.184) | copy-start | bytes 3538948
  225.3 15.3 %collective-permute-start.18 = (bf16[4,96,768]{2,1,0:T(8,128)(2,1)S(1)}, bf16[4,96,768]{2,1,0:T(8,128)(2,1)S(1)}, u32[]{:S(2)}, u32[]{:S(2)}) collective-permute-start(bf16[4,96,768]{2,1,0:T(8,128)(2,1)S(1)} %slice_bitcast_fusion.4), channel_id=1, source_target_pairs={{0,1},{1,0},{2,3},{3,2},{4,5},{5,4},{6,7},{7,6},{8,9},{9,8},{10,11... | collective-permute-start | bytes 1769480 | tf_op jit(solution)/shard_map/ppermute | solution.py:33
  227.7 14.8 %collective-permute-start.17 = (bf16[4,96,768]{2,1,0:T(8,128)(2,1)}, bf16[4,96,768]{2,1,0:T(8,128)(2,1)S(1)}, u32[]{:S(2)}, u32[]{:S(2)}) collective-permute-start(bf16[4,96,768]{2,1,0:T(8,128)(2,1)} %slice_bitcast_fusion.5), channel_id=1, source_target_pairs={{0,16},{8,24},{16,0},{24,8},{1,17},{9,25},{17,1},{25,9},{2,18},{10... | collective-permute-start | bytes 1769480 | tf_op jit(solution)/shard_map/ppermute | solution.py:33
  240.6 7.0 %copy-start.4 = (bf16[16,104,768]{2,1,0:T(8,128)(2,1)S(1)}, bf16[16,104,768]{2,1,0:T(8,128)(2,1)}, u32[]{:S(2)}) copy-start(bf16[16,104,768]{2,1,0:T(8,128)(2,1)} %get-tuple-element.129) | copy-start | bytes 7667716
  240.7 35.6 %copy-start.1 = (bf16[4,96,768]{2,1,0:T(8,128)(2,1)}, bf16[4,96,768]{2,1,0:T(8,128)(2,1)S(1)}, u32[]{:S(2)}) copy-start(bf16[4,96,768]{2,1,0:T(8,128)(2,1)S(1)} %bitcast_add_fusion.refs_3_) | copy-start | bytes 1769476
  242.5 8.6 %copy-start.2 = (bf16[4,96,768]{2,1,0:T(8,128)(2,1)}, bf16[4,96,768]{2,1,0:T(8,128)(2,1)S(1)}, u32[]{:S(2)}) copy-start(bf16[4,96,768]{2,1,0:T(8,128)(2,1)S(1)} %bitcast_add_fusion.1.refs_0_) | copy-start | bytes 1769476
  242.5 5.1 %collective-permute-start.21 = (bf16[16,104,768]{2,1,0:T(8,128)(2,1)}, bf16[16,104,768]{2,1,0:T(8,128)(2,1)S(1)}, u32[]{:S(2)}, u32[]{:S(2)}) collective-permute-start(bf16[16,104,768]{2,1,0:T(8,128)(2,1)} %get-tuple-element.123), channel_id=1, source_target_pairs={{0,8},{8,0},{16,24},{24,16},{1,9},{9,1},{17,25},{25,17},{2,10},{10... | collective-permute-start | bytes 7667720 | tf_op jit(solution)/shard_map/ppermute | solution.py:33
  242.6 13.1 %collective-permute-start.22 = (bf16[2,1024,384]{2,1,0:T(8,128)(2,1)}, bf16[2,1024,384]{2,1,0:T(8,128)(2,1)}, u32[]{:S(2)}, u32[]{:S(2)}) collective-permute-start(bf16[2,1024,384]{2,1,0:T(8,128)(2,1)} %get-tuple-element.126), channel_id=1, source_target_pairs={{0,8},{8,0},{16,24},{24,16},{1,9},{9,1},{17,25},{25,17},{2,10},{10... | collective-permute-start | bytes 4718600 | tf_op jit(solution)/shard_map/ppermute | solution.py:33
  249.3 20.3 %collective-permute-start.24 = (bf16[4,2,48,768]{3,2,0,1:T(8,128)(2,1)}, bf16[4,2,48,768]{3,2,0,1:T(8,128)(2,1)}, u32[]{:S(2)}, u32[]{:S(2)}) collective-permute-start(bf16[4,2,48,768]{3,2,0,1:T(8,128)(2,1)} %bitcast.89), channel_id=1, source_target_pairs={{0,16},{8,24},{16,0},{24,8},{1,17},{9,25},{17,1},{25,9},{2,18},{10... | collective-permute-start | bytes 1769480 | tf_op jit(solution)/shard_map/ppermute | solution.py:33
  250.6 20.1 %collective-permute-start.23 = (bf16[2,4,56,768]{3,2,1,0:T(8,128)(2,1)}, bf16[2,4,56,768]{3,2,1,0:T(8,128)(2,1)}, u32[]{:S(2)}, u32[]{:S(2)}) collective-permute-start(bf16[2,4,56,768]{3,2,1,0:T(8,128)(2,1)} %slice_bitcast_fusion.2), channel_id=1, source_target_pairs={{0,1},{1,0},{2,3},{3,2},{4,5},{5,4},{6,7},{7,6},{8,9},{9,8},{10,11... | collective-permute-start | bytes 2064392 | tf_op jit(solution)/shard_map/ppermute | solution.py:33
  252.6 12.8 %collective-permute-start.20 = (bf16[2,96,768]{2,1,0:T(8,128)(2,1)}, bf16[2,96,768]{2,1,0:T(8,128)(2,1)S(1)}, u32[]{:S(2)}, u32[]{:S(2)}) collective-permute-start(bf16[2,96,768]{2,1,0:T(8,128)(2,1)} %slice.165), channel_id=1, source_target_pairs={{0,6},{1,7},{2,4},{3,5},{4,2},{5,3},{6,0},{7,1},{8,14},{9,15},{10,... | collective-permute-start | bytes 884744 | tf_op jit(solution)/shard_map/ppermute | solution.py:33
  255.7 13.9 %collective-permute-start.19 = (bf16[2,96,768]{2,1,0:T(8,128)(2,1)}, bf16[2,96,768]{2,1,0:T(8,128)(2,1)}, u32[]{:S(2)}, u32[]{:S(2)}) collective-permute-start(bf16[2,96,768]{2,1,0:T(8,128)(2,1)} %slice.164), channel_id=1, source_target_pairs={{0,2},{1,3},{2,0},{3,1},{4,6},{5,7},{6,4},{7,5},{8,10},{9,11},{10,... | collective-permute-start | bytes 884744 | tf_op jit(solution)/shard_map/ppermute | solution.py:33
  265.4 10.9 %copy-start.8 = (bf16[2,96,768]{2,1,0:T(8,128)(2,1)}, bf16[2,96,768]{2,1,0:T(8,128)(2,1)S(1)}, u32[]{:S(2)}) copy-start(bf16[2,96,768]{2,1,0:T(8,128)(2,1)S(1)} %collective-permute-done.20.refs_4_) | copy-start | bytes 884740
  271.9 9.0 %collective-permute-start.26 = (bf16[4,48,768]{2,1,0:T(8,128)(2,1)S(1)}, bf16[4,48,768]{2,1,0:T(8,128)(2,1)S(1)}, u32[]{:S(2)}, u32[]{:S(2)}) collective-permute-start(bf16[4,48,768]{2,1,0:T(8,128)(2,1)S(1)} %slice_bitcast_fusion.7), channel_id=1, source_target_pairs={{0,1},{1,0},{2,3},{3,2},{4,5},{5,4},{6,7},{7,6},{8,9},{9,8},{10,11... | collective-permute-start | bytes 884744 | tf_op jit(solution)/shard_map/ppermute | solution.py:33
  274.6 9.8 %collective-permute-start.25 = (bf16[4,56,768]{2,1,0:T(8,128)(2,1)S(1)}, bf16[4,56,768]{2,1,0:T(8,128)(2,1)S(1)}, u32[]{:S(2)}, u32[]{:S(2)}) collective-permute-start(bf16[4,56,768]{2,1,0:T(8,128)(2,1)S(1)} %slice_bitcast_fusion.6), channel_id=1, source_target_pairs={{0,16},{8,24},{16,0},{24,8},{1,17},{9,25},{17,1},{25,9},{2,18},{10... | collective-permute-start | bytes 1032200 | tf_op jit(solution)/shard_map/ppermute | solution.py:33
  276.3 8.1 %collective-permute-start.28 = (bf16[96,768]{1,0:T(8,128)(2,1)S(1)}, bf16[96,768]{1,0:T(8,128)(2,1)S(1)}, u32[]{:S(2)}, u32[]{:S(2)}) collective-permute-start(bf16[96,768]{1,0:T(8,128)(2,1)S(1)} %add_bitcast_fusion), channel_id=1, source_target_pairs={{0,2},{1,3},{2,0},{3,1},{4,6},{5,7},{6,4},{7,5},{8,10},{9,11},{10,... | collective-permute-start | bytes 442376 | tf_op jit(solution)/shard_map/ppermute | solution.py:33
  276.9 7.9 %collective-permute-start.27 = (bf16[96,768]{1,0:T(8,128)(2,1)S(1)}, bf16[96,768]{1,0:T(8,128)(2,1)S(1)}, u32[]{:S(2)}, u32[]{:S(2)}) collective-permute-start(bf16[96,768]{1,0:T(8,128)(2,1)S(1)} %add_bitcast_fusion.1), channel_id=1, source_target_pairs={{0,6},{1,7},{2,4},{3,5},{4,2},{5,3},{6,0},{7,1},{8,14},{9,15},{10,... | collective-permute-start | bytes 442376 | tf_op jit(solution)/shard_map/ppermute | solution.py:33
  281.0 14.5 %copy-start.6 = (bf16[4,48,768]{2,1,0:T(8,128)(2,1)}, bf16[4,48,768]{2,1,0:T(8,128)(2,1)S(1)}, u32[]{:S(2)}) copy-start(bf16[4,48,768]{2,1,0:T(8,128)(2,1)S(1)} %bitcast_add_fusion.3.refs_3_) | copy-start | bytes 884740
  284.4 11.1 %copy-start.3 = (bf16[4,56,768]{2,1,0:T(8,128)(2,1)}, bf16[4,56,768]{2,1,0:T(8,128)(2,1)S(1)}, u32[]{:S(2)}) copy-start(bf16[4,56,768]{2,1,0:T(8,128)(2,1)S(1)} %bitcast_add_fusion.2.refs_0_) | copy-start | bytes 1032196
  284.8 8.9 %collective-permute-start.29 = (bf16[2,56,768]{2,1,0:T(8,128)(2,1)S(1)}, bf16[2,56,768]{2,1,0:T(8,128)(2,1)S(1)}, u32[]{:S(2)}, u32[]{:S(2)}) collective-permute-start(bf16[2,56,768]{2,1,0:T(8,128)(2,1)S(1)} %slice.178), channel_id=1, source_target_pairs={{0,2},{1,3},{2,0},{3,1},{4,6},{5,7},{6,4},{7,5},{8,10},{9,11},{10,... | collective-permute-start | bytes 516104 | tf_op jit(solution)/shard_map/ppermute | solution.py:33
  286.6 7.1 %collective-permute-start.30 = (bf16[2,48,768]{2,1,0:T(8,128)(2,1)S(1)}, bf16[2,48,768]{2,1,0:T(8,128)(2,1)S(1)}, u32[]{:S(2)}, u32[]{:S(2)}) collective-permute-start(bf16[2,48,768]{2,1,0:T(8,128)(2,1)S(1)} %slice.179), channel_id=1, source_target_pairs={{0,6},{1,7},{2,4},{3,5},{4,2},{5,3},{6,0},{7,1},{8,14},{9,15},{10,... | collective-permute-start | bytes 442376 | tf_op jit(solution)/shard_map/ppermute | solution.py:33
  293.7 7.1 %copy-start.10 = (bf16[2,48,768]{2,1,0:T(8,128)(2,1)}, bf16[2,48,768]{2,1,0:T(8,128)(2,1)S(1)}, u32[]{:S(2)}) copy-start(bf16[2,48,768]{2,1,0:T(8,128)(2,1)S(1)} %collective-permute-done.30.refs_4_) | copy-start | bytes 442372
  293.7 7.1 %copy-start.9 = (bf16[2,56,768]{2,1,0:T(8,128)(2,1)}, bf16[2,56,768]{2,1,0:T(8,128)(2,1)S(1)}, u32[]{:S(2)}) copy-start(bf16[2,56,768]{2,1,0:T(8,128)(2,1)S(1)} %collective-permute-done.29.refs_1_) | copy-start | bytes 516100
  293.7 7.1 %collective-permute-start.31 = (bf16[56,768]{1,0:T(8,128)(2,1)S(1)}, bf16[56,768]{1,0:T(8,128)(2,1)S(1)}, u32[]{:S(2)}, u32[]{:S(2)}) collective-permute-start(bf16[56,768]{1,0:T(8,128)(2,1)S(1)} %add_bitcast_fusion.2), channel_id=1, source_target_pairs={{0,6},{1,7},{2,4},{3,5},{4,2},{5,3},{6,0},{7,1},{8,14},{9,15},{10,... | collective-permute-start | bytes 258056 | tf_op jit(solution)/shard_map/ppermute | solution.py:33
  295.5 5.3 %collective-permute-start.32 = (bf16[48,768]{1,0:T(8,128)(2,1)S(1)}, bf16[48,768]{1,0:T(8,128)(2,1)S(1)}, u32[]{:S(2)}, u32[]{:S(2)}) collective-permute-start(bf16[48,768]{1,0:T(8,128)(2,1)S(1)} %add_bitcast_fusion.3), channel_id=1, source_target_pairs={{0,2},{1,3},{2,0},{3,1},{4,6},{5,7},{6,4},{7,5},{8,10},{9,11},{10,... | collective-permute-start | bytes 221192 | tf_op jit(solution)/shard_map/ppermute | solution.py:33
  (13 other events, 34.3 us)
Sparse Core Ops, SparseCore 0:
  11.6 93.4 all-gather.2
